TPU v7x, 32 devices: a whole 2x2x4 slice. The times are simulated.
32 devices in a mesh: lon: 16 (over z, y, x), lat: 2 (over core).
Axes of the slice: x: 2, y: 2, z: 4, core: 2. Of those that a mesh axis runs over, the one named last changes fastest.
Arguments:
- sketch: float32 [64, 256, 512], P(None, 'lon', 'lat'), may hold values from -6 to 6
- probe_bits: int32 [2, 256, 512], P(None, 'lon', 'lat'), may hold values from 0 to 65535
- ocean: int32 [256, 512], P('lon', 'lat'), may hold values 0 or 1
- east_cond: float32 [256, 512], P('lon', 'lat'), may hold values from 0.2 to 2
- north_cond: float32 [256, 512], P('lon', 'lat'), may hold values from 0.1 to 1
- kappa_sq: float32 [256, 512], P('lon', 'lat'), may hold values from 0.05 to 0.5
- inv_area: float32 [256, 512], P('lon', 'lat'), may hold values from 0.05 to 0.2
Outputs:
- image_out: float32 [64, 256, 512], P(None, 'lon', 'lat')
- gram_out: float32 [96, 96], replicated
Inputs may be any that keep to these rules, and one draw needn't show every extreme that they name: `probe_bits`: each word holds 16 independent sign bits, bit b of word w giving probe column 16 w + b.
All inputs are finite; a program needn't handle non-finite values. No bound on the sum of `ocean` on one device may be relied on, other than what follows from the above.
Results may differ from a plain program's by a relative error of at most 0.00015.
Values sent between devices are 32-bit elements; how exact they have to be, the bound alone decides.
No kernel may reach another device: no remote copies, remote signals or barrier semaphores. Data moves between devices by JAX's collectives and lax.ppermute only.
A program may use at most 64 MiB of HBM per device.

v0:
```python
import jax
import jax.numpy as jnp
from jax import lax
from jax.sharding import PartitionSpec as P


def padded_2(cells, sides, width, closed):
    for axis, dim in sides:
        count = lax.axis_size(axis)
        ends = count if closed else count - 1
        head = lax.slice_in_dim(cells, 0, width, axis=dim)
        tail = lax.slice_in_dim(cells, cells.shape[dim] - width, cells.shape[dim], axis=dim)
        cells = jnp.concatenate(
            [
                lax.ppermute(tail, axis, [(i, (i + 1) % count) for i in range(ends)]),
                cells,
                lax.ppermute(head, axis, [((i + 1) % count, i) for i in range(ends)]),
            ],
            axis=dim,
        )
    return cells


def sign_columns(probe_bits):
    shifts = jnp.arange(16, dtype=jnp.int32)
    picked = jnp.right_shift(probe_bits[:, None], shifts[None, :, None, None])
    flipped = jnp.bitwise_and(picked, 1)
    return (1 - 2 * flipped).astype(jnp.float32).reshape((-1,) + probe_bits.shape[1:])


def operate(padded, weights):
    middle = padded[:, 1:-1, 1:-1]
    return weights[0] * (
        weights[1] * middle
        - weights[2] * padded[:, 2:, 1:-1]
        - weights[3] * padded[:, :-2, 1:-1]
        - weights[4] * padded[:, 1:-1, 2:]
        - weights[5] * padded[:, 1:-1, :-2]
    )


def extend(field_in, thickness):
    wider = padded_2(field_in, (("lon", 1),), thickness, True)
    return padded_2(wider, (("lat", 2),), thickness, False)


def pair_gram(left, right):
    left_flat = left.reshape(left.shape[0], -1)
    right_flat = right.reshape(right.shape[0], -1)
    return jnp.einsum("ac,bc->ab", left_flat, right_flat, precision=lax.Precision.HIGHEST)


def local(sketch, probe_bits, ocean, east_cond, north_cond, kappa_sq, inv_area):
    lon_count, lat_count = ocean.shape
    sea_mask = ocean.astype(jnp.float32)
    stacked = jnp.stack([sea_mask, east_cond, north_cond, kappa_sq, inv_area])
    widened = padded_2(stacked, (("lon", 1),), 2, True)
    widened = padded_2(widened, (("lat", 2),), 2, False)
    sea_wide = widened[0]
    east_wide = widened[1]
    north_wide = widened[2]
    kappa_wide = widened[3]
    area_wide = widened[4]
    east_edges = east_wide[:-1] * sea_wide[:-1] * sea_wide[1:]
    north_edges = north_wide[:, :-1] * sea_wide[:, :-1] * sea_wide[:, 1:]
    offset = 2 - 0
    span_lon = lon_count + 2 * 0
    span_lat = lat_count + 2 * 0

    def window(array, shift_lon, shift_lat):
        return array[
            offset + shift_lon : offset + shift_lon + span_lon,
            offset + shift_lat : offset + shift_lat + span_lat,
        ]

    east_weight = window(east_edges, 0, 0)
    west_weight = window(east_edges, -1, 0)
    north_weight = window(north_edges, 0, 0)
    south_weight = window(north_edges, 0, -1)
    center_term = window(kappa_wide, 0, 0) + east_weight + west_weight + north_weight + south_weight
    interior = (
        window(sea_wide, 0, 0),
        center_term,
        east_weight,
        west_weight,
        north_weight,
        south_weight,
        window(area_wide, 0, 0),
    )
    sketch_masked = sketch * sea_mask
    columns = jnp.concatenate([sketch_masked, sign_columns(probe_bits) * sea_mask], axis=0)
    sketch_count = sketch.shape[0]
    thickness = 1
    columns_wide = extend(columns, thickness)
    first_pass = operate(columns_wide, interior)
    scaled = first_pass * interior[6]
    second = operate(extend(scaled[:sketch_count], 1), interior)
    local_gram = pair_gram(first_pass, scaled)
    summed = lax.psum(local_gram, ("lon", "lat"))
    cell_total = lax.axis_size("lon") * lon_count * lax.axis_size("lat") * lat_count
    return (second, summed / cell_total)


def solution(mesh):
    in_specs = (
        P(None, "lon", "lat"),
        P(None, "lon", "lat"),
        P("lon", "lat"),
        P("lon", "lat"),
        P("lon", "lat"),
        P("lon", "lat"),
        P("lon", "lat"),
    )
    out_specs = (P(None, "lon", "lat"), P())
    return jax.shard_map(local, mesh=mesh, in_specs=in_specs, out_specs=out_specs, check_vma=False)
```

profile of v0, /device:TPU:0, one launch (start us, length us, event | category | flops | bytes accessed | tf_op | source)
XLA Modules:
  0.0 94.0 jit_solution(9568899763508457570)
XLA Ops:
  0.6 0.7 bitcast_dynamic-update-slice_fusion.4
  1.4 0.7 bitcast_dynamic-update-slice_fusion.3
  2.1 0.7 bitcast_dynamic-update-slice_fusion.2
  2.8 0.7 bitcast_dynamic-update-slice_fusion.1
  3.5 0.7 bitcast_dynamic-update-slice_fusion
  4.3 3.0 %collective-permute-start = (f32[5,2,256]{2,1,0:T(2,128)S(1)}, f32[5,2,256]{2,1,0:T(2,128)S(1)}, u32[]{:S(2)}, u32[]{:S(2)}) collective-permute-start(f32[5,2,256]{2,1,0:T(2,128)S(1)} %get-tuple-element.20), channel_id=1, source_target_pairs={{0,2},{2,4},{4,6},{6,8},{8,10},{10,12},{12,14},{14,16},{16,18},{18... | collective-permute-start | bytes 30728 | tf_op jit(solution)/shard_map/ppermute | solution.py:15
  7.3 4.1 %collective-permute-start.1 = (f32[5,2,256]{2,1,0:T(2,128)S(1)}, f32[5,2,256]{2,1,0:T(2,128)S(1)}, u32[]{:S(2)}, u32[]{:S(2)}) collective-permute-start(f32[5,2,256]{2,1,0:T(2,128)S(1)} %get-tuple-element.21), channel_id=1, source_target_pairs={{2,0},{4,2},{6,4},{8,6},{10,8},{12,10},{14,12},{16,14},{18,16},{20... | collective-permute-start | bytes 30728 | tf_op jit(solution)/shard_map/ppermute | solution.py:17
  11.3 0.7 convert_element_type.7
  12.1 1.8 %copy_multiply_fusion = f32[64,16,256]{2,0,1:T(8,128)S(1)} fusion(f32[64,16,256]{2,1,0:T(8,128)} %param.7, f32[16,256]{1,0:T(8,128)S(1)} %convert_element_type.7), kind=kLoop, calls=%fused_computation.47 | loop fusion | flops 262144 | bytes 2113536 | tf_op jit(solution)/shard_map/mul | solution.py:90
  14.3 1.5 %collective-permute-start.2 = (f32[5,20,2]{2,1,0:T(8,128)S(1)}, f32[5,20,2]{2,1,0:T(8,128)S(1)}, u32[]{:S(2)}, u32[]{:S(2)}) collective-permute-start(f32[5,20,2]{2,1,0:T(8,128)S(1)} %get-tuple-element.18), channel_id=1, source_target_pairs={{0,1},{2,3},{4,5},{6,7},{8,9},{10,11},{12,13},{14,15},{16,17},{18,... | collective-permute-start | bytes 2408 | tf_op jit(solution)/shard_map/ppermute | solution.py:15
  15.8 1.3 %collective-permute-start.3 = (f32[5,20,2]{2,1,0:T(8,128)S(1)}, f32[5,20,2]{2,1,0:T(8,128)S(1)}, u32[]{:S(2)}, u32[]{:S(2)}) collective-permute-start(f32[5,20,2]{2,1,0:T(8,128)S(1)} %get-tuple-element.19), channel_id=1, source_target_pairs={{1,0},{3,2},{5,4},{7,6},{9,8},{11,10},{13,12},{15,14},{17,16},{19,... | collective-permute-start | bytes 2408 | tf_op jit(solution)/shard_map/ppermute | solution.py:17
  17.2 5.6 %collective-permute-start.4 = (f32[96,1,256]{2,0,1:T(8,128)S(1)}, f32[96,1,256]{2,0,1:T(8,128)S(1)}, u32[]{:S(2)}, u32[]{:S(2)}) collective-permute-start(f32[96,1,256]{2,0,1:T(8,128)S(1)} %get-tuple-element.11), channel_id=1, source_target_pairs={{2,0},{4,2},{6,4},{8,6},{10,8},{12,10},{14,12},{16,14},{18,16},{20... | collective-permute-start | bytes 294920 | tf_op jit(solution)/shard_map/ppermute | solution.py:17
  23.0 0.6 slice_bitcast_fusion.2
  23.6 0.7 slice_multiply_fusion
  24.9 1.4 %collective-permute-done.5 = f32[96,1,256]{2,0,1:T(8,128)S(1)} collective-permute-done((f32[96,1,256]{2,0,1:T(8,128)S(1)}, f32[96,1,256]{2,0,1:T(8,128)S(1)}, u32[]{:S(2)}, u32[]{:S(2)}) %collective-permute-start.5) | collective-permute-done | bytes 98336 | tf_op jit(solution)/shard_map/ppermute | solution.py:15
  26.9 1.0 %copy.13 = f32[96,18,1]{0,1,2:T(8,128)} copy(f32[96,18,1]{2,0,1:T(8,128)S(1)} %get-tuple-element.6) | data formatting | bytes 13824 | tf_op jit(solution)/shard_map/slice | solution.py:11
  28.3 2.6 %collective-permute-start.7 = (f32[96,18,1]{0,1,2:T(8,128)S(1)}, f32[96,18,1]{0,1,2:T(8,128)}, u32[]{:S(2)}, u32[]{:S(2)}) collective-permute-start(f32[96,18,1]{0,1,2:T(8,128)S(1)} %copy.15), channel_id=1, source_target_pairs={{0,1},{2,3},{4,5},{6,7},{8,9},{10,11},{12,13},{14,15},{16,17},{18,... | collective-permute-start | bytes 20744 | tf_op jit(solution)/shard_map/ppermute | solution.py:15
  30.9 1.3 %collective-permute-start.6 = (f32[96,18,1]{0,1,2:T(8,128)}, f32[96,18,1]{0,1,2:T(8,128)S(1)}, u32[]{:S(2)}, u32[]{:S(2)}) collective-permute-start(f32[96,18,1]{0,1,2:T(8,128)} %copy.13), channel_id=1, source_target_pairs={{1,0},{3,2},{5,4},{7,6},{9,8},{11,10},{13,12},{15,14},{17,16},{19,... | collective-permute-start | bytes 20744 | tf_op jit(solution)/shard_map/ppermute | solution.py:17
  32.2 1.6 %fusion.29 = (f32[16,256]{1,0:T(8,128)S(1)}, f32[16,256]{1,0:T(8,128)}, f32[16,256]{1,0:T(8,128)}, f32[16,256]{1,0:T(8,128)}, f32[16,256]{1,0:T(8,128)}) fusion(f32[20,260]{1,0:T(8,128)} %get-tuple-element.14, f32[20,259]{1,0:T(8,128)} %slice_multiply_fusion, f32[19,260]{1,0:T(8,128)} %fusion.26), kind=kLoop, calls=%fused_computation.72 | loop fusion | flops 16384 | bytes 163840 | tf_op jit(solution)/shard_map/add | solution.py:80
  33.8 0.7 slice.174
  34.4 1.4 %slice.195 = f32[16,256]{1,0:T(8,128)} slice(f32[20,260]{1,0:T(8,128)} %get-tuple-element.15), slice={[2:18], [2:258]} | slice | bytes 32768 | tf_op jit(solution)/shard_map/slice | solution.py:71
  36.2 1.0 %copy.16 = f32[96,18,1]{2,0,1:T(8,128)S(1)} copy(f32[96,18,1]{0,1,2:T(8,128)} %collective-permute-done.7) | data formatting | bytes 13824 | tf_op jit(solution)/shard_map/ppermute | solution.py:15
  37.3 3.8 %broadcast_multiply_fusion = (f32[96,16,256]{2,0,1:T(8,128)S(1)}, f32[96,16,256]{2,0,1:T(8,128)S(1)}) fusion(f32[16,256]{1,0:T(8,128)} %slice.195, f32[96,1,256]{2,0,1:T(8,128)S(1)} %copy-done.1, f32[32,16,256]{2,0,1:T(8,128)S(1)} %fusion.23, f32[64,16,256]{2,0,1:T(8,128)S(1)} %copy_multiply_fusion, f32[96,1,256]{2,0,1:T(8,128)S(1)} %collective-permute-done.5, ...), kind=kLoop, calls=%fused_computation.48 | loop fusion | flops 9437184 | bytes 5043712 | tf_op jit(solution)/shard_map/mul | solution.py:96
  41.1 5.6 %collective-permute-start.8 = (f32[64,1,256]{2,0,1:T(8,128)S(1)}, f32[64,1,256]{2,0,1:T(8,128)S(1)}, u32[]{:S(2)}, u32[]{:S(2)}) collective-permute-start(f32[64,1,256]{2,0,1:T(8,128)S(1)} %get-tuple-element.9), channel_id=1, source_target_pairs={{2,0},{4,2},{6,4},{8,6},{10,8},{12,10},{14,12},{16,14},{18,16},{20... | collective-permute-start | bytes 196616 | tf_op jit(solution)/shard_map/ppermute | solution.py:17
  46.8 1.5 %convolution_bitcast_fusion = f32[96,96]{1,0:T(8,128)S(1)} fusion(f32[96,16,256]{2,0,1:T(8,128)S(1)} %get-tuple-element.5, f32[16,256]{1,0:T(8,128)S(1)} %copy-done.7), kind=kOutput, calls=%fused_computation.29 | convolution fusion | flops 453378048 | bytes 1626112 | tf_op jit(solution)/shard_map/ac,bc->ab/dot_general | solution.py:50
  48.3 37.3 %psum.7 = f32[96,96]{1,0:T(8,128)S(1)} all-reduce(f32[96,96]{1,0:T(8,128)S(1)} %convolution_bitcast_fusion), channel_id=1, replica_groups=mesh['lon'=16,'lat'=2] {'lon','lat'}, use_global_device_ids=true, to_apply=%region_0.0 | all-reduce | flops 9216 | bytes 73728 | tf_op jit(solution)/shard_map/psum | solution.py:99
  86.6 1.3 %collective-permute-start.11 = (f32[64,18,1]{0,1,2:T(8,128)S(1)}, f32[64,18,1]{0,1,2:T(8,128)S(1)}, u32[]{:S(2)}, u32[]{:S(2)}) collective-permute-start(f32[64,18,1]{0,1,2:T(8,128)S(1)} %copy.19), channel_id=1, source_target_pairs={{0,1},{2,3},{4,5},{6,7},{8,9},{10,11},{12,13},{14,15},{16,17},{18,... | collective-permute-start | bytes 13832 | tf_op jit(solution)/shard_map/ppermute | solution.py:15
  87.9 1.3 %collective-permute-start.10 = (f32[64,18,1]{0,1,2:T(8,128)S(1)}, f32[64,18,1]{0,1,2:T(8,128)S(1)}, u32[]{:S(2)}, u32[]{:S(2)}) collective-permute-start(f32[64,18,1]{0,1,2:T(8,128)S(1)} %copy.17), channel_id=1, source_target_pairs={{1,0},{3,2},{5,4},{7,6},{9,8},{11,10},{13,12},{15,14},{17,16},{19,... | collective-permute-start | bytes 13832 | tf_op jit(solution)/shard_map/ppermute | solution.py:17
  89.2 0.6 broadcast_multiply_fusion.2
  89.9 1.1 %collective-permute-done.10 = f32[64,18,1]{0,1,2:T(8,128)S(1)} collective-permute-done((f32[64,18,1]{0,1,2:T(8,128)S(1)}, f32[64,18,1]{0,1,2:T(8,128)S(1)}, u32[]{:S(2)}, u32[]{:S(2)}) %collective-permute-start.10) | collective-permute-done | bytes 4640 | tf_op jit(solution)/shard_map/ppermute | solution.py:17
  91.6 0.8 fusion.12
  92.4 1.6 %copy.21 = f32[64,16,256]{2,1,0:T(8,128)} copy(f32[64,16,256]{2,0,1:T(8,128)S(1)} %fusion.12) | data formatting | bytes 2097152
  (52 shorter events, 4.2 us)
Async XLA Ops:
  0.6 13.4 %copy-start.8 = (s32[2,16,256]{2,1,0:T(8,128)S(1)}, s32[2,16,256]{2,1,0:T(8,128)}, u32[]{:S(2)}) copy-start(s32[2,16,256]{2,1,0:T(8,128)} %param.8) | copy-start | bytes 98308
  4.3 9.9 %collective-permute-start = (f32[5,2,256]{2,1,0:T(2,128)S(1)}, f32[5,2,256]{2,1,0:T(2,128)S(1)}, u32[]{:S(2)}, u32[]{:S(2)}) collective-permute-start(f32[5,2,256]{2,1,0:T(2,128)S(1)} %get-tuple-element.20), channel_id=1, source_target_pairs={{0,2},{2,4},{4,6},{6,8},{8,10},{10,12},{12,14},{14,16},{16,18},{18... | collective-permute-start | bytes 30728 | tf_op jit(solution)/shard_map/ppermute | solution.py:15
  7.3 6.9 %collective-permute-start.1 = (f32[5,2,256]{2,1,0:T(2,128)S(1)}, f32[5,2,256]{2,1,0:T(2,128)S(1)}, u32[]{:S(2)}, u32[]{:S(2)}) collective-permute-start(f32[5,2,256]{2,1,0:T(2,128)S(1)} %get-tuple-element.21), channel_id=1, source_target_pairs={{2,0},{4,2},{6,4},{8,6},{10,8},{12,10},{14,12},{16,14},{18,16},{20... | collective-permute-start | bytes 30728 | tf_op jit(solution)/shard_map/ppermute | solution.py:17
  14.3 8.5 %collective-permute-start.2 = (f32[5,20,2]{2,1,0:T(8,128)S(1)}, f32[5,20,2]{2,1,0:T(8,128)S(1)}, u32[]{:S(2)}, u32[]{:S(2)}) collective-permute-start(f32[5,20,2]{2,1,0:T(8,128)S(1)} %get-tuple-element.18), channel_id=1, source_target_pairs={{0,1},{2,3},{4,5},{6,7},{8,9},{10,11},{12,13},{14,15},{16,17},{18,... | collective-permute-start | bytes 2408 | tf_op jit(solution)/shard_map/ppermute | solution.py:15
  15.8 7.0 %collective-permute-start.3 = (f32[5,20,2]{2,1,0:T(8,128)S(1)}, f32[5,20,2]{2,1,0:T(8,128)S(1)}, u32[]{:S(2)}, u32[]{:S(2)}) collective-permute-start(f32[5,20,2]{2,1,0:T(8,128)S(1)} %get-tuple-element.19), channel_id=1, source_target_pairs={{1,0},{3,2},{5,4},{7,6},{9,8},{11,10},{13,12},{15,14},{17,16},{19,... | collective-permute-start | bytes 2408 | tf_op jit(solution)/shard_map/ppermute | solution.py:17
  17.1 9.2 %collective-permute-start.5 = (f32[96,1,256]{2,0,1:T(8,128)S(1)}, f32[96,1,256]{2,0,1:T(8,128)S(1)}, u32[]{:S(2)}, u32[]{:S(2)}) collective-permute-start(f32[96,1,256]{2,0,1:T(8,128)S(1)} %get-tuple-element.10), channel_id=1, source_target_pairs={{0,2},{2,4},{4,6},{6,8},{8,10},{10,12},{12,14},{14,16},{16,18},{18... | collective-permute-start | bytes 294920 | tf_op jit(solution)/shard_map/ppermute | solution.py:15
  17.2 9.1 %collective-permute-start.4 = (f32[96,1,256]{2,0,1:T(8,128)S(1)}, f32[96,1,256]{2,0,1:T(8,128)S(1)}, u32[]{:S(2)}, u32[]{:S(2)}) collective-permute-start(f32[96,1,256]{2,0,1:T(8,128)S(1)} %get-tuple-element.11), channel_id=1, source_target_pairs={{2,0},{4,2},{6,4},{8,6},{10,8},{12,10},{14,12},{16,14},{18,16},{20... | collective-permute-start | bytes 294920 | tf_op jit(solution)/shard_map/ppermute | solution.py:17
  26.3 0.6 copy-start
  27.9 9.4 %copy-start.1 = (f32[96,1,256]{2,0,1:T(8,128)S(1)}, f32[96,1,256]{2,0,1:T(8,128)}, u32[]{:S(2)}) copy-start(f32[96,1,256]{2,0,1:T(8,128)} %copy-done) | copy-start | bytes 294916
  28.3 7.9 %collective-permute-start.7 = (f32[96,18,1]{0,1,2:T(8,128)S(1)}, f32[96,18,1]{0,1,2:T(8,128)}, u32[]{:S(2)}, u32[]{:S(2)}) collective-permute-start(f32[96,18,1]{0,1,2:T(8,128)S(1)} %copy.15), channel_id=1, source_target_pairs={{0,1},{2,3},{4,5},{6,7},{8,9},{10,11},{12,13},{14,15},{16,17},{18,... | collective-permute-start | bytes 20744 | tf_op jit(solution)/shard_map/ppermute | solution.py:15
  30.9 5.0 %collective-permute-start.6 = (f32[96,18,1]{0,1,2:T(8,128)}, f32[96,18,1]{0,1,2:T(8,128)S(1)}, u32[]{:S(2)}, u32[]{:S(2)}) collective-permute-start(f32[96,18,1]{0,1,2:T(8,128)} %copy.13), channel_id=1, source_target_pairs={{1,0},{3,2},{5,4},{7,6},{9,8},{11,10},{13,12},{15,14},{17,16},{19,... | collective-permute-start | bytes 20744 | tf_op jit(solution)/shard_map/ppermute | solution.py:17
  37.3 9.5 %copy-start.7 = (f32[16,256]{1,0:T(8,128)S(1)}, f32[16,256]{1,0:T(8,128)}, u32[]{:S(2)}) copy-start(f32[16,256]{1,0:T(8,128)} %slice.195) | copy-start | bytes 49156
  41.1 44.6 %collective-permute-start.9 = (f32[64,1,256]{2,0,1:T(8,128)S(1)}, f32[64,1,256]{2,0,1:T(8,128)S(1)}, u32[]{:S(2)}, u32[]{:S(2)}) collective-permute-start(f32[64,1,256]{2,0,1:T(8,128)S(1)} %get-tuple-element.8), channel_id=1, source_target_pairs={{0,2},{2,4},{4,6},{6,8},{8,10},{10,12},{12,14},{14,16},{16,18},{18... | collective-permute-start | bytes 196616 | tf_op jit(solution)/shard_map/ppermute | solution.py:15
  41.1 44.5 %collective-permute-start.8 = (f32[64,1,256]{2,0,1:T(8,128)S(1)}, f32[64,1,256]{2,0,1:T(8,128)S(1)}, u32[]{:S(2)}, u32[]{:S(2)}) collective-permute-start(f32[64,1,256]{2,0,1:T(8,128)S(1)} %get-tuple-element.9), channel_id=1, source_target_pairs={{2,0},{4,2},{6,4},{8,6},{10,8},{12,10},{14,12},{16,14},{18,16},{20... | collective-permute-start | bytes 196616 | tf_op jit(solution)/shard_map/ppermute | solution.py:17
  86.0 5.6 %copy-start.2 = (f32[16,256]{1,0:T(8,128)S(1)}, f32[16,256]{1,0:T(8,128)}, u32[]{:S(2)}) copy-start(f32[16,256]{1,0:T(8,128)} %get-tuple-element.23) | copy-start | bytes 49156
  86.0 5.6 %copy-start.3 = (f32[16,256]{1,0:T(8,128)S(1)}, f32[16,256]{1,0:T(8,128)}, u32[]{:S(2)}) copy-start(f32[16,256]{1,0:T(8,128)} %get-tuple-element.24) | copy-start | bytes 49156
  86.0 5.6 %copy-start.4 = (f32[16,256]{1,0:T(8,128)S(1)}, f32[16,256]{1,0:T(8,128)}, u32[]{:S(2)}) copy-start(f32[16,256]{1,0:T(8,128)} %get-tuple-element.25) | copy-start | bytes 49156
  86.0 5.6 %copy-start.5 = (f32[16,256]{1,0:T(8,128)S(1)}, f32[16,256]{1,0:T(8,128)}, u32[]{:S(2)}) copy-start(f32[16,256]{1,0:T(8,128)} %get-tuple-element.26) | copy-start | bytes 49156
  86.0 5.6 %copy-start.6 = (f32[16,256]{1,0:T(8,128)S(1)}, f32[16,256]{1,0:T(8,128)}, u32[]{:S(2)}) copy-start(f32[16,256]{1,0:T(8,128)} %slice.174) | copy-start | bytes 49156
  86.6 4.6 %collective-permute-start.11 = (f32[64,18,1]{0,1,2:T(8,128)S(1)}, f32[64,18,1]{0,1,2:T(8,128)S(1)}, u32[]{:S(2)}, u32[]{:S(2)}) collective-permute-start(f32[64,18,1]{0,1,2:T(8,128)S(1)} %copy.19), channel_id=1, source_target_pairs={{0,1},{2,3},{4,5},{6,7},{8,9},{10,11},{12,13},{14,15},{16,17},{18,... | collective-permute-start | bytes 13832 | tf_op jit(solution)/shard_map/ppermute | solution.py:15
  87.9 3.1 %collective-permute-start.10 = (f32[64,18,1]{0,1,2:T(8,128)S(1)}, f32[64,18,1]{0,1,2:T(8,128)S(1)}, u32[]{:S(2)}, u32[]{:S(2)}) collective-permute-start(f32[64,18,1]{0,1,2:T(8,128)S(1)} %copy.17), channel_id=1, source_target_pairs={{1,0},{3,2},{5,4},{7,6},{9,8},{11,10},{13,12},{15,14},{17,16},{19,... | collective-permute-start | bytes 13832 | tf_op jit(solution)/shard_map/ppermute | solution.py:17
where the time goes:
time: 95.8 us; the launch traced here: 94 us
  blocking collectives  37.3 us (39%)
  starting transfers between devices  27.6 us (29%)
  local copies, waits for them, and re-layouts  12.1 us (13%)
  other arithmetic  11.9 us (12%)
  waiting for transfers between devices  2.54 us (3%)
  matrix products  1.45 us (2%)
  between operations  0.99 us (1%)
    psum x1, blocking collectives, local(): summed = lax.psum(local_gram, ('lon', 'lat'))  37.3 us
    ppermute x6, starting transfers between devices, padded_2(): lax.ppermute(head, axis, [((i + 1) % count, i) for i in range(ends)])  19.1 us
    ppermute x6, starting transfers between devices, padded_2(): lax.ppermute(tail, axis, [(i, (i + 1) % count) for i in range(ends)])  8.51 us
    unnamed x23, local copies, waits for them, and re-layouts  4.01 us
    mul x1, other arithmetic, local(): scaled = first_pass * interior[6]  3.76 us
    slice x2, local copies, waits for them, and re-layouts, window(): array[offset + shift_lon:offset + shift_lon + span_lon, offset + shift_la...  2.12 us
  transfers between devices with their start and end apart: 12, of which 2 were waited for; matrix products, arithmetic and copies ran while one was open for 12% of the time, Pallas kernels for 0%

commit v1 on v0

--- a/solution.py
+++ b/solution.py
@@ -50,6 +50,24 @@
     return jnp.einsum("ac,bc->ab", left_flat, right_flat, precision=lax.Precision.HIGHEST)
 
 
+def mesh_sum(part):
+    lons, lats = lax.axis_size("lon"), lax.axis_size("lat")
+    if lons & (lons - 1) or lats & (lats - 1):
+        return lax.psum(part, ("lon", "lat"))
+    step = 1
+    while step < lats:
+        part = part + lax.ppermute(part, "lat", [(i, i ^ step) for i in range(lats)])
+        step *= 2
+    step = 1
+    while step < lons:
+        pairs = [
+            (i * lats + j, (i ^ step) * lats + (lats - 1 - j)) for i in range(lons) for j in range(lats)
+        ]
+        part = part + lax.ppermute(part, ("lon", "lat"), pairs)
+        step *= 2
+    return part
+
+
 def local(sketch, probe_bits, ocean, east_cond, north_cond, kappa_sq, inv_area):
     lon_count, lat_count = ocean.shape
     sea_mask = ocean.astype(jnp.float32)
@@ -96,7 +114,7 @@
     scaled = first_pass * interior[6]
     second = operate(extend(scaled[:sketch_count], 1), interior)
     local_gram = pair_gram(first_pass, scaled)
-    summed = lax.psum(local_gram, ("lon", "lat"))
+    summed = mesh_sum(local_gram)
     cell_total = lax.axis_size("lon") * lon_count * lax.axis_size("lat") * lat_count
     return (second, summed / cell_total)
 

time: 95.8 us -> 69.7 us (0.73)
  blocking collectives: 37.3 us -> 0 us
  waiting for transfers between devices: 2.54 us -> 11.5 us
  starting transfers between devices: 27.6 us -> 30.9 us
    psum x1 -> x0, blocking collectives: 37.3 us -> none  [local(): summed = lax.psum(local_gram, ('lon', 'lat'))]
    ppermute x0 -> x5, waiting for transfers between devices: none -> 9.54 us  [the longest x4 9.54 us: mesh_sum(): part = part + lax.ppermute(part, ('lon', 'lat'), pairs)]
    ppermute x6, starting transfers between devices: 8.51 us -> 10.2 us  [padded_2(): lax.ppermute(tail, axis, [(i, (i + 1) % count) for i in range(ends)])]
    ppermute x0 -> x5, starting transfers between devices: none -> 1.46 us  [the longest x1 1.19 us: mesh_sum(): lax.ppermute(part, 'lat', [(i, i ^ step) for i in range(lats)])]
    ppermute x6, waiting for transfers between devices: 1.16 us -> 0.02 us  [padded_2(): lax.ppermute(head, axis, [((i + 1) % count, i) for i in range(ends)])]
  transfers between devices with their start and end apart: 12 -> 17, of which waited for: 2 -> 5; matrix products, arithmetic and copies ran while one was open for 12% -> 19% of each run, Pallas kernels for 0% -> 0%
where the time goes in v1:
time: 69.7 us; the launch traced here: 68.8 us
  starting transfers between devices  30.9 us (44%)
  local copies, waits for them, and re-layouts  12.1 us (17%)
  other arithmetic  11.9 us (17%)
  waiting for transfers between devices  11.5 us (16%)
  matrix products  1.45 us (2%)
  between operations  1.03 us (1%)
    ppermute x6, starting transfers between devices, padded_2(): lax.ppermute(head, axis, [((i + 1) % count, i) for i in range(ends)])  19.1 us
    ppermute x6, starting transfers between devices, padded_2(): lax.ppermute(tail, axis, [(i, (i + 1) % count) for i in range(ends)])  10.2 us
    ppermute x4, waiting for transfers between devices, mesh_sum(): part = part + lax.ppermute(part, ('lon', 'lat'), pairs)  9.54 us
    unnamed x23, local copies, waits for them, and re-layouts  4.01 us
    mul x1, other arithmetic, local(): scaled = first_pass * interior[6]  3.76 us
    slice x2, local copies, waits for them, and re-layouts, window(): array[offset + shift_lon:offset + shift_lon + span_lon, offset + shift_la...  2.11 us
    ppermute x6, waiting for transfers between devices, padded_2(): lax.ppermute(tail, axis, [(i, (i + 1) % count) for i in range(ends)])  1.92 us
    mul x1, other arithmetic, local(): sketch_masked = sketch * sea_mask  1.84 us
  transfers between devices with their start and end apart: 17, of which 5 were waited for; matrix products, arithmetic and copies ran while one was open for 19% of the time, Pallas kernels for 0%

profile of v1, /device:TPU:0, one launch (start us, length us, event | category | flops | bytes accessed | tf_op | source)
XLA Modules:
  0.0 68.8 jit_solution(10705173228262900051)
XLA Ops:
  0.6 0.7 %bitcast_dynamic-update-slice_fusion.4 = f32[5,16,256]{2,1,0:T(8,128)S(1)} fusion(s32[16,256]{1,0:T(8,128)} %param.9), kind=kLoop, calls=%fused_computation.77 | loop fusion | flops 4095 | bytes 32768
  1.4 0.7 %bitcast_dynamic-update-slice_fusion.3 = f32[5,16,256]{2,1,0:T(8,128)S(1)} fusion(f32[5,16,256]{2,1,0:T(8,128)S(1)} %bitcast_dynamic-update-slice_fusion.4, f32[16,256]{1,0:T(8,128)} %param.10), kind=kLoop, calls=%fused_computation.76 | loop fusion | bytes 32768
  2.1 0.7 %bitcast_dynamic-update-slice_fusion.2 = f32[5,16,256]{2,1,0:T(8,128)S(1)} fusion(f32[5,16,256]{2,1,0:T(8,128)S(1)} %bitcast_dynamic-update-slice_fusion.3, f32[16,256]{1,0:T(8,128)} %param.11), kind=kLoop, calls=%fused_computation.75 | loop fusion | bytes 32768
  2.8 0.7 %bitcast_dynamic-update-slice_fusion.1 = f32[5,16,256]{2,1,0:T(8,128)S(1)} fusion(f32[5,16,256]{2,1,0:T(8,128)S(1)} %bitcast_dynamic-update-slice_fusion.2, f32[16,256]{1,0:T(8,128)} %param.12), kind=kLoop, calls=%fused_computation.74 | loop fusion | bytes 32768
  3.5 0.7 %bitcast_dynamic-update-slice_fusion = f32[5,16,256]{2,1,0:T(8,128)S(1)} fusion(f32[5,16,256]{2,1,0:T(8,128)S(1)} %bitcast_dynamic-update-slice_fusion.1, f32[16,256]{1,0:T(8,128)} %param.13), kind=kLoop, calls=%fused_computation.73 | loop fusion | bytes 32768 | tf_op jit(solution)/shard_map/stack | solution.py:74
  4.3 3.0 %collective-permute-start = (f32[5,2,256]{2,1,0:T(2,128)S(1)}, f32[5,2,256]{2,1,0:T(2,128)S(1)}, u32[]{:S(2)}, u32[]{:S(2)}) collective-permute-start(f32[5,2,256]{2,1,0:T(2,128)S(1)} %get-tuple-element.20), channel_id=1, source_target_pairs={{0,2},{2,4},{4,6},{6,8},{8,10},{10,12},{12,14},{14,16},{16,18},{18... | collective-permute-start | bytes 30728 | tf_op jit(solution)/shard_map/ppermute | solution.py:15
  7.3 4.1 %collective-permute-start.1 = (f32[5,2,256]{2,1,0:T(2,128)S(1)}, f32[5,2,256]{2,1,0:T(2,128)S(1)}, u32[]{:S(2)}, u32[]{:S(2)}) collective-permute-start(f32[5,2,256]{2,1,0:T(2,128)S(1)} %get-tuple-element.21), channel_id=1, source_target_pairs={{2,0},{4,2},{6,4},{8,6},{10,8},{12,10},{14,12},{16,14},{18,16},{20... | collective-permute-start | bytes 30728 | tf_op jit(solution)/shard_map/ppermute | solution.py:17
  11.3 0.7 %convert_element_type.7 = f32[16,256]{1,0:T(8,128)S(1)} convert(s32[16,256]{1,0:T(8,128)} %param.9) | non-fusion elementwise | flops 4096 | bytes 32768 | tf_op jit(solution)/shard_map/convert_element_type | solution.py:73
  12.1 1.8 %copy_multiply_fusion = f32[64,16,256]{2,0,1:T(8,128)S(1)} fusion(f32[64,16,256]{2,1,0:T(8,128)} %param.7, f32[16,256]{1,0:T(8,128)S(1)} %convert_element_type.7), kind=kLoop, calls=%fused_computation.47 | loop fusion | flops 262144 | bytes 2113536 | tf_op jit(solution)/shard_map/mul | solution.py:108
  14.3 1.5 %collective-permute-start.2 = (f32[5,20,2]{2,1,0:T(8,128)S(1)}, f32[5,20,2]{2,1,0:T(8,128)S(1)}, u32[]{:S(2)}, u32[]{:S(2)}) collective-permute-start(f32[5,20,2]{2,1,0:T(8,128)S(1)} %get-tuple-element.18), channel_id=1, source_target_pairs={{0,1},{2,3},{4,5},{6,7},{8,9},{10,11},{12,13},{14,15},{16,17},{18,... | collective-permute-start | bytes 2408 | tf_op jit(solution)/shard_map/ppermute | solution.py:15
  15.8 1.3 %collective-permute-start.3 = (f32[5,20,2]{2,1,0:T(8,128)S(1)}, f32[5,20,2]{2,1,0:T(8,128)S(1)}, u32[]{:S(2)}, u32[]{:S(2)}) collective-permute-start(f32[5,20,2]{2,1,0:T(8,128)S(1)} %get-tuple-element.19), channel_id=1, source_target_pairs={{1,0},{3,2},{5,4},{7,6},{9,8},{11,10},{13,12},{15,14},{17,16},{19,... | collective-permute-start | bytes 2408 | tf_op jit(solution)/shard_map/ppermute | solution.py:17
  17.2 5.6 %collective-permute-start.4 = (f32[96,1,256]{2,0,1:T(8,128)S(1)}, f32[96,1,256]{2,0,1:T(8,128)S(1)}, u32[]{:S(2)}, u32[]{:S(2)}) collective-permute-start(f32[96,1,256]{2,0,1:T(8,128)S(1)} %get-tuple-element.11), channel_id=1, source_target_pairs={{2,0},{4,2},{6,4},{8,6},{10,8},{12,10},{14,12},{16,14},{18,16},{20... | collective-permute-start | bytes 294920 | tf_op jit(solution)/shard_map/ppermute | solution.py:17
  23.6 0.7 slice_multiply_fusion
  24.9 1.4 %collective-permute-done.5 = f32[96,1,256]{2,0,1:T(8,128)S(1)} collective-permute-done((f32[96,1,256]{2,0,1:T(8,128)S(1)}, f32[96,1,256]{2,0,1:T(8,128)S(1)}, u32[]{:S(2)}, u32[]{:S(2)}) %collective-permute-start.5) | collective-permute-done | bytes 98336 | tf_op jit(solution)/shard_map/ppermute | solution.py:15
  26.9 1.0 %copy.13 = f32[96,18,1]{0,1,2:T(8,128)} copy(f32[96,18,1]{2,0,1:T(8,128)S(1)} %get-tuple-element.6) | data formatting | bytes 13824 | tf_op jit(solution)/shard_map/slice | solution.py:11
  28.3 2.6 %collective-permute-start.7 = (f32[96,18,1]{0,1,2:T(8,128)S(1)}, f32[96,18,1]{0,1,2:T(8,128)}, u32[]{:S(2)}, u32[]{:S(2)}) collective-permute-start(f32[96,18,1]{0,1,2:T(8,128)S(1)} %copy.15), channel_id=1, source_target_pairs={{0,1},{2,3},{4,5},{6,7},{8,9},{10,11},{12,13},{14,15},{16,17},{18,... | collective-permute-start | bytes 20744 | tf_op jit(solution)/shard_map/ppermute | solution.py:15
  30.9 1.3 %collective-permute-start.6 = (f32[96,18,1]{0,1,2:T(8,128)}, f32[96,18,1]{0,1,2:T(8,128)S(1)}, u32[]{:S(2)}, u32[]{:S(2)}) collective-permute-start(f32[96,18,1]{0,1,2:T(8,128)} %copy.13), channel_id=1, source_target_pairs={{1,0},{3,2},{5,4},{7,6},{9,8},{11,10},{13,12},{15,14},{17,16},{19,... | collective-permute-start | bytes 20744 | tf_op jit(solution)/shard_map/ppermute | solution.py:17
  32.2 1.5 %fusion.29 = (f32[16,256]{1,0:T(8,128)S(1)}, f32[16,256]{1,0:T(8,128)}, f32[16,256]{1,0:T(8,128)}, f32[16,256]{1,0:T(8,128)}, f32[16,256]{1,0:T(8,128)}) fusion(f32[20,260]{1,0:T(8,128)} %get-tuple-element.14, f32[20,259]{1,0:T(8,128)} %slice_multiply_fusion, f32[19,260]{1,0:T(8,128)} %fusion.26), kind=kLoop, calls=%fused_computation.72 | loop fusion | flops 16384 | bytes 163840 | tf_op jit(solution)/shard_map/add | solution.py:98
  33.7 0.7 slice.174
  34.4 1.4 %slice.195 = f32[16,256]{1,0:T(8,128)} slice(f32[20,260]{1,0:T(8,128)} %get-tuple-element.15), slice={[2:18], [2:258]} | slice | bytes 32768 | tf_op jit(solution)/shard_map/slice | solution.py:89
  36.2 1.0 %copy.16 = f32[96,18,1]{2,0,1:T(8,128)S(1)} copy(f32[96,18,1]{0,1,2:T(8,128)} %collective-permute-done.7) | data formatting | bytes 13824 | tf_op jit(solution)/shard_map/ppermute | solution.py:15
  37.3 3.8 %broadcast_multiply_fusion = (f32[96,16,256]{2,0,1:T(8,128)S(1)}, f32[96,16,256]{2,0,1:T(8,128)S(1)}) fusion(f32[16,256]{1,0:T(8,128)} %slice.195, f32[96,1,256]{2,0,1:T(8,128)S(1)} %copy-done.1, f32[32,16,256]{2,0,1:T(8,128)S(1)} %fusion.23, f32[64,16,256]{2,0,1:T(8,128)S(1)} %copy_multiply_fusion, f32[96,1,256]{2,0,1:T(8,128)S(1)} %collective-permute-done.5, ...), kind=kLoop, calls=%fused_computation.48 | loop fusion | flops 9437184 | bytes 5043712 | tf_op jit(solution)/shard_map/mul | solution.py:114
  41.1 1.4 %convolution_bitcast_fusion = f32[96,96]{1,0:T(8,128)S(1)} fusion(f32[96,16,256]{2,0,1:T(8,128)S(1)} %get-tuple-element.5, f32[16,256]{1,0:T(8,128)S(1)} %copy-done.7), kind=kOutput, calls=%fused_computation.29 | convolution fusion | flops 453378048 | bytes 1626112 | tf_op jit(solution)/shard_map/ac,bc->ab/dot_general | solution.py:50
  42.5 1.2 %collective-permute-start.12 = (f32[96,96]{1,0:T(8,128)S(1)}, f32[96,96]{1,0:T(8,128)S(1)}, u32[]{:S(2)}, u32[]{:S(2)}) collective-permute-start(f32[96,96]{1,0:T(8,128)S(1)} %convolution_bitcast_fusion), channel_id=1, source_target_pairs={{0,1},{1,0},{2,3},{3,2},{4,5},{5,4},{6,7},{7,6},{8,9},{9,8},{10,11... | collective-permute-start | bytes 110600 | tf_op jit(solution)/shard_map/ppermute | solution.py:59
  43.8 5.6 %collective-permute-start.8 = (f32[64,1,256]{2,0,1:T(8,128)S(1)}, f32[64,1,256]{2,0,1:T(8,128)S(1)}, u32[]{:S(2)}, u32[]{:S(2)}) collective-permute-start(f32[64,1,256]{2,0,1:T(8,128)S(1)} %get-tuple-element.9), channel_id=1, source_target_pairs={{2,0},{4,2},{6,4},{8,6},{10,8},{12,10},{14,12},{16,14},{18,16},{20... | collective-permute-start | bytes 196616 | tf_op jit(solution)/shard_map/ppermute | solution.py:17
  49.6 3.8 %collective-permute-done.13 = f32[96,96]{1,0:T(8,128)S(1)} collective-permute-done((f32[96,96]{1,0:T(8,128)S(1)}, f32[96,96]{1,0:T(8,128)S(1)}, u32[]{:S(2)}, u32[]{:S(2)}) %collective-permute-start.13) | collective-permute-done | bytes 36896 | tf_op jit(solution)/shard_map/ppermute | solution.py:66
  53.6 3.7 %collective-permute-done.14 = f32[96,96]{1,0:T(8,128)S(1)} collective-permute-done((f32[96,96]{1,0:T(8,128)S(1)}, f32[96,96]{1,0:T(8,128)S(1)}, u32[]{:S(2)}, u32[]{:S(2)}) %collective-permute-start.14) | collective-permute-done | bytes 36896 | tf_op jit(solution)/shard_map/ppermute | solution.py:66
  58.0 1.3 %collective-permute-start.10 = (f32[64,18,1]{0,1,2:T(8,128)S(1)}, f32[64,18,1]{0,1,2:T(8,128)S(1)}, u32[]{:S(2)}, u32[]{:S(2)}) collective-permute-start(f32[64,18,1]{0,1,2:T(8,128)S(1)} %copy.17), channel_id=1, source_target_pairs={{1,0},{3,2},{5,4},{7,6},{9,8},{11,10},{13,12},{15,14},{17,16},{19,... | collective-permute-start | bytes 13832 | tf_op jit(solution)/shard_map/ppermute | solution.py:17
  59.6 3.0 %collective-permute-start.11 = (f32[64,18,1]{0,1,2:T(8,128)S(1)}, f32[64,18,1]{0,1,2:T(8,128)S(1)}, u32[]{:S(2)}, u32[]{:S(2)}) collective-permute-start(f32[64,18,1]{0,1,2:T(8,128)S(1)} %copy.19), channel_id=1, source_target_pairs={{0,1},{2,3},{4,5},{6,7},{8,9},{10,11},{12,13},{14,15},{16,17},{18,... | collective-permute-start | bytes 13832 | tf_op jit(solution)/shard_map/ppermute | solution.py:15
  63.8 0.8 %fusion.12 = f32[64,16,256]{2,0,1:T(8,128)S(1)} fusion(f32[64,18,1]{2,0,1:T(8,128)S(1)} %copy.20, f32[64,1,256]{2,0,1:T(8,128)S(1)} %collective-permute-done.8, f32[64,16,256]{2,0,1:T(8,128)S(1)} %slice.196, f32[64,1,256]{2,0,1:T(8,128)S(1)} %collective-permute-done.9, f32[64,18,1]{2,0,1:T(8,128)S(1)} %copy.18, f32[16,256]{1,0:T(8,128)S(1)} %copy-done.4, ...), kind=kLoop, calls=%fused_computation.33 | loop fusion | flops 4718592 | bytes 2335744 | tf_op jit(solution)/shard_map/mul | solution.py:33
  64.6 1.6 %copy.21 = f32[64,16,256]{2,1,0:T(8,128)} copy(f32[64,16,256]{2,0,1:T(8,128)S(1)} %fusion.12) | data formatting | bytes 2097152
  66.2 2.0 %collective-permute-done.16 = f32[96,96]{1,0:T(8,128)S(1)} collective-permute-done((f32[96,96]{1,0:T(8,128)S(1)}, f32[96,96]{1,0:T(8,128)S(1)}, u32[]{:S(2)}, u32[]{:S(2)}) %collective-permute-start.16) | collective-permute-done | bytes 36896 | tf_op jit(solution)/shard_map/ppermute | solution.py:66
  (65 shorter events, 6.3 us)
Async XLA Ops:
  0.6 13.4 %copy-start.8 = (s32[2,16,256]{2,1,0:T(8,128)S(1)}, s32[2,16,256]{2,1,0:T(8,128)}, u32[]{:S(2)}) copy-start(s32[2,16,256]{2,1,0:T(8,128)} %param.8) | copy-start | bytes 98308
  4.3 9.9 %collective-permute-start = (f32[5,2,256]{2,1,0:T(2,128)S(1)}, f32[5,2,256]{2,1,0:T(2,128)S(1)}, u32[]{:S(2)}, u32[]{:S(2)}) collective-permute-start(f32[5,2,256]{2,1,0:T(2,128)S(1)} %get-tuple-element.20), channel_id=1, source_target_pairs={{0,2},{2,4},{4,6},{6,8},{8,10},{10,12},{12,14},{14,16},{16,18},{18... | collective-permute-start | bytes 30728 | tf_op jit(solution)/shard_map/ppermute | solution.py:15
  7.3 6.9 %collective-permute-start.1 = (f32[5,2,256]{2,1,0:T(2,128)S(1)}, f32[5,2,256]{2,1,0:T(2,128)S(1)}, u32[]{:S(2)}, u32[]{:S(2)}) collective-permute-start(f32[5,2,256]{2,1,0:T(2,128)S(1)} %get-tuple-element.21), channel_id=1, source_target_pairs={{2,0},{4,2},{6,4},{8,6},{10,8},{12,10},{14,12},{16,14},{18,16},{20... | collective-permute-start | bytes 30728 | tf_op jit(solution)/shard_map/ppermute | solution.py:17
  14.3 8.5 %collective-permute-start.2 = (f32[5,20,2]{2,1,0:T(8,128)S(1)}, f32[5,20,2]{2,1,0:T(8,128)S(1)}, u32[]{:S(2)}, u32[]{:S(2)}) collective-permute-start(f32[5,20,2]{2,1,0:T(8,128)S(1)} %get-tuple-element.18), channel_id=1, source_target_pairs={{0,1},{2,3},{4,5},{6,7},{8,9},{10,11},{12,13},{14,15},{16,17},{18,... | collective-permute-start | bytes 2408 | tf_op jit(solution)/shard_map/ppermute | solution.py:15
  15.8 7.0 %collective-permute-start.3 = (f32[5,20,2]{2,1,0:T(8,128)S(1)}, f32[5,20,2]{2,1,0:T(8,128)S(1)}, u32[]{:S(2)}, u32[]{:S(2)}) collective-permute-start(f32[5,20,2]{2,1,0:T(8,128)S(1)} %get-tuple-element.19), channel_id=1, source_target_pairs={{1,0},{3,2},{5,4},{7,6},{9,8},{11,10},{13,12},{15,14},{17,16},{19,... | collective-permute-start | bytes 2408 | tf_op jit(solution)/shard_map/ppermute | solution.py:17
  17.1 9.2 %collective-permute-start.5 = (f32[96,1,256]{2,0,1:T(8,128)S(1)}, f32[96,1,256]{2,0,1:T(8,128)S(1)}, u32[]{:S(2)}, u32[]{:S(2)}) collective-permute-start(f32[96,1,256]{2,0,1:T(8,128)S(1)} %get-tuple-element.10), channel_id=1, source_target_pairs={{0,2},{2,4},{4,6},{6,8},{8,10},{10,12},{12,14},{14,16},{16,18},{18... | collective-permute-start | bytes 294920 | tf_op jit(solution)/shard_map/ppermute | solution.py:15
  17.2 9.1 %collective-permute-start.4 = (f32[96,1,256]{2,0,1:T(8,128)S(1)}, f32[96,1,256]{2,0,1:T(8,128)S(1)}, u32[]{:S(2)}, u32[]{:S(2)}) collective-permute-start(f32[96,1,256]{2,0,1:T(8,128)S(1)} %get-tuple-element.11), channel_id=1, source_target_pairs={{2,0},{4,2},{6,4},{8,6},{10,8},{12,10},{14,12},{16,14},{18,16},{20... | collective-permute-start | bytes 294920 | tf_op jit(solution)/shard_map/ppermute | solution.py:17
  26.3 0.6 copy-start
  27.9 9.4 %copy-start.1 = (f32[96,1,256]{2,0,1:T(8,128)S(1)}, f32[96,1,256]{2,0,1:T(8,128)}, u32[]{:S(2)}) copy-start(f32[96,1,256]{2,0,1:T(8,128)} %copy-done) | copy-start | bytes 294916
  28.3 7.9 %collective-permute-start.7 = (f32[96,18,1]{0,1,2:T(8,128)S(1)}, f32[96,18,1]{0,1,2:T(8,128)}, u32[]{:S(2)}, u32[]{:S(2)}) collective-permute-start(f32[96,18,1]{0,1,2:T(8,128)S(1)} %copy.15), channel_id=1, source_target_pairs={{0,1},{2,3},{4,5},{6,7},{8,9},{10,11},{12,13},{14,15},{16,17},{18,... | collective-permute-start | bytes 20744 | tf_op jit(solution)/shard_map/ppermute | solution.py:15
  30.9 5.0 %collective-permute-start.6 = (f32[96,18,1]{0,1,2:T(8,128)}, f32[96,18,1]{0,1,2:T(8,128)S(1)}, u32[]{:S(2)}, u32[]{:S(2)}) collective-permute-start(f32[96,18,1]{0,1,2:T(8,128)} %copy.13), channel_id=1, source_target_pairs={{1,0},{3,2},{5,4},{7,6},{9,8},{11,10},{13,12},{15,14},{17,16},{19,... | collective-permute-start | bytes 20744 | tf_op jit(solution)/shard_map/ppermute | solution.py:17
  37.3 3.8 %copy-start.7 = (f32[16,256]{1,0:T(8,128)S(1)}, f32[16,256]{1,0:T(8,128)}, u32[]{:S(2)}) copy-start(f32[16,256]{1,0:T(8,128)} %slice.195) | copy-start | bytes 49156
  42.5 6.9 %collective-permute-start.12 = (f32[96,96]{1,0:T(8,128)S(1)}, f32[96,96]{1,0:T(8,128)S(1)}, u32[]{:S(2)}, u32[]{:S(2)}) collective-permute-start(f32[96,96]{1,0:T(8,128)S(1)} %convolution_bitcast_fusion), channel_id=1, source_target_pairs={{0,1},{1,0},{2,3},{3,2},{4,5},{5,4},{6,7},{7,6},{8,9},{9,8},{10,11... | collective-permute-start | bytes 110600 | tf_op jit(solution)/shard_map/ppermute | solution.py:59
  43.7 9.8 %collective-permute-start.9 = (f32[64,1,256]{2,0,1:T(8,128)S(1)}, f32[64,1,256]{2,0,1:T(8,128)S(1)}, u32[]{:S(2)}, u32[]{:S(2)}) collective-permute-start(f32[64,1,256]{2,0,1:T(8,128)S(1)} %get-tuple-element.8), channel_id=1, source_target_pairs={{0,2},{2,4},{4,6},{6,8},{8,10},{10,12},{12,14},{14,16},{16,18},{18... | collective-permute-start | bytes 196616 | tf_op jit(solution)/shard_map/ppermute | solution.py:15
  43.8 9.7 %collective-permute-start.8 = (f32[64,1,256]{2,0,1:T(8,128)S(1)}, f32[64,1,256]{2,0,1:T(8,128)S(1)}, u32[]{:S(2)}, u32[]{:S(2)}) collective-permute-start(f32[64,1,256]{2,0,1:T(8,128)S(1)} %get-tuple-element.9), channel_id=1, source_target_pairs={{2,0},{4,2},{6,4},{8,6},{10,8},{12,10},{14,12},{16,14},{18,16},{20... | collective-permute-start | bytes 196616 | tf_op jit(solution)/shard_map/ppermute | solution.py:17
  49.4 4.0 %collective-permute-start.13 = (f32[96,96]{1,0:T(8,128)S(1)}, f32[96,96]{1,0:T(8,128)S(1)}, u32[]{:S(2)}, u32[]{:S(2)}) collective-permute-start(f32[96,96]{1,0:T(8,128)S(1)} %add.31), channel_id=1, source_target_pairs={{0,3},{1,2},{2,1},{3,0},{4,7},{5,6},{6,5},{7,4},{8,11},{9,10},{10,... | collective-permute-start | bytes 110600 | tf_op jit(solution)/shard_map/ppermute | solution.py:66
  53.4 3.9 %collective-permute-start.14 = (f32[96,96]{1,0:T(8,128)S(1)}, f32[96,96]{1,0:T(8,128)S(1)}, u32[]{:S(2)}, u32[]{:S(2)}) collective-permute-start(f32[96,96]{1,0:T(8,128)S(1)} %add.32), channel_id=1, source_target_pairs={{0,5},{1,4},{2,7},{3,6},{4,1},{5,0},{6,3},{7,2},{8,13},{9,12},{10,... | collective-permute-start | bytes 110600 | tf_op jit(solution)/shard_map/ppermute | solution.py:66
  57.3 6.4 %collective-permute-start.15 = (f32[96,96]{1,0:T(8,128)S(1)}, f32[96,96]{1,0:T(8,128)S(1)}, u32[]{:S(2)}, u32[]{:S(2)}) collective-permute-start(f32[96,96]{1,0:T(8,128)S(1)} %add.33), channel_id=1, source_target_pairs={{0,9},{1,8},{2,11},{3,10},{4,13},{5,12},{6,15},{7,14},{8,1},{9,0},... | collective-permute-start | bytes 110600 | tf_op jit(solution)/shard_map/ppermute | solution.py:66
  57.6 6.2 %copy-start.2 = (f32[16,256]{1,0:T(8,128)S(1)}, f32[16,256]{1,0:T(8,128)}, u32[]{:S(2)}) copy-start(f32[16,256]{1,0:T(8,128)} %get-tuple-element.23) | copy-start | bytes 49156
  57.6 6.2 %copy-start.3 = (f32[16,256]{1,0:T(8,128)S(1)}, f32[16,256]{1,0:T(8,128)}, u32[]{:S(2)}) copy-start(f32[16,256]{1,0:T(8,128)} %get-tuple-element.24) | copy-start | bytes 49156
  57.7 6.2 %copy-start.4 = (f32[16,256]{1,0:T(8,128)S(1)}, f32[16,256]{1,0:T(8,128)}, u32[]{:S(2)}) copy-start(f32[16,256]{1,0:T(8,128)} %get-tuple-element.25) | copy-start | bytes 49156
  57.7 6.2 %copy-start.5 = (f32[16,256]{1,0:T(8,128)S(1)}, f32[16,256]{1,0:T(8,128)}, u32[]{:S(2)}) copy-start(f32[16,256]{1,0:T(8,128)} %get-tuple-element.26) | copy-start | bytes 49156
  57.7 6.2 %copy-start.6 = (f32[16,256]{1,0:T(8,128)S(1)}, f32[16,256]{1,0:T(8,128)}, u32[]{:S(2)}) copy-start(f32[16,256]{1,0:T(8,128)} %slice.174) | copy-start | bytes 49156
  58.0 4.6 %collective-permute-start.10 = (f32[64,18,1]{0,1,2:T(8,128)S(1)}, f32[64,18,1]{0,1,2:T(8,128)S(1)}, u32[]{:S(2)}, u32[]{:S(2)}) collective-permute-start(f32[64,18,1]{0,1,2:T(8,128)S(1)} %copy.17), channel_id=1, source_target_pairs={{1,0},{3,2},{5,4},{7,6},{9,8},{11,10},{13,12},{15,14},{17,16},{19,... | collective-permute-start | bytes 13832 | tf_op jit(solution)/shard_map/ppermute | solution.py:17
  59.6 3.9 %collective-permute-start.11 = (f32[64,18,1]{0,1,2:T(8,128)S(1)}, f32[64,18,1]{0,1,2:T(8,128)S(1)}, u32[]{:S(2)}, u32[]{:S(2)}) collective-permute-start(f32[64,18,1]{0,1,2:T(8,128)S(1)} %copy.19), channel_id=1, source_target_pairs={{0,1},{2,3},{4,5},{6,7},{8,9},{10,11},{12,13},{14,15},{16,17},{18,... | collective-permute-start | bytes 13832 | tf_op jit(solution)/shard_map/ppermute | solution.py:15
  63.7 4.5 %collective-permute-start.16 = (f32[96,96]{1,0:T(8,128)S(1)}, f32[96,96]{1,0:T(8,128)S(1)}, u32[]{:S(2)}, u32[]{:S(2)}) collective-permute-start(f32[96,96]{1,0:T(8,128)S(1)} %add.34), channel_id=1, source_target_pairs={{0,17},{1,16},{2,19},{3,18},{4,21},{5,20},{6,23},{7,22},{8,25},{9,... | collective-permute-start | bytes 110600 | tf_op jit(solution)/shard_map/ppermute | solution.py:66

commit v2 on v1

v2 whole, which is shorter than its diff:
```python
import functools

import jax
import jax.numpy as jnp
from jax import lax
from jax.experimental import pallas as pl
from jax.experimental.pallas import tpu as pltpu
from jax.sharding import PartitionSpec as P

LANES = 128
BITS = 16
F32 = jnp.float32


def lane_ids(rows):
    return lax.broadcasted_iota(jnp.int32, (rows, LANES), 1)


def spread(words):
    shape = (BITS, words.shape[-1])
    shifts = lax.broadcasted_iota(jnp.int32, shape, 0)
    bits = jnp.bitwise_and(jnp.right_shift(jnp.broadcast_to(words, shape), shifts), 1)
    return (1 - 2 * bits).astype(F32)


def halves(field):
    return [field[:, h : h + LANES] for h in range(0, field.shape[-1], LANES)]


def lat_shifts(field, low_edge, high_edge):
    ids = lane_ids(field[0].shape[0])
    up = [pltpu.roll(part, LANES - 1, 1) for part in field] + [high_edge]
    down = [low_edge] + [pltpu.roll(part, 1, 1) for part in field]
    north = [jnp.where(ids == LANES - 1, up[h + 1], up[h]) for h in range(len(field))]
    south = [jnp.where(ids == 0, down[h], down[h + 1]) for h in range(len(field))]
    return north, south


def stencil(weights, middle, east, west, north, south):
    return [
        c * m - e * xe - w * xw - n * xn - s * xs
        for (c, e, w, n, s), m, xe, xw, xn, xs in zip(weights, middle, east, west, north, south)
    ]


def edge_at(edge, lane, target):
    return pltpu.roll(edge, (target - lane) % LANES, 1)


class Sizes:
    def __init__(self, sketch, probe_bits):
        self.count, self.lons, self.lats = sketch.shape
        self.words = probe_bits.shape[0]
        self.cols = self.count + BITS * self.words
        self.rows = -(-(self.count + self.words + 5) // 8) * 8
        self.edge_rows = -(-(self.count + 2) // 8) * 8
        self.lat_axis = lax.axis_size("lat")
        self.paired = self.lat_axis == 2


def edge_rows_of(sizes, low, high, lane, rows):
    if sizes.paired:
        first = lax.axis_index("lat") == 0
        picked = lax.select(first, high, low)
        shift = jnp.where(first, (lane + 1) % LANES, lane)
        return [pltpu.roll(picked, shift, 1)]
    return [pltpu.roll(low, lane, 1), pltpu.roll(high, (lane + 1) % LANES, 1)]


def pack_kernel(sizes, sk, wd, oc, ea, no, ka, ar, first_a, first_b, second_a, second_b, *edges):
    n, count = sizes.lons, sizes.count
    even = lax.rem(lax.axis_index("lon"), 2) == 0
    for first, second, ends in ((first_b, second_b, (0, n - 1)), (first_a, second_a, (n - 1, 0))):
        inner = tuple(1 if r == 0 else n - 2 for r in ends)

        def pick(get, where):
            return lax.select(even, get(where[0]), get(where[1]))

        first[0:count, :] = pick(lambda r: sk[:, r, :], ends)
        second[0:count, :] = pick(lambda r: sk[:, r, :], inner)
        for w in range(sizes.words):
            first[count + w : count + w + 1, :] = pick(lambda r: wd[w, r : r + 1, :], ends).astype(F32)
        base = count + sizes.words
        first[base : base + 1, :] = pick(lambda r: oc[r : r + 1, :], ends).astype(F32)
        for k, ref in enumerate((ea, no, ka, ar)):
            first[base + 1 + k : base + 2 + k, :] = pick(lambda r: ref[r : r + 1, :], ends)
        rest = first.shape[0] - base - 5
        if rest:
            first[base + 5 :, :] = jnp.zeros((rest, sizes.lats), F32)
        second[count : count + 1, :] = pick(lambda r: oc[r : r + 1, :], inner).astype(F32)
        second[count + 1 : count + 2, :] = pick(lambda r: ea[r : r + 1, :], inner)
        second[count + 2 :, :] = jnp.zeros((second.shape[0] - count - 2, sizes.lats), F32)

    last = sizes.lats - LANES
    for start in range(0, count, BITS):
        ids = lane_ids(BITS)
        total = [jnp.zeros((BITS, LANES), F32) for _ in edges]
        for i in range(n):
            low = sk[start : start + BITS, i, 0:LANES]
            high = sk[start : start + BITS, i, last:]
            moved = edge_rows_of(sizes, low, high, i, BITS)
            total = [jnp.where(ids == i, m, t) for m, t in zip(moved, total)]
        for edge, t in zip(edges, total):
            edge[start : start + BITS, :] = t

    def ends_of(at):
        parts = [wd[w, :, at : at + LANES].astype(F32) for w in range(sizes.words)]
        parts += [oc[:, at : at + LANES].astype(F32), no[:, at : at + LANES]]
        spare = LANES - n * len(parts)
        parts.append(jnp.zeros((spare, LANES), F32))
        return jnp.concatenate(parts, axis=0).T

    low, high = ends_of(0)[0:1, :], ends_of(last)[LANES - 1 :, :]
    if sizes.paired:
        rows = [lax.select(lax.axis_index("lat") == 0, high, low)]
    else:
        rows = [low, high]
    for edge, row in zip(edges, rows):
        edge[count:, :] = jnp.broadcast_to(row, (sizes.edge_rows - count, LANES))


def halo_rows(got_a, got_b, rows):
    even = lax.rem(lax.axis_index("lon"), 2) == 0
    a, b = got_a[rows, :], got_b[rows, :]
    return lax.select(even, b, a), lax.select(even, a, b)


def edge_columns(edge, sizes, index):
    row = edge[sizes.count : sizes.count + 1, :]
    turned = jnp.broadcast_to(row, (LANES, LANES)).T
    return turned[index * sizes.lons : (index + 1) * sizes.lons, 0:1]


def gram_kernel(
    sizes, sk, wd, oc, ea, no, ka, ar, got_a, got_b, got_low, got_high,
    gram, applied, coef, split_hi, split_lo, ext, root,
):
    n, count, lats, words = sizes.lons, sizes.count, sizes.lats, sizes.words
    base = count + words
    lat_id = lax.axis_index("lat")
    before, after = halo_rows(got_a, got_b, slice(base, base + 3))

    sea = oc[...].astype(F32)
    ext[0, 8 : 8 + n, :] = sea
    ext[0, 8 + n : 9 + n, :] = after[0:1]
    ext[1, 8 : 8 + n, :] = ea[...] * sea * ext[0, 9 : 9 + n, :]
    ext[1, 7:8, :] = before[1:2] * before[0:1] * sea[0:1]
    east_w = ext[1, 8 : 8 + n, :]
    west_w = ext[1, 7 : 7 + n, :]

    sea_low, north_low = (edge_columns(got_low, sizes, words + k) for k in (0, 1))
    sea_high = edge_columns(got_high, sizes, words)
    ids = lane_ids(n)
    sea_parts = halves(sea)
    half_north = [no[:, h * LANES : (h + 1) * LANES] * part for h, part in enumerate(sea_parts)]
    at_low = jnp.where(lat_id == 0, 0.0, 1.0)
    at_high = jnp.where(lat_id == sizes.lat_axis - 1, 0.0, 1.0)
    edge_high = jnp.broadcast_to(sea_high * at_high, (n, LANES))
    edge_low = jnp.broadcast_to(sea_low * north_low * at_low, (n, LANES))
    sea_north, _ = lat_shifts(sea_parts, edge_low, edge_high)
    _, flow_south = lat_shifts(half_north, edge_low, edge_high)
    north_w = jnp.concatenate([a * b for a, b in zip(half_north, sea_north)], axis=1)
    south_w = jnp.concatenate([a * b for a, b in zip(flow_south, sea_parts)], axis=1)
    coef[0] = sea * (ka[...] + east_w + west_w + north_w + south_w)
    coef[1] = east_w
    coef[2] = west_w
    coef[3] = north_w
    coef[4] = south_w
    root[...] = jnp.sqrt(ar[...])

    def weights_at(i):
        rows = [coef[k, i : i + 1, :] for k in range(5)]
        return list(zip(*[halves(r) for r in rows]))

    def one_block(start, get, low_edge, high_edge, keep):
        west, middle = get(-1), get(0)
        for i in range(n):
            east = get(i + 1)
            north, south = lat_shifts(
                middle, edge_at(low_edge, i, 0), edge_at(high_edge, i, LANES - 1)
            )
            out = stencil(weights_at(i), middle, east, west, north, south)
            for h, part in enumerate(out):
                if keep:
                    applied[i, pl.ds(start, BITS), h * LANES : (h + 1) * LANES] = part
                scaled = part * root[i : i + 1, h * LANES : (h + 1) * LANES]
                high = scaled.astype(jnp.bfloat16)
                at = slice(i * lats + h * LANES, i * lats + (h + 1) * LANES)
                split_hi[pl.ds(start, BITS), at] = high
                split_lo[pl.ds(start, BITS), at] = (scaled - high.astype(F32)).astype(jnp.bfloat16)
            west, middle = middle, east

    even = lax.rem(lax.axis_index("lon"), 2) == 0

    def sketch_block(k, carry):
        start = pl.multiple_of(k * BITS, BITS)
        rows = pl.ds(start, BITS)

        def get(i):
            if i == -1:
                return halves(lax.select(even, got_b[rows, :], got_a[rows, :]))
            if i == n:
                return halves(lax.select(even, got_a[rows, :], got_b[rows, :]))
            return halves(sk[rows, i, :])

        one_block(start, get, got_low[rows, :], got_high[rows, :], True)
        return carry

    lax.fori_loop(0, count // BITS, sketch_block, 0)
    for w in range(words):
        before_w, after_w = halo_rows(got_a, got_b, slice(count + w, count + w + 1))

        def get(i):
            if i == -1:
                row = before_w.astype(jnp.int32)
            elif i == n:
                row = after_w.astype(jnp.int32)
            else:
                row = wd[w, i : i + 1, :]
            return [spread(part) for part in halves(row)]

        edges = []
        for got in (got_low, got_high):
            row = got[count : count + 1, :].astype(jnp.int32)
            edges.append(spread(pltpu.roll(row, (LANES - w * n) % LANES, 1)))
        one_block(count + w * BITS, get, edges[0], edges[1], False)

    dims = (((1,), (1,)), ((), ()))
    main = lax.dot_general(split_hi[...], split_hi[...], dims, preferred_element_type=F32)
    cross = lax.dot_general(split_hi[...], split_lo[...], dims, preferred_element_type=F32)
    gram[...] = main + cross + cross.T


def edge_kernel(sizes, ar, got_a, got_b, applied, *edges):
    n, count, lats = sizes.lons, sizes.count, sizes.lats
    last = lats - LANES
    base = count + sizes.words
    even = lax.rem(lax.axis_index("lon"), 2) == 0

    def block(k, carry):
        start = pl.multiple_of(k * BITS, BITS)
        rows = pl.ds(start, BITS)
        ids = lane_ids(BITS)
        total = [jnp.zeros((BITS, LANES), F32) for _ in edges]
        for i in range(n + 2):
            if i < n:
                low = applied[i, rows, 0:LANES] * ar[i : i + 1, 0:LANES]
                high = applied[i, rows, last:] * ar[i : i + 1, last:]
            else:
                side = (got_b, got_a) if i == n else (got_a, got_b)
                low = lax.select(even, side[0][rows, 0:LANES], side[1][rows, 0:LANES])
                high = lax.select(even, side[0][rows, last:], side[1][rows, last:])
            moved = edge_rows_of(sizes, low, high, i, BITS)
            total = [jnp.where(ids == i, m, t) for m, t in zip(moved, total)]
        for edge, t in zip(edges, total):
            edge[rows, :] = t
        return carry

    lax.fori_loop(0, count // BITS, block, 0)
    tails = [jnp.zeros((8, LANES), F32) for _ in edges]
    ids, sub = lane_ids(8), lax.broadcasted_iota(jnp.int32, (8, LANES), 0)
    for k, row in enumerate((base, base + 2)):
        ends = halo_rows(got_a, got_b, slice(row, row + 1))
        for side, end in enumerate(ends):
            moved = edge_rows_of(
                sizes,
                jnp.broadcast_to(end[:, 0:LANES], (8, LANES)),
                jnp.broadcast_to(end[:, last:], (8, LANES)),
                n + side,
                8,
            )
            spot = (ids == n + side) & (sub == k)
            tails = [jnp.where(spot, m, t) for m, t in zip(moved, tails)]
    for edge, t in zip(edges, tails):
        edge[count : count + 8, :] = t


def image_kernel(
    sizes, sk, oc, ar, got_a, got_b, far_a, far_b, applied, coef, got_low, got_high, out,
):
    n, count, lats = sizes.lons, sizes.count, sizes.lats
    base = count + sizes.words
    even = lax.rem(lax.axis_index("lon"), 2) == 0
    lat_id = lax.axis_index("lat")
    at_low = jnp.where(lat_id == 0, 0.0, 1.0)
    at_high = jnp.where(lat_id == sizes.lat_axis - 1, 0.0, 1.0)
    near = halo_rows(got_a, got_b, slice(base, base + 5))
    far = halo_rows(far_a, far_b, slice(count, count + 2))
    ghost = []
    for side in (0, 1):
        rows = near[side]
        sea, east, north, kappa, area = (rows[k : k + 1] for k in range(5))
        if side == 0:
            east_w = coef[2, 0:1, :]
            west_w = far[0][1:2] * far[0][0:1] * sea
        else:
            east_w = east * sea * far[1][0:1]
            west_w = coef[1, n - 1 : n, :]
        lane = n + side
        low = got_low[count : count + 8, :]
        high = got_high[count : count + 8, :]
        edge_high = edge_at(high[0:1], lane, LANES - 1) * at_high
        edge_low = edge_at(low[0:1] * low[1:2], lane, 0) * at_low
        sea_parts = halves(sea)
        flow = halves(north * sea)
        sea_north, _ = lat_shifts(sea_parts, edge_low, edge_high)
        _, flow_south = lat_shifts(flow, edge_low, edge_high)
        north_w = jnp.concatenate([a * b for a, b in zip(flow, sea_north)], axis=1)
        south_w = jnp.concatenate([a * b for a, b in zip(flow_south, sea_parts)], axis=1)
        center = sea * (kappa + east_w + west_w + north_w + south_w)
        ghost.append(list(zip(*[halves(r * area) for r in (center, east_w, west_w, north_w, south_w)])))

    def weights_at(i):
        rows = [coef[k, i : i + 1, :] for k in range(5)]
        return list(zip(*[halves(r) for r in rows]))

    def block(k, carry):
        start = pl.multiple_of(k * BITS, BITS)
        rows = pl.ds(start, BITS)
        low_edge, high_edge = got_low[rows, :], got_high[rows, :]

        def pick(a, b):
            return halves(lax.select(even, a[rows, :], b[rows, :]))

        def get(i):
            if 0 <= i < n:
                return halves(applied[i, rows, :] * ar[i : i + 1, :])
            side = 0 if i < 0 else 1
            middle = pick(got_b, got_a) if side == 0 else pick(got_a, got_b)
            beyond = pick(far_b, far_a) if side == 0 else pick(far_a, far_b)
            inner = halves(sk[rows, 0 if side == 0 else n - 1, :])
            east, west = (inner, beyond) if side == 0 else (beyond, inner)
            north, south = lat_shifts(
                middle,
                edge_at(low_edge, n + side, 0),
                edge_at(high_edge, n + side, LANES - 1),
            )
            return stencil(ghost[side], middle, east, west, north, south)

        west, middle = get(-1), get(0)
        for i in range(n):
            east = get(i + 1)
            north, south = lat_shifts(
                middle, edge_at(low_edge, i, 0), edge_at(high_edge, i, LANES - 1)
            )
            parts = stencil(weights_at(i), middle, east, west, north, south)
            for h, part in enumerate(parts):
                out[rows, i, h * LANES : (h + 1) * LANES] = part
            west, middle = middle, east
        return carry

    lax.fori_loop(0, count // BITS, block, 0)


def call(kernel, sizes, outs, args, scratch=()):
    vmem = pl.BlockSpec(memory_space=pltpu.VMEM)
    return pl.pallas_call(
        functools.partial(kernel, sizes),
        out_shape=[jax.ShapeDtypeStruct(shape, F32) for shape in outs],
        in_specs=[vmem] * len(args),
        out_specs=[vmem] * len(outs),
        scratch_shapes=list(scratch),
    )(*args)


def mesh_sum(part):
    lons, lats = lax.axis_size("lon"), lax.axis_size("lat")
    if lons & (lons - 1) or lats & (lats - 1):
        return lax.psum(part, ("lon", "lat"))
    step = 1
    while step < lats:
        part = part + lax.ppermute(part, "lat", [(i, i ^ step) for i in range(lats)])
        step *= 2
    step = 1
    while step < lons:
        pairs = [
            (i * lats + j, (i ^ step) * lats + (lats - 1 - j)) for i in range(lons) for j in range(lats)
        ]
        part = part + lax.ppermute(part, ("lon", "lat"), pairs)
        step *= 2
    return part


def swap_edges(edges):
    count = lax.axis_size("lat")
    if len(edges) == 1:
        got = lax.ppermute(edges[0], "lat", [(0, 1), (1, 0)])
        return got, got
    low, high = edges
    from_low = lax.ppermute(high, "lat", [(i, (i + 1) % count) for i in range(count)])
    from_high = lax.ppermute(low, "lat", [((i + 1) % count, i) for i in range(count)])
    return from_low, from_high


def local(sketch, probe_bits, ocean, east_cond, north_cond, kappa_sq, inv_area):
    sizes = Sizes(sketch, probe_bits)
    n, lats, count = sizes.lons, sizes.lats, sizes.count
    lon_axis = lax.axis_size("lon")
    pairs_a = [(i, i ^ 1) for i in range(lon_axis)]
    pairs_b = [(i, (i + 1) % lon_axis if i % 2 else (i - 1) % lon_axis) for i in range(lon_axis)]
    fields = (sketch, probe_bits, ocean, east_cond, north_cond, kappa_sq, inv_area)
    line, far_line = (sizes.rows, lats), (sizes.edge_rows, lats)
    edge = (sizes.edge_rows, LANES)
    edge_count = 1 if sizes.paired else 2

    packed = call(pack_kernel, sizes, [line, line, far_line, far_line] + [edge] * edge_count, fields)
    first_a, first_b, second_a, second_b = packed[:4]
    got_b = lax.ppermute(first_b, "lon", pairs_b)
    got_a = lax.ppermute(first_a, "lon", pairs_a)
    low, high = swap_edges(packed[4:])
    far_b = lax.ppermute(second_b, "lon", pairs_b)
    far_a = lax.ppermute(second_a, "lon", pairs_a)

    gram, applied, coef = call(
        gram_kernel,
        sizes,
        [(sizes.cols, sizes.cols), (n, count, lats), (5, n, lats)],
        fields + (got_a, got_b, low, high),
        [
            pltpu.VMEM((sizes.cols, n * lats), jnp.bfloat16),
            pltpu.VMEM((sizes.cols, n * lats), jnp.bfloat16),
            pltpu.VMEM((2, n + 16, lats), F32),
            pltpu.VMEM((n, lats), F32),
        ],
    )
    edges = call(edge_kernel, sizes, [edge] * edge_count, (inv_area, got_a, got_b, applied))
    low2, high2 = swap_edges(edges)
    (image,) = call(
        image_kernel,
        sizes,
        [sketch.shape],
        (sketch, ocean, inv_area, got_a, got_b, far_a, far_b, applied, coef, low2, high2),
    )
    cells = lon_axis * n * sizes.lat_axis * lats
    return image, mesh_sum(gram) / cells


def solution(mesh):
    field, flat = P(None, "lon", "lat"), P("lon", "lat")
    return jax.shard_map(
        local,
        mesh=mesh,
        in_specs=(field, field, flat, flat, flat, flat, flat),
        out_specs=(field, P()),
        check_vma=False,
    )
```

time: 69.7 us -> 40.9 us (0.59)
  starting transfers between devices: 30.9 us -> 12.8 us
  Pallas kernels: 0 us -> 13.7 us
  local copies, waits for them, and re-layouts: 12.1 us -> 1.27 us
  other arithmetic: 11.9 us -> 1.46 us
  matrix products: 1.45 us -> 0 us
  waiting for transfers between devices: 11.5 us -> 10.8 us
    ppermute x12 -> x6, starting transfers between devices: 29.4 us -> 12.3 us  [the longest x1 4.59 us: local(): far_b = lax.ppermute(second_b, 'lon', pairs_b)]
    pallas_call x0 -> x4, Pallas kernels: none -> 13.7 us  [call(): pl.pallas_call(functools.partial(kernel, sizes), out_shape=[jax.ShapeDtyp...]
    mul x6 -> x0, other arithmetic: 7.84 us -> none  [the longest x1 3.76 us: local(): scaled = first_pass * interior[6]]
    slice x12 -> x0, local copies, waits for them, and re-layouts: 4.75 us -> none  [the longest x2 2.11 us: window(): array[offset + shift_lon:offset + shift_lon + span_lon, offset + shift_la...]
    ppermute x4, waiting for transfers between devices: 9.54 us -> 5.7 us  [mesh_sum(): part = part + lax.ppermute(part, ('lon', 'lat'), pairs)]
    unnamed x23 -> x16, local copies, waits for them, and re-layouts: 4.01 us -> 1.27 us
    ppermute x4 -> x0, local copies, waits for them, and re-layouts: 1.88 us -> none  [the longest x2 1.29 us: padded_2(): lax.ppermute(tail, axis, [(i, (i + 1) % count) for i in range(ends)])]
    ppermute x12 -> x6, waiting for transfers between devices: 1.94 us -> 3.63 us  [the longest x1 2.2 us: local(): got_b = lax.ppermute(first_b, 'lon', pairs_b)]
  transfers between devices with their start and end apart: 17 -> 11, of which waited for: 5 -> 6; matrix products, arithmetic and copies ran while one was open for 19% -> 0% of each run, Pallas kernels for 0% -> 17%
where the time goes in v2:
time: 40.9 us; the launch traced here: 40.6 us
  Pallas kernels  13.7 us (33%)
  starting transfers between devices  12.8 us (31%)
  waiting for transfers between devices  10.8 us (26%)
  other arithmetic  1.46 us (4%)
  local copies, waits for them, and re-layouts  1.27 us (3%)
  between operations  0.73 us (2%)
    pallas_call x4, Pallas kernels, call(): pl.pallas_call(functools.partial(kernel, sizes), out_shape=[jax.ShapeDtyp...  13.7 us
    ppermute x4, waiting for transfers between devices, mesh_sum(): part = part + lax.ppermute(part, ('lon', 'lat'), pairs)  5.7 us
    ppermute x1, starting transfers between devices, local(): far_b = lax.ppermute(second_b, 'lon', pairs_b)  4.59 us
    ppermute x1, starting transfers between devices, local(): got_b = lax.ppermute(first_b, 'lon', pairs_b)  4.53 us
    ppermute x1, starting transfers between devices, local(): got_a = lax.ppermute(first_a, 'lon', pairs_a)  2.97 us
    ppermute x1, waiting for transfers between devices, local(): got_b = lax.ppermute(first_b, 'lon', pairs_b)  2.2 us
    ppermute x1, waiting for transfers between devices, mesh_sum(): lax.ppermute(part, 'lat', [(i, i ^ step) for i in range(lats)])  1.44 us
    ppermute x2, waiting for transfers between devices, swap_edges(): got = lax.ppermute(edges[0], 'lat', [(0, 1), (1, 0)])  1.42 us
  transfers between devices with their start and end apart: 11, of which 6 were waited for; matrix products, arithmetic and copies ran while one was open for 0% of the time, Pallas kernels for 17%

profile of v2, /device:TPU:0, one launch (start us, length us, event | category | flops | bytes accessed | tf_op | source)
XLA Modules:
  0.0 40.6 jit_solution(8994728344945601764)
XLA Ops:
  0.6 2.5 %shard_map.86 = (f32[72,256]{1,0:T(8,128)}, f32[72,256]{1,0:T(8,128)}, f32[72,256]{1,0:T(8,128)}, f32[72,256]{1,0:T(8,128)}, f32[72,128]{1,0:T(8,128)}) custom-call(f32[64,16,256]{2,1,0:T(8,128)} %sk.5, s32[2,16,256]{2,1,0:T(8,128)} %wd.3, s32[16,256]{1,0:T(8,128)} %oc.5, f32[16,256]{1,0:T(8,128)} %ea.3, f32[16,256]{1,0:T(8,128)} %no.3, f32[16,256]{1,0:T(8,128)} %ka.3, ...), custom_call_target="tpu_custom_call" | custom-call | tf_op jit(solution)/shard_map/pallas_call | solution.py:357
  3.2 3.0 %collective-permute-start = (f32[72,256]{1,0:T(8,128)}, f32[72,256]{1,0:T(8,128)S(1)}, u32[]{:S(2)}, u32[]{:S(2)}) collective-permute-start(f32[72,256]{1,0:T(8,128)} %get-tuple-element.10), channel_id=1, source_target_pairs={{0,2},{2,0},{4,6},{6,4},{8,10},{10,8},{12,14},{14,12},{16,18},{18,... | collective-permute-start | bytes 221192 | tf_op jit(solution)/shard_map/ppermute | solution.py:409
  6.1 4.5 %collective-permute-start.1 = (f32[72,256]{1,0:T(8,128)}, f32[72,256]{1,0:T(8,128)S(1)}, u32[]{:S(2)}, u32[]{:S(2)}) collective-permute-start(f32[72,256]{1,0:T(8,128)} %get-tuple-element.11), channel_id=1, source_target_pairs={{0,30},{2,4},{4,2},{6,8},{8,6},{10,12},{12,10},{14,16},{16,14},{18... | collective-permute-start | bytes 221192 | tf_op jit(solution)/shard_map/ppermute | solution.py:408
  10.7 0.0 collective-permute-start.4
  10.7 1.4 %collective-permute-done.4.got_low.got_high = f32[72,128]{1,0:T(8,128)S(1)} collective-permute-done((f32[72,128]{1,0:T(8,128)}, f32[72,128]{1,0:T(8,128)S(1)}, u32[]{:S(2)}, u32[]{:S(2)}) %collective-permute-start.4) | collective-permute-done | bytes 36896 | tf_op jit(solution)/shard_map/ppermute | solution.py:387
  12.1 0.0 collective-permute-done.got_a
  12.1 2.2 %collective-permute-done.1.got_b = f32[72,256]{1,0:T(8,128)S(1)} collective-permute-done((f32[72,256]{1,0:T(8,128)}, f32[72,256]{1,0:T(8,128)S(1)}, u32[]{:S(2)}, u32[]{:S(2)}) %collective-permute-start.1) | collective-permute-done | bytes 73760 | tf_op jit(solution)/shard_map/ppermute | solution.py:408
  14.3 0.6 %copy-done.1 = f32[72,256]{1,0:T(8,128)} copy-done((f32[72,256]{1,0:T(8,128)}, f32[72,256]{1,0:T(8,128)S(1)}, u32[]{:S(2)}) %copy-start.1) | copy-done | bytes 73752
  14.9 4.3 %shard_map.87 = (f32[96,96]{1,0:T(8,128)}, f32[16,64,256]{2,1,0:T(8,128)}, f32[5,16,256]{2,1,0:T(8,128)}) custom-call(f32[64,16,256]{2,1,0:T(8,128)} %sk.5, s32[2,16,256]{2,1,0:T(8,128)} %wd.3, s32[16,256]{1,0:T(8,128)} %oc.5, f32[16,256]{1,0:T(8,128)} %ea.3, f32[16,256]{1,0:T(8,128)} %no.3, f32[16,256]{1,0:T(8,128)} %ka.3, f32[16,256]{1,0:T(8,128)} %ar.7, ...), custom_call_target="tpu_custom_call" | custom-call | tf_op jit(solution)/shard_map/pallas_call | solution.py:357
  19.2 0.0 collective-permute-start.6
  19.2 1.4 %collective-permute-done.6 = f32[96,96]{1,0:T(8,128)S(1)} collective-permute-done((f32[96,96]{1,0:T(8,128)}, f32[96,96]{1,0:T(8,128)S(1)}, u32[]{:S(2)}, u32[]{:S(2)}) %collective-permute-start.6) | collective-permute-done | bytes 36896 | tf_op jit(solution)/shard_map/ppermute | solution.py:372
  20.7 0.8 %add.15 = f32[96,96]{1,0:T(8,128)S(1)} add(f32[96,96]{1,0:T(8,128)} %get-tuple-element.17, f32[96,96]{1,0:T(8,128)S(1)} %collective-permute-done.6) | non-fusion elementwise | flops 9216 | bytes 110592 | tf_op jit(solution)/shard_map/add | solution.py:372
  21.5 0.1 collective-permute-start.7
  21.6 3.7 %collective-permute-done.7 = f32[96,96]{1,0:T(8,128)S(1)} collective-permute-done((f32[96,96]{1,0:T(8,128)S(1)}, f32[96,96]{1,0:T(8,128)S(1)}, u32[]{:S(2)}, u32[]{:S(2)}) %collective-permute-start.7) | collective-permute-done | bytes 36896 | tf_op jit(solution)/shard_map/ppermute | solution.py:379
  25.3 0.1 collective-permute-start.8
  25.4 0.1 collective-permute-start.2
  25.4 4.6 %collective-permute-start.3 = (f32[72,256]{1,0:T(8,128)S(1)}, f32[72,256]{1,0:T(8,128)S(1)}, u32[]{:S(2)}, u32[]{:S(2)}) collective-permute-start(f32[72,256]{1,0:T(8,128)S(1)} %copy-done.6), channel_id=1, source_target_pairs={{0,30},{2,4},{4,2},{6,8},{8,6},{10,12},{12,10},{14,16},{16,14},{18... | collective-permute-start | bytes 221192 | tf_op jit(solution)/shard_map/ppermute | solution.py:411
  30.0 0.0 collective-permute-done.8
  30.0 0.1 collective-permute-start.9
  30.1 2.4 %shard_map.88 = f32[72,128]{1,0:T(8,128)} custom-call(f32[16,256]{1,0:T(8,128)} %ar.7, f32[72,256]{1,0:T(8,128)} %copy-done, f32[72,256]{1,0:T(8,128)} %copy-done.1, f32[16,64,256]{2,1,0:T(8,128)} %get-tuple-element.15.applied), custom_call_target="tpu_custom_call" | custom-call | tf_op jit(solution)/shard_map/pallas_call | solution.py:357
  32.6 0.1 collective-permute-start.5
  32.7 1.4 %collective-permute-done.9 = f32[96,96]{1,0:T(8,128)S(1)} collective-permute-done((f32[96,96]{1,0:T(8,128)S(1)}, f32[96,96]{1,0:T(8,128)S(1)}, u32[]{:S(2)}, u32[]{:S(2)}) %collective-permute-start.9) | collective-permute-done | bytes 36896 | tf_op jit(solution)/shard_map/ppermute | solution.py:379
  34.1 0.3 collective-permute-start.10
  34.4 0.0 collective-permute-done.2.far_a
  34.4 0.0 collective-permute-done.3.far_b
  34.4 0.0 copy-start.2
  34.4 0.6 %copy-done.4 = f32[72,256]{1,0:T(8,128)} copy-done((f32[72,256]{1,0:T(8,128)}, f32[72,256]{1,0:T(8,128)S(1)}, u32[]{:S(2)}) %copy-start.4) | copy-done | bytes 73752
  35.0 0.0 copy-done.5
  35.0 0.0 copy-done.2
  35.0 4.4 %shard_map.89 = f32[64,16,256]{2,1,0:T(8,128)} custom-call(f32[64,16,256]{2,1,0:T(8,128)} %sk.5, s32[16,256]{1,0:T(8,128)} %oc.5, f32[16,256]{1,0:T(8,128)} %ar.7, f32[72,256]{1,0:T(8,128)} %copy-done, f32[72,256]{1,0:T(8,128)} %copy-done.1, f32[72,256]{1,0:T(8,128)} %copy-done.4, f32[72,256]{1,0:T(8,128)} %copy-done.5, ...), custom_call_target="tpu_custom_call" | custom-call | tf_op jit(solution)/shard_map/pallas_call | solution.py:357
  39.4 0.6 %collective-permute-done.10 = f32[96,96]{1,0:T(8,128)S(1)} collective-permute-done((f32[96,96]{1,0:T(8,128)S(1)}, f32[96,96]{1,0:T(8,128)S(1)}, u32[]{:S(2)}, u32[]{:S(2)}) %collective-permute-start.10) | collective-permute-done | bytes 36896 | tf_op jit(solution)/shard_map/ppermute | solution.py:379
  40.0 0.6 %add_multiply_fusion = f32[96,96]{1,0:T(8,128)} fusion(f32[96,96]{1,0:T(8,128)S(1)} %add.18, f32[96,96]{1,0:T(8,128)S(1)} %collective-permute-done.10), kind=kLoop, calls=%fused_computation | loop fusion | flops 18432 | bytes 110592 | tf_op jit(solution)/shard_map/div | solution.py:435
  (15 shorter events, 0.0 us)
Async XLA Ops:
  3.2 8.9 %collective-permute-start = (f32[72,256]{1,0:T(8,128)}, f32[72,256]{1,0:T(8,128)S(1)}, u32[]{:S(2)}, u32[]{:S(2)}) collective-permute-start(f32[72,256]{1,0:T(8,128)} %get-tuple-element.10), channel_id=1, source_target_pairs={{0,2},{2,0},{4,6},{6,4},{8,10},{10,8},{12,14},{14,12},{16,18},{18,... | collective-permute-start | bytes 221192 | tf_op jit(solution)/shard_map/ppermute | solution.py:409
  6.1 8.2 %collective-permute-start.1 = (f32[72,256]{1,0:T(8,128)}, f32[72,256]{1,0:T(8,128)S(1)}, u32[]{:S(2)}, u32[]{:S(2)}) collective-permute-start(f32[72,256]{1,0:T(8,128)} %get-tuple-element.11), channel_id=1, source_target_pairs={{0,30},{2,4},{4,2},{6,8},{8,6},{10,12},{12,10},{14,16},{16,14},{18... | collective-permute-start | bytes 221192 | tf_op jit(solution)/shard_map/ppermute | solution.py:408
  10.7 1.4 %collective-permute-start.4 = (f32[72,128]{1,0:T(8,128)}, f32[72,128]{1,0:T(8,128)S(1)}, u32[]{:S(2)}, u32[]{:S(2)}) collective-permute-start(f32[72,128]{1,0:T(8,128)} %get-tuple-element.14), channel_id=1, source_target_pairs={{0,1},{1,0},{2,3},{3,2},{4,5},{5,4},{6,7},{7,6},{8,9},{9,8},{10,11... | collective-permute-start | bytes 110600 | tf_op jit(solution)/shard_map/ppermute | solution.py:387
  12.1 2.2 %copy-start.3 = (f32[72,128]{1,0:T(8,128)}, f32[72,128]{1,0:T(8,128)S(1)}, u32[]{:S(2)}) copy-start(f32[72,128]{1,0:T(8,128)S(1)} %collective-permute-done.4.got_low.got_high) | copy-start | bytes 110596
  12.1 2.2 %copy-start = (f32[72,256]{1,0:T(8,128)}, f32[72,256]{1,0:T(8,128)S(1)}, u32[]{:S(2)}) copy-start(f32[72,256]{1,0:T(8,128)S(1)} %collective-permute-done.got_a) | copy-start | bytes 221188
  14.3 0.6 %copy-start.1 = (f32[72,256]{1,0:T(8,128)}, f32[72,256]{1,0:T(8,128)S(1)}, u32[]{:S(2)}) copy-start(f32[72,256]{1,0:T(8,128)S(1)} %collective-permute-done.1.got_b) | copy-start | bytes 221188
  19.2 1.4 %collective-permute-start.6 = (f32[96,96]{1,0:T(8,128)}, f32[96,96]{1,0:T(8,128)S(1)}, u32[]{:S(2)}, u32[]{:S(2)}) collective-permute-start(f32[96,96]{1,0:T(8,128)} %get-tuple-element.17), channel_id=1, source_target_pairs={{0,1},{1,0},{2,3},{3,2},{4,5},{5,4},{6,7},{7,6},{8,9},{9,8},{10,11... | collective-permute-start | bytes 110600 | tf_op jit(solution)/shard_map/ppermute | solution.py:372
  21.5 3.9 %copy-start.7 = (f32[72,256]{1,0:T(8,128)S(1)}, f32[72,256]{1,0:T(8,128)}, u32[]{:S(2)}) copy-start(f32[72,256]{1,0:T(8,128)} %get-tuple-element.12) | copy-start | bytes 221188
  21.5 3.9 %copy-start.6 = (f32[72,256]{1,0:T(8,128)S(1)}, f32[72,256]{1,0:T(8,128)}, u32[]{:S(2)}) copy-start(f32[72,256]{1,0:T(8,128)} %get-tuple-element.13) | copy-start | bytes 221188
  21.5 3.8 %collective-permute-start.7 = (f32[96,96]{1,0:T(8,128)S(1)}, f32[96,96]{1,0:T(8,128)S(1)}, u32[]{:S(2)}, u32[]{:S(2)}) collective-permute-start(f32[96,96]{1,0:T(8,128)S(1)} %add.15), channel_id=1, source_target_pairs={{0,3},{1,2},{2,1},{3,0},{4,7},{5,6},{6,5},{7,4},{8,11},{9,10},{10,... | collective-permute-start | bytes 110600 | tf_op jit(solution)/shard_map/ppermute | solution.py:379
  25.3 4.8 %collective-permute-start.8 = (f32[96,96]{1,0:T(8,128)S(1)}, f32[96,96]{1,0:T(8,128)S(1)}, u32[]{:S(2)}, u32[]{:S(2)}) collective-permute-start(f32[96,96]{1,0:T(8,128)S(1)} %add.16), channel_id=1, source_target_pairs={{0,5},{1,4},{2,7},{3,6},{4,1},{5,0},{6,3},{7,2},{8,13},{9,12},{10,... | collective-permute-start | bytes 110600 | tf_op jit(solution)/shard_map/ppermute | solution.py:379
  25.4 9.0 %collective-permute-start.2 = (f32[72,256]{1,0:T(8,128)S(1)}, f32[72,256]{1,0:T(8,128)S(1)}, u32[]{:S(2)}, u32[]{:S(2)}) collective-permute-start(f32[72,256]{1,0:T(8,128)S(1)} %copy-done.7), channel_id=1, source_target_pairs={{0,2},{2,0},{4,6},{6,4},{8,10},{10,8},{12,14},{14,12},{16,18},{18,... | collective-permute-start | bytes 221192 | tf_op jit(solution)/shard_map/ppermute | solution.py:412
  25.4 8.9 %collective-permute-start.3 = (f32[72,256]{1,0:T(8,128)S(1)}, f32[72,256]{1,0:T(8,128)S(1)}, u32[]{:S(2)}, u32[]{:S(2)}) collective-permute-start(f32[72,256]{1,0:T(8,128)S(1)} %copy-done.6), channel_id=1, source_target_pairs={{0,30},{2,4},{4,2},{6,8},{8,6},{10,12},{12,10},{14,16},{16,14},{18... | collective-permute-start | bytes 221192 | tf_op jit(solution)/shard_map/ppermute | solution.py:411
  30.0 4.0 %collective-permute-start.9 = (f32[96,96]{1,0:T(8,128)S(1)}, f32[96,96]{1,0:T(8,128)S(1)}, u32[]{:S(2)}, u32[]{:S(2)}) collective-permute-start(f32[96,96]{1,0:T(8,128)S(1)} %add.17), channel_id=1, source_target_pairs={{0,9},{1,8},{2,11},{3,10},{4,13},{5,12},{6,15},{7,14},{8,1},{9,0},... | collective-permute-start | bytes 110600 | tf_op jit(solution)/shard_map/ppermute | solution.py:379
  32.6 1.8 %collective-permute-start.5 = (f32[72,128]{1,0:T(8,128)}, f32[72,128]{1,0:T(8,128)S(1)}, u32[]{:S(2)}, u32[]{:S(2)}) collective-permute-start(f32[72,128]{1,0:T(8,128)} %shard_map.88), channel_id=1, source_target_pairs={{0,1},{1,0},{2,3},{3,2},{4,5},{5,4},{6,7},{7,6},{8,9},{9,8},{10,11... | collective-permute-start | bytes 110600 | tf_op jit(solution)/shard_map/ppermute | solution.py:387
  34.1 5.9 %collective-permute-start.10 = (f32[96,96]{1,0:T(8,128)S(1)}, f32[96,96]{1,0:T(8,128)S(1)}, u32[]{:S(2)}, u32[]{:S(2)}) collective-permute-start(f32[96,96]{1,0:T(8,128)S(1)} %add.18), channel_id=1, source_target_pairs={{0,17},{1,16},{2,19},{3,18},{4,21},{5,20},{6,23},{7,22},{8,25},{9,... | collective-permute-start | bytes 110600 | tf_op jit(solution)/shard_map/ppermute | solution.py:379
  34.4 0.6 %copy-start.4 = (f32[72,256]{1,0:T(8,128)}, f32[72,256]{1,0:T(8,128)S(1)}, u32[]{:S(2)}) copy-start(f32[72,256]{1,0:T(8,128)S(1)} %collective-permute-done.2.far_a) | copy-start | bytes 221188
  34.4 0.6 %copy-start.5 = (f32[72,256]{1,0:T(8,128)}, f32[72,256]{1,0:T(8,128)S(1)}, u32[]{:S(2)}) copy-start(f32[72,256]{1,0:T(8,128)S(1)} %collective-permute-done.3.far_b) | copy-start | bytes 221188
  34.4 0.6 %copy-start.2 = (f32[72,128]{1,0:T(8,128)}, f32[72,128]{1,0:T(8,128)S(1)}, u32[]{:S(2)}) copy-start(f32[72,128]{1,0:T(8,128)S(1)} %collective-permute-done.5.got_low.got_high) | copy-start | bytes 110596

commit v3 on v2

--- a/solution.py
+++ b/solution.py
@@ -6,6 +6,7 @@
 from jax.experimental import pallas as pl
 from jax.experimental.pallas import tpu as pltpu
 from jax.sharding import PartitionSpec as P
+
 
 LANES = 128
 BITS = 16
@@ -56,9 +57,11 @@
         self.edge_rows = -(-(self.count + 2) // 8) * 8
         self.lat_axis = lax.axis_size("lat")
         self.paired = self.lat_axis == 2
-
-
-def edge_rows_of(sizes, low, high, lane, rows):
+        self.folded = 4 * self.cols == 3 * LANES and self.cols % 48 == 0
+        self.cells = lax.axis_size("lon") * self.lons * self.lat_axis * self.lats
+
+
+def edge_rows_of(sizes, low, high, lane):
     if sizes.paired:
         first = lax.axis_index("lat") == 0
         picked = lax.select(first, high, low)
@@ -67,30 +70,39 @@
     return [pltpu.roll(low, lane, 1), pltpu.roll(high, (lane + 1) % LANES, 1)]
 
 
-def pack_kernel(sizes, sk, wd, oc, ea, no, ka, ar, first_a, first_b, second_a, second_b, *edges):
+def end_row(sizes, sk, wd, oc, fields, first, r):
+    count, base = sizes.count, sizes.count + sizes.words
+    first[0:count, :] = sk[:, r, :]
+    for w in range(sizes.words):
+        first[count + w : count + w + 1, :] = wd[w, r : r + 1, :].astype(F32)
+    first[base : base + 1, :] = oc[r : r + 1, :].astype(F32)
+    for k, ref in enumerate(fields):
+        first[base + 1 + k : base + 2 + k, :] = ref[r : r + 1, :]
+    rest = first.shape[0] - base - 5
+    if rest:
+        first[base + 5 :, :] = jnp.zeros((rest, sizes.lats), F32)
+
+
+def load_kernel(sizes, *refs):
+    given, held, rows, sems = refs[:7], refs[7:14], refs[14:18], refs[18]
     n, count = sizes.lons, sizes.count
-    even = lax.rem(lax.axis_index("lon"), 2) == 0
-    for first, second, ends in ((first_b, second_b, (0, n - 1)), (first_a, second_a, (n - 1, 0))):
-        inner = tuple(1 if r == 0 else n - 2 for r in ends)
-
-        def pick(get, where):
-            return lax.select(even, get(where[0]), get(where[1]))
-
-        first[0:count, :] = pick(lambda r: sk[:, r, :], ends)
-        second[0:count, :] = pick(lambda r: sk[:, r, :], inner)
-        for w in range(sizes.words):
-            first[count + w : count + w + 1, :] = pick(lambda r: wd[w, r : r + 1, :], ends).astype(F32)
-        base = count + sizes.words
-        first[base : base + 1, :] = pick(lambda r: oc[r : r + 1, :], ends).astype(F32)
-        for k, ref in enumerate((ea, no, ka, ar)):
-            first[base + 1 + k : base + 2 + k, :] = pick(lambda r: ref[r : r + 1, :], ends)
-        rest = first.shape[0] - base - 5
-        if rest:
-            first[base + 5 :, :] = jnp.zeros((rest, sizes.lats), F32)
-        second[count : count + 1, :] = pick(lambda r: oc[r : r + 1, :], inner).astype(F32)
-        second[count + 1 : count + 2, :] = pick(lambda r: ea[r : r + 1, :], inner)
-        second[count + 2 :, :] = jnp.zeros((second.shape[0] - count - 2, sizes.lats), F32)
-
+    copies = [pltpu.make_async_copy(g, h, sems.at[k]) for k, (g, h) in enumerate(zip(given, held))]
+    for copy in copies:
+        copy.start()
+    for copy in copies:
+        copy.wait()
+    sk, wd, oc, ea = held[:4]
+    for ref, r in zip(rows[:2], (n - 1, 0)):
+        end_row(sizes, sk, wd, oc, held[3:], ref, r)
+    for ref, r in zip(rows[2:], (n - 2, 1)):
+        ref[0:count, :] = sk[:, r, :]
+        ref[count : count + 1, :] = oc[r : r + 1, :].astype(F32)
+        ref[count + 1 : count + 2, :] = ea[r : r + 1, :]
+        ref[count + 2 :, :] = jnp.zeros((ref.shape[0] - count - 2, sizes.lats), F32)
+
+
+def pack_kernel(sizes, sk, wd, oc, no, *edges):
+    n, count = sizes.lons, sizes.count
     last = sizes.lats - LANES
     for start in range(0, count, BITS):
         ids = lane_ids(BITS)
@@ -98,7 +110,7 @@
         for i in range(n):
             low = sk[start : start + BITS, i, 0:LANES]
             high = sk[start : start + BITS, i, last:]
-            moved = edge_rows_of(sizes, low, high, i, BITS)
+            moved = edge_rows_of(sizes, low, high, i)
             total = [jnp.where(ids == i, m, t) for m, t in zip(moved, total)]
         for edge, t in zip(edges, total):
             edge[start : start + BITS, :] = t
@@ -119,12 +131,6 @@
         edge[count:, :] = jnp.broadcast_to(row, (sizes.edge_rows - count, LANES))
 
 
-def halo_rows(got_a, got_b, rows):
-    even = lax.rem(lax.axis_index("lon"), 2) == 0
-    a, b = got_a[rows, :], got_b[rows, :]
-    return lax.select(even, b, a), lax.select(even, a, b)
-
-
 def edge_columns(edge, sizes, index):
     row = edge[sizes.count : sizes.count + 1, :]
     turned = jnp.broadcast_to(row, (LANES, LANES)).T
@@ -132,13 +138,13 @@
 
 
 def gram_kernel(
-    sizes, sk, wd, oc, ea, no, ka, ar, got_a, got_b, got_low, got_high,
-    gram, applied, coef, split_hi, split_lo, ext, root,
+    sizes, sk, wd, oc, ea, no, ka, ar, west_row, east_row, got_low, got_high,
+    gram, applied, coef, split_hi, split_lo, ext, root, whole,
 ):
     n, count, lats, words = sizes.lons, sizes.count, sizes.lats, sizes.words
     base = count + words
     lat_id = lax.axis_index("lat")
-    before, after = halo_rows(got_a, got_b, slice(base, base + 3))
+    before, after = west_row[base : base + 3, :], east_row[base : base + 1, :]
 
     sea = oc[...].astype(F32)
     ext[0, 8 : 8 + n, :] = sea
@@ -190,17 +196,15 @@
                 split_lo[pl.ds(start, BITS), at] = (scaled - high.astype(F32)).astype(jnp.bfloat16)
             west, middle = middle, east
 
-    even = lax.rem(lax.axis_index("lon"), 2) == 0
-
     def sketch_block(k, carry):
         start = pl.multiple_of(k * BITS, BITS)
         rows = pl.ds(start, BITS)
 
         def get(i):
             if i == -1:
-                return halves(lax.select(even, got_b[rows, :], got_a[rows, :]))
+                return halves(west_row[rows, :])
             if i == n:
-                return halves(lax.select(even, got_a[rows, :], got_b[rows, :]))
+                return halves(east_row[rows, :])
             return halves(sk[rows, i, :])
 
         one_block(start, get, got_low[rows, :], got_high[rows, :], True)
@@ -208,7 +212,7 @@
 
     lax.fori_loop(0, count // BITS, sketch_block, 0)
     for w in range(words):
-        before_w, after_w = halo_rows(got_a, got_b, slice(count + w, count + w + 1))
+        before_w, after_w = (ref[count + w : count + w + 1, :] for ref in (west_row, east_row))
 
         def get(i):
             if i == -1:
@@ -228,14 +232,41 @@
     dims = (((1,), (1,)), ((), ()))
     main = lax.dot_general(split_hi[...], split_hi[...], dims, preferred_element_type=F32)
     cross = lax.dot_general(split_hi[...], split_lo[...], dims, preferred_element_type=F32)
-    gram[...] = main + cross + cross.T
-
-
-def edge_kernel(sizes, ar, got_a, got_b, applied, *edges):
+    total = main + cross + cross.T
+    if not sizes.folded:
+        gram[...] = total
+        return
+    block, short = sizes.cols // 3, sizes.cols // 6
+    whole[:, 0 : sizes.cols] = total
+    rows = [whole[k * short : (k + 1) * short, :] for k in range(6)]
+    ids = lane_ids(block)
+    gram[0:block, :] = jnp.where(ids < sizes.cols, whole[0:block, :], pltpu.roll(whole[block : 2 * block, :], 2 * block, 1))
+    ids = lane_ids(short) // block
+    moved = [pltpu.roll(rows[2], 2 * block, 1), pltpu.roll(rows[3], 3 * block, 1), rows[4], pltpu.roll(rows[5], block, 1)]
+    gram[block:, :] = jnp.where(ids == 0, moved[0], jnp.where(ids == 1, moved[1], jnp.where(ids == 2, moved[2], moved[3])))
+
+
+def unfold_kernel(sizes, mine, other, out):
+    total = (mine[...] + other[...]) / sizes.cells
+    if not sizes.folded:
+        out[...] = total
+        return
+    block = sizes.cols // 3
+    top, low = total[0:block, :], total[block:, :]
+    ids = lane_ids(block)
+    middle = jnp.concatenate([pltpu.roll(low, 2 * block, 1), pltpu.roll(low, block, 1)], axis=0)
+    second = jnp.where(ids < 2 * block, pltpu.roll(top, 2 * block, 1), middle)
+    third = jnp.concatenate([low, pltpu.roll(low, 3 * block, 1)], axis=0)
+    upper = jnp.concatenate([top, second, third, jnp.zeros((block, LANES), F32)], axis=0)
+    across = lane_ids(LANES) // block
+    down = lax.broadcasted_iota(jnp.int32, (LANES, LANES), 0) // block
+    out[...] = jnp.where(down <= across, upper, upper.T)[0 : sizes.cols, 0 : sizes.cols]
+
+
+def edge_kernel(sizes, ar, west_row, east_row, applied, *edges):
     n, count, lats = sizes.lons, sizes.count, sizes.lats
     last = lats - LANES
     base = count + sizes.words
-    even = lax.rem(lax.axis_index("lon"), 2) == 0
 
     def block(k, carry):
         start = pl.multiple_of(k * BITS, BITS)
@@ -247,10 +278,9 @@
                 low = applied[i, rows, 0:LANES] * ar[i : i + 1, 0:LANES]
                 high = applied[i, rows, last:] * ar[i : i + 1, last:]
             else:
-                side = (got_b, got_a) if i == n else (got_a, got_b)
-                low = lax.select(even, side[0][rows, 0:LANES], side[1][rows, 0:LANES])
-                high = lax.select(even, side[0][rows, last:], side[1][rows, last:])
-            moved = edge_rows_of(sizes, low, high, i, BITS)
+                side = west_row if i == n else east_row
+                low, high = side[rows, 0:LANES], side[rows, last:]
+            moved = edge_rows_of(sizes, low, high, i)
             total = [jnp.where(ids == i, m, t) for m, t in zip(moved, total)]
         for edge, t in zip(edges, total):
             edge[rows, :] = t
@@ -260,14 +290,13 @@
     tails = [jnp.zeros((8, LANES), F32) for _ in edges]
     ids, sub = lane_ids(8), lax.broadcasted_iota(jnp.int32, (8, LANES), 0)
     for k, row in enumerate((base, base + 2)):
-        ends = halo_rows(got_a, got_b, slice(row, row + 1))
+        ends = [ref[row : row + 1, :] for ref in (west_row, east_row)]
         for side, end in enumerate(ends):
             moved = edge_rows_of(
                 sizes,
                 jnp.broadcast_to(end[:, 0:LANES], (8, LANES)),
                 jnp.broadcast_to(end[:, last:], (8, LANES)),
                 n + side,
-                8,
             )
             spot = (ids == n + side) & (sub == k)
             tails = [jnp.where(spot, m, t) for m, t in zip(moved, tails)]
@@ -276,16 +305,15 @@
 
 
 def image_kernel(
-    sizes, sk, oc, ar, got_a, got_b, far_a, far_b, applied, coef, got_low, got_high, out,
+    sizes, sk, oc, ar, west_row, east_row, far_west, far_east, applied, coef, got_low, got_high, out,
 ):
-    n, count, lats = sizes.lons, sizes.count, sizes.lats
+    n, count = sizes.lons, sizes.count
     base = count + sizes.words
-    even = lax.rem(lax.axis_index("lon"), 2) == 0
     lat_id = lax.axis_index("lat")
     at_low = jnp.where(lat_id == 0, 0.0, 1.0)
     at_high = jnp.where(lat_id == sizes.lat_axis - 1, 0.0, 1.0)
-    near = halo_rows(got_a, got_b, slice(base, base + 5))
-    far = halo_rows(far_a, far_b, slice(count, count + 2))
+    near = [ref[base : base + 5, :] for ref in (west_row, east_row)]
+    far = [ref[count : count + 2, :] for ref in (far_west, far_east)]
     ghost = []
     for side in (0, 1):
         rows = near[side]
@@ -319,15 +347,12 @@
         rows = pl.ds(start, BITS)
         low_edge, high_edge = got_low[rows, :], got_high[rows, :]
 
-        def pick(a, b):
-            return halves(lax.select(even, a[rows, :], b[rows, :]))
-
         def get(i):
             if 0 <= i < n:
                 return halves(applied[i, rows, :] * ar[i : i + 1, :])
             side = 0 if i < 0 else 1
-            middle = pick(got_b, got_a) if side == 0 else pick(got_a, got_b)
-            beyond = pick(far_b, far_a) if side == 0 else pick(far_a, far_b)
+            middle = halves((west_row, east_row)[side][rows, :])
+            beyond = halves((far_west, far_east)[side][rows, :])
             inner = halves(sk[rows, 0 if side == 0 else n - 1, :])
             east, west = (inner, beyond) if side == 0 else (beyond, inner)
             north, south = lat_shifts(
@@ -352,33 +377,31 @@
     lax.fori_loop(0, count // BITS, block, 0)
 
 
-def call(kernel, sizes, outs, args, scratch=()):
+def call(kernel, sizes, outs, args, scratch=(), inputs=pltpu.VMEM, limit=16 << 20):
+    outs = [o if isinstance(o, jax.ShapeDtypeStruct) else jax.ShapeDtypeStruct(o, F32) for o in outs]
     vmem = pl.BlockSpec(memory_space=pltpu.VMEM)
     return pl.pallas_call(
         functools.partial(kernel, sizes),
-        out_shape=[jax.ShapeDtypeStruct(shape, F32) for shape in outs],
-        in_specs=[vmem] * len(args),
+        out_shape=outs,
+        in_specs=[pl.BlockSpec(memory_space=inputs)] * len(args),
         out_specs=[vmem] * len(outs),
         scratch_shapes=list(scratch),
+        compiler_params=pltpu.CompilerParams(vmem_limit_bytes=limit),
     )(*args)
 
 
-def mesh_sum(part):
+def exchanges():
     lons, lats = lax.axis_size("lon"), lax.axis_size("lat")
-    if lons & (lons - 1) or lats & (lats - 1):
-        return lax.psum(part, ("lon", "lat"))
-    step = 1
-    while step < lats:
-        part = part + lax.ppermute(part, "lat", [(i, i ^ step) for i in range(lats)])
-        step *= 2
-    step = 1
-    while step < lons:
-        pairs = [
-            (i * lats + j, (i ^ step) * lats + (lats - 1 - j)) for i in range(lons) for j in range(lats)
-        ]
-        part = part + lax.ppermute(part, ("lon", "lat"), pairs)
-        step *= 2
-    return part
+    steps = [[(i * lats + j, i * lats + (j ^ bit)) for i in range(lons) for j in range(lats)] for bit in powers(lats)]
+    steps += [
+        [(i * lats + j, (i ^ bit) * lats + (lats - 1 - j)) for i in range(lons) for j in range(lats)]
+        for bit in powers(lons)
+    ]
+    return steps
+
+
+def powers(limit):
+    return [1 << k for k in range(limit.bit_length() - 1)]
 
 
 def swap_edges(edges):
@@ -396,43 +419,59 @@
     sizes = Sizes(sketch, probe_bits)
     n, lats, count = sizes.lons, sizes.lats, sizes.count
     lon_axis = lax.axis_size("lon")
-    pairs_a = [(i, i ^ 1) for i in range(lon_axis)]
-    pairs_b = [(i, (i + 1) % lon_axis if i % 2 else (i - 1) % lon_axis) for i in range(lon_axis)]
+    eastward = [(i, (i + 1) % lon_axis) for i in range(lon_axis)]
+    westward = [((i + 1) % lon_axis, i) for i in range(lon_axis)]
     fields = (sketch, probe_bits, ocean, east_cond, north_cond, kappa_sq, inv_area)
     line, far_line = (sizes.rows, lats), (sizes.edge_rows, lats)
     edge = (sizes.edge_rows, LANES)
     edge_count = 1 if sizes.paired else 2
 
-    packed = call(pack_kernel, sizes, [line, line, far_line, far_line] + [edge] * edge_count, fields)
-    first_a, first_b, second_a, second_b = packed[:4]
-    got_b = lax.ppermute(first_b, "lon", pairs_b)
-    got_a = lax.ppermute(first_a, "lon", pairs_a)
-    low, high = swap_edges(packed[4:])
-    far_b = lax.ppermute(second_b, "lon", pairs_b)
-    far_a = lax.ppermute(second_a, "lon", pairs_a)
+    shapes = [jax.ShapeDtypeStruct(f.shape, f.dtype) for f in fields]
+    *fields, to_east, to_west, far_to_east, far_to_west = call(
+        load_kernel,
+        sizes,
+        shapes + [line, line, far_line, far_line],
+        [pltpu.with_memory_space_constraint(f, pltpu.HBM) for f in fields],
+        [pltpu.SemaphoreType.DMA((7,))],
+        inputs=pltpu.HBM,
+    )
+    fields = tuple(fields)
+    sketch, probe_bits, ocean, _, north_cond, _, inv_area = fields
+    west_row = lax.ppermute(to_east, "lon", eastward)
+    east_row = lax.ppermute(to_west, "lon", westward)
+    far_east = lax.ppermute(far_to_west, "lon", westward)
+    packed = call(pack_kernel, sizes, [edge] * edge_count, (sketch, probe_bits, ocean, north_cond))
+    low, high = swap_edges(packed)
+    far_west = lax.ppermute(far_to_east, "lon", eastward)
 
     gram, applied, coef = call(
         gram_kernel,
         sizes,
-        [(sizes.cols, sizes.cols), (n, count, lats), (5, n, lats)],
-        fields + (got_a, got_b, low, high),
+        [(sizes.cols // 2, LANES) if sizes.folded else (sizes.cols, sizes.cols), (n, count, lats), (5, n, lats)],
+        fields + (west_row, east_row, low, high),
         [
             pltpu.VMEM((sizes.cols, n * lats), jnp.bfloat16),
             pltpu.VMEM((sizes.cols, n * lats), jnp.bfloat16),
             pltpu.VMEM((2, n + 16, lats), F32),
             pltpu.VMEM((n, lats), F32),
+            pltpu.VMEM((sizes.cols, LANES), F32),
         ],
     )
-    edges = call(edge_kernel, sizes, [edge] * edge_count, (inv_area, got_a, got_b, applied))
+    edges = call(edge_kernel, sizes, [edge] * edge_count, (inv_area, west_row, east_row, applied))
     low2, high2 = swap_edges(edges)
     (image,) = call(
         image_kernel,
         sizes,
         [sketch.shape],
-        (sketch, ocean, inv_area, got_a, got_b, far_a, far_b, applied, coef, low2, high2),
+        (sketch, ocean, inv_area, west_row, east_row, far_west, far_east, applied, coef, low2, high2),
     )
-    cells = lon_axis * n * sizes.lat_axis * lats
-    return image, mesh_sum(gram) / cells
+    steps = exchanges()
+    for k, pairs in enumerate(steps):
+        other = lax.ppermute(gram, ("lon", "lat"), pairs)
+        if k < len(steps) - 1:
+            gram = gram + other
+    (gram,) = call(unfold_kernel, sizes, [(sizes.cols, sizes.cols)], (gram, other))
+    return image, gram
 
 
 def solution(mesh):

time: 40.9 us -> 33.3 us (0.81)
  Pallas kernels: 13.7 us -> 8.28 us
  other arithmetic: 1.46 us -> 0.02 us
  local copies, waits for them, and re-layouts: 1.27 us -> 0 us
  starting transfers between devices: 12.8 us -> 13.8 us
  waiting for transfers between devices: 10.8 us -> 10.3 us
    pallas_call x4 -> x6, Pallas kernels: 13.7 us -> 8.28 us  [call(): pl.pallas_call(functools.partial(kernel, sizes), out_shape=outs, in_specs...]
    unnamed x16 -> x0, local copies, waits for them, and re-layouts: 1.27 us -> none
    ppermute x9, starting transfers between devices: 12.6 us -> 13.6 us  [the longest x1 4.12 us: local(): far_east = lax.ppermute(far_to_west, 'lon', westward)]
    add x4, other arithmetic: 0.83 us -> 0.02 us  [local(): gram = gram + other]
    div x1 -> x0, other arithmetic: 0.63 us -> none  [local(): return (image, mesh_sum(gram) / cells)]
  transfers between devices with their start and end apart: 11 -> 11, of which waited for: 6 -> 6; matrix products, arithmetic and copies ran while one was open for 0% -> 0% of each run, Pallas kernels for 17% -> 11%
where the time goes in v3:
time: 33.3 us; the launch traced here: 33.1 us
  starting transfers between devices  13.8 us (41%)
  waiting for transfers between devices  10.3 us (31%)
  Pallas kernels  8.28 us (25%)
  between operations  0.69 us (2%)
    ppermute x5, waiting for transfers between devices, local(): other = lax.ppermute(gram, ('lon', 'lat'), pairs)  8.58 us
    pallas_call x6, Pallas kernels, call(): pl.pallas_call(functools.partial(kernel, sizes), out_shape=outs, in_specs...  8.28 us
    ppermute x1, starting transfers between devices, local(): far_east = lax.ppermute(far_to_west, 'lon', westward)  4.12 us
    ppermute x1, starting transfers between devices, local(): east_row = lax.ppermute(to_west, 'lon', westward)  4.06 us
    ppermute x1, starting transfers between devices, local(): west_row = lax.ppermute(to_east, 'lon', eastward)  3.02 us
    ppermute x1, starting transfers between devices, local(): far_west = lax.ppermute(far_to_east, 'lon', eastward)  1.5 us
    ppermute x2, waiting for transfers between devices, swap_edges(): got = lax.ppermute(edges[0], 'lat', [(0, 1), (1, 0)])  1.2 us
    ppermute x5, starting transfers between devices, local(): other = lax.ppermute(gram, ('lon', 'lat'), pairs)  0.95 us
  transfers between devices with their start and end apart: 11, of which 6 were waited for; matrix products, arithmetic and copies ran while one was open for 0% of the time, Pallas kernels for 11%

profile of v3, /device:TPU:0, one launch (start us, length us, event | category | flops | bytes accessed | tf_op | source)
XLA Modules:
  0.0 33.1 jit_solution(13896638204415944723)
XLA Ops:
  0.6 1.4 %shard_map.86 = (f32[64,16,256]{2,1,0:T(8,128)S(1)}, s32[2,16,256]{2,1,0:T(8,128)S(1)}, s32[16,256]{1,0:T(8,128)S(1)}, f32[16,256]{1,0:T(8,128)S(1)}, f32[16,256...) custom-call(f32[64,16,256]{2,1,0:T(8,128)} %refs_0_.1, ...), custom_call_target="tpu_custom_call" | custom-call | tf_op jit(solution)/shard_map/pallas_call | solution.py:383
  2.1 3.0 %collective-permute-start = (f32[72,256]{1,0:T(8,128)S(1)}, f32[72,256]{1,0:T(8,128)S(1)}, u32[]{:S(2)}, u32[]{:S(2)}) collective-permute-start(f32[72,256]{1,0:T(8,128)S(1)} %get-tuple-element.19), channel_id=1, source_target_pairs={{0,2},{2,4},{4,6},{6,8},{8,10},{10,12},{12,14},{14,16},{16,18},{18... | collective-permute-start | bytes 221192 | tf_op jit(solution)/shard_map/ppermute | solution.py:440
  5.1 4.1 %collective-permute-start.1 = (f32[72,256]{1,0:T(8,128)S(1)}, f32[72,256]{1,0:T(8,128)S(1)}, u32[]{:S(2)}, u32[]{:S(2)}) collective-permute-start(f32[72,256]{1,0:T(8,128)S(1)} %get-tuple-element.20), channel_id=1, source_target_pairs={{2,0},{4,2},{6,4},{8,6},{10,8},{12,10},{14,12},{16,14},{18,16},{20... | collective-permute-start | bytes 221192 | tf_op jit(solution)/shard_map/ppermute | solution.py:441
  9.1 0.5 %shard_map.87 = f32[72,128]{1,0:T(8,128)S(1)} custom-call(f32[64,16,256]{2,1,0:T(8,128)S(1)} %get-tuple-element.16.sk, s32[2,16,256]{2,1,0:T(8,128)S(1)} %get-tuple-element.23.wd, s32[16,256]{1,0:T(8,128)S(1)} %get-tuple-element.17.oc, f32[16,256]{1,0:T(8,128)S(1)} %get-tuple-element.25.no), custom_call_target="tpu_custom_call" | custom-call | tf_op jit(solution)/shard_map/pallas_call | solution.py:383
  9.6 0.1 collective-permute-start.4
  9.7 1.2 %collective-permute-done.4.got_low.got_high = f32[72,128]{1,0:T(8,128)S(1)} collective-permute-done((f32[72,128]{1,0:T(8,128)S(1)}, f32[72,128]{1,0:T(8,128)S(1)}, u32[]{:S(2)}, u32[]{:S(2)}) %collective-permute-start.4) | collective-permute-done | bytes 36896 | tf_op jit(solution)/shard_map/ppermute | solution.py:410
  10.9 0.6 %collective-permute-done.west_row = f32[72,256]{1,0:T(8,128)S(1)} collective-permute-done((f32[72,256]{1,0:T(8,128)S(1)}, f32[72,256]{1,0:T(8,128)S(1)}, u32[]{:S(2)}, u32[]{:S(2)}) %collective-permute-start) | collective-permute-done | bytes 73760 | tf_op jit(solution)/shard_map/ppermute | solution.py:440
  11.4 0.0 collective-permute-done.1.east_row
  11.5 2.3 %shard_map.88 = (f32[48,128]{1,0:T(8,128)S(1)}, f32[16,64,256]{2,1,0:T(8,128)S(1)}, f32[5,16,256]{2,1,0:T(8,128)S(1)}) custom-call(f32[64,16,256]{2,1,0:T(8,128)S(1)} %get-tuple-element.16.sk, s32[2,16,256]{2,1,0:T(8,128)S(1)} %get-tuple-element.23.wd, s32[16,256]{1,0:T(8,128)S(1)} %get-tuple-element.17.oc, f32[16,256]{1,0:T(8,128)S(1)} %get-tuple-element.24.ea, ...), custom_call_target="tpu_custom_call" | custom-call | tf_op jit(solution)/shard_map/pallas_call | solution.py:383
  13.8 0.1 collective-permute-start.6
  13.9 1.2 %collective-permute-done.6 = f32[48,128]{1,0:T(8,128)S(1)} collective-permute-done((f32[48,128]{1,0:T(8,128)S(1)}, f32[48,128]{1,0:T(8,128)S(1)}, u32[]{:S(2)}, u32[]{:S(2)}) %collective-permute-start.6) | collective-permute-done | bytes 24608 | tf_op jit(solution)/shard_map/ppermute | solution.py:470
  15.1 0.3 collective-permute-start.7
  15.4 1.5 %collective-permute-start.2 = (f32[72,256]{1,0:T(8,128)S(1)}, f32[72,256]{1,0:T(8,128)S(1)}, u32[]{:S(2)}, u32[]{:S(2)}) collective-permute-start(f32[72,256]{1,0:T(8,128)S(1)} %get-tuple-element.21), channel_id=1, source_target_pairs={{0,2},{2,4},{4,6},{6,8},{8,10},{10,12},{12,14},{14,16},{16,18},{18... | collective-permute-start | bytes 221192 | tf_op jit(solution)/shard_map/ppermute | solution.py:445
  16.9 4.1 %collective-permute-start.3 = (f32[72,256]{1,0:T(8,128)S(1)}, f32[72,256]{1,0:T(8,128)S(1)}, u32[]{:S(2)}, u32[]{:S(2)}) collective-permute-start(f32[72,256]{1,0:T(8,128)S(1)} %get-tuple-element.22), channel_id=1, source_target_pairs={{2,0},{4,2},{6,4},{8,6},{10,8},{12,10},{14,12},{16,14},{18,16},{20... | collective-permute-start | bytes 221192 | tf_op jit(solution)/shard_map/ppermute | solution.py:442
  21.0 0.0 collective-permute-done.7
  21.0 0.1 collective-permute-start.8
  21.1 3.5 %collective-permute-done.8 = f32[48,128]{1,0:T(8,128)S(1)} collective-permute-done((f32[48,128]{1,0:T(8,128)S(1)}, f32[48,128]{1,0:T(8,128)S(1)}, u32[]{:S(2)}, u32[]{:S(2)}) %collective-permute-start.8) | collective-permute-done | bytes 24608 | tf_op jit(solution)/shard_map/ppermute | solution.py:470
  24.5 0.0 collective-permute-start.9
  24.5 0.5 %shard_map.89 = f32[72,128]{1,0:T(8,128)S(1)} custom-call(f32[16,256]{1,0:T(8,128)S(1)} %get-tuple-element.18.ar, f32[72,256]{1,0:T(8,128)S(1)} %collective-permute-done.west_row, f32[72,256]{1,0:T(8,128)S(1)} %collective-permute-done.1.east_row, f32[16,64,256]{2,1,0:T(8,128)S(1)} %get-tuple-element.27.applied), custom_call_target="tpu_custom_call" | custom-call | tf_op jit(solution)/shard_map/pallas_call | solution.py:383
  25.1 0.1 collective-permute-start.5
  25.2 2.6 %collective-permute-done.9 = f32[48,128]{1,0:T(8,128)S(1)} collective-permute-done((f32[48,128]{1,0:T(8,128)S(1)}, f32[48,128]{1,0:T(8,128)S(1)}, u32[]{:S(2)}, u32[]{:S(2)}) %collective-permute-start.9) | collective-permute-done | bytes 24608 | tf_op jit(solution)/shard_map/ppermute | solution.py:470
  27.8 0.5 %collective-permute-start.10 = (f32[48,128]{1,0:T(8,128)S(1)}, f32[48,128]{1,0:T(8,128)S(1)}, u32[]{:S(2)}, u32[]{:S(2)}) collective-permute-start(f32[48,128]{1,0:T(8,128)S(1)} %add.15.mine), channel_id=1, source_target_pairs={{0,17},{1,16},{2,19},{3,18},{4,21},{5,20},{6,23},{7,22},{8,25},{9,... | collective-permute-start | bytes 73736 | tf_op jit(solution)/shard_map/ppermute | solution.py:470
  28.3 0.0 collective-permute-done.2.far_west
  28.3 0.0 collective-permute-done.3.far_east
  28.3 0.0 collective-permute-done.5.got_low.got_high
  28.3 2.7 %shard_map.90 = f32[64,16,256]{2,1,0:T(8,128)} custom-call(f32[64,16,256]{2,1,0:T(8,128)S(1)} %get-tuple-element.16.sk, s32[16,256]{1,0:T(8,128)S(1)} %get-tuple-element.17.oc, f32[16,256]{1,0:T(8,128)S(1)} %get-tuple-element.18.ar, f32[72,256]{1,0:T(8,128)S(1)} %collective-permute-done.west_row, f32[72,256]{1,0:T(8,128)S(1)} %collective-permute-done.1.east_row, ...), custom_call_target="tpu_custom_call" | custom-call | tf_op jit(solution)/shard_map/pallas_call | solution.py:383
  31.1 1.3 %collective-permute-done.10.other = f32[48,128]{1,0:T(8,128)S(1)} collective-permute-done((f32[48,128]{1,0:T(8,128)S(1)}, f32[48,128]{1,0:T(8,128)S(1)}, u32[]{:S(2)}, u32[]{:S(2)}) %collective-permute-start.10) | collective-permute-done | bytes 24608 | tf_op jit(solution)/shard_map/ppermute | solution.py:470
  32.4 0.8 %shard_map.91 = f32[96,96]{1,0:T(8,128)} custom-call(f32[48,128]{1,0:T(8,128)S(1)} %add.15.mine, f32[48,128]{1,0:T(8,128)S(1)} %collective-permute-done.10.other), custom_call_target="tpu_custom_call" | custom-call | tf_op jit(solution)/shard_map/pallas_call | solution.py:383
  (4 shorter events, 0.0 us)
Async XLA Ops:
  2.1 9.4 %collective-permute-start = (f32[72,256]{1,0:T(8,128)S(1)}, f32[72,256]{1,0:T(8,128)S(1)}, u32[]{:S(2)}, u32[]{:S(2)}) collective-permute-start(f32[72,256]{1,0:T(8,128)S(1)} %get-tuple-element.19), channel_id=1, source_target_pairs={{0,2},{2,4},{4,6},{6,8},{8,10},{10,12},{12,14},{14,16},{16,18},{18... | collective-permute-start | bytes 221192 | tf_op jit(solution)/shard_map/ppermute | solution.py:440
  5.1 6.4 %collective-permute-start.1 = (f32[72,256]{1,0:T(8,128)S(1)}, f32[72,256]{1,0:T(8,128)S(1)}, u32[]{:S(2)}, u32[]{:S(2)}) collective-permute-start(f32[72,256]{1,0:T(8,128)S(1)} %get-tuple-element.20), channel_id=1, source_target_pairs={{2,0},{4,2},{6,4},{8,6},{10,8},{12,10},{14,12},{16,14},{18,16},{20... | collective-permute-start | bytes 221192 | tf_op jit(solution)/shard_map/ppermute | solution.py:441
  9.6 1.3 %collective-permute-start.4 = (f32[72,128]{1,0:T(8,128)S(1)}, f32[72,128]{1,0:T(8,128)S(1)}, u32[]{:S(2)}, u32[]{:S(2)}) collective-permute-start(f32[72,128]{1,0:T(8,128)S(1)} %shard_map.87), channel_id=1, source_target_pairs={{0,1},{1,0},{2,3},{3,2},{4,5},{5,4},{6,7},{7,6},{8,9},{9,8},{10,11... | collective-permute-start | bytes 110600 | tf_op jit(solution)/shard_map/ppermute | solution.py:410
  13.8 1.3 %collective-permute-start.6 = (f32[48,128]{1,0:T(8,128)S(1)}, f32[48,128]{1,0:T(8,128)S(1)}, u32[]{:S(2)}, u32[]{:S(2)}) collective-permute-start(f32[48,128]{1,0:T(8,128)S(1)} %get-tuple-element.29), channel_id=1, source_target_pairs={{0,1},{1,0},{2,3},{3,2},{4,5},{5,4},{6,7},{7,6},{8,9},{9,8},{10,11... | collective-permute-start | bytes 73736 | tf_op jit(solution)/shard_map/ppermute | solution.py:470
  15.1 5.9 %collective-permute-start.7 = (f32[48,128]{1,0:T(8,128)S(1)}, f32[48,128]{1,0:T(8,128)S(1)}, u32[]{:S(2)}, u32[]{:S(2)}) collective-permute-start(f32[48,128]{1,0:T(8,128)S(1)} %add.12), channel_id=1, source_target_pairs={{0,3},{1,2},{2,1},{3,0},{4,7},{5,6},{6,5},{7,4},{8,11},{9,10},{10,... | collective-permute-start | bytes 73736 | tf_op jit(solution)/shard_map/ppermute | solution.py:470
  15.4 13.0 %collective-permute-start.2 = (f32[72,256]{1,0:T(8,128)S(1)}, f32[72,256]{1,0:T(8,128)S(1)}, u32[]{:S(2)}, u32[]{:S(2)}) collective-permute-start(f32[72,256]{1,0:T(8,128)S(1)} %get-tuple-element.21), channel_id=1, source_target_pairs={{0,2},{2,4},{4,6},{6,8},{8,10},{10,12},{12,14},{14,16},{16,18},{18... | collective-permute-start | bytes 221192 | tf_op jit(solution)/shard_map/ppermute | solution.py:445
  16.9 11.5 %collective-permute-start.3 = (f32[72,256]{1,0:T(8,128)S(1)}, f32[72,256]{1,0:T(8,128)S(1)}, u32[]{:S(2)}, u32[]{:S(2)}) collective-permute-start(f32[72,256]{1,0:T(8,128)S(1)} %get-tuple-element.22), channel_id=1, source_target_pairs={{2,0},{4,2},{6,4},{8,6},{10,8},{12,10},{14,12},{16,14},{18,16},{20... | collective-permute-start | bytes 221192 | tf_op jit(solution)/shard_map/ppermute | solution.py:442
  21.0 3.5 %collective-permute-start.8 = (f32[48,128]{1,0:T(8,128)S(1)}, f32[48,128]{1,0:T(8,128)S(1)}, u32[]{:S(2)}, u32[]{:S(2)}) collective-permute-start(f32[48,128]{1,0:T(8,128)S(1)} %add.13), channel_id=1, source_target_pairs={{0,5},{1,4},{2,7},{3,6},{4,1},{5,0},{6,3},{7,2},{8,13},{9,12},{10,... | collective-permute-start | bytes 73736 | tf_op jit(solution)/shard_map/ppermute | solution.py:470
  24.5 3.3 %collective-permute-start.9 = (f32[48,128]{1,0:T(8,128)S(1)}, f32[48,128]{1,0:T(8,128)S(1)}, u32[]{:S(2)}, u32[]{:S(2)}) collective-permute-start(f32[48,128]{1,0:T(8,128)S(1)} %add.14), channel_id=1, source_target_pairs={{0,9},{1,8},{2,11},{3,10},{4,13},{5,12},{6,15},{7,14},{8,1},{9,0},... | collective-permute-start | bytes 73736 | tf_op jit(solution)/shard_map/ppermute | solution.py:470
  25.1 3.2 %collective-permute-start.5 = (f32[72,128]{1,0:T(8,128)S(1)}, f32[72,128]{1,0:T(8,128)S(1)}, u32[]{:S(2)}, u32[]{:S(2)}) collective-permute-start(f32[72,128]{1,0:T(8,128)S(1)} %shard_map.89), channel_id=1, source_target_pairs={{0,1},{1,0},{2,3},{3,2},{4,5},{5,4},{6,7},{7,6},{8,9},{9,8},{10,11... | collective-permute-start | bytes 110600 | tf_op jit(solution)/shard_map/ppermute | solution.py:410
  27.8 4.6 %collective-permute-start.10 = (f32[48,128]{1,0:T(8,128)S(1)}, f32[48,128]{1,0:T(8,128)S(1)}, u32[]{:S(2)}, u32[]{:S(2)}) collective-permute-start(f32[48,128]{1,0:T(8,128)S(1)} %add.15.mine), channel_id=1, source_target_pairs={{0,17},{1,16},{2,19},{3,18},{4,21},{5,20},{6,23},{7,22},{8,25},{9,... | collective-permute-start | bytes 73736 | tf_op jit(solution)/shard_map/ppermute | solution.py:470

commit v4 on v3

--- a/solution.py
+++ b/solution.py
@@ -84,7 +84,7 @@
 
 
 def load_kernel(sizes, *refs):
-    given, held, rows, sems = refs[:7], refs[7:14], refs[14:18], refs[18]
+    given, held, rows, edges, sems = refs[:7], refs[7:14], refs[14:18], refs[18:-1], refs[-1]
     n, count = sizes.lons, sizes.count
     copies = [pltpu.make_async_copy(g, h, sems.at[k]) for k, (g, h) in enumerate(zip(given, held))]
     for copy in copies:
@@ -101,8 +101,7 @@
         ref[count + 2 :, :] = jnp.zeros((ref.shape[0] - count - 2, sizes.lats), F32)
 
 
-def pack_kernel(sizes, sk, wd, oc, no, *edges):
-    n, count = sizes.lons, sizes.count
+    no = held[4]
     last = sizes.lats - LANES
     for start in range(0, count, BITS):
         ids = lane_ids(BITS)
@@ -137,68 +136,145 @@
     return turned[index * sizes.lons : (index + 1) * sizes.lons, 0:1]
 
 
+def far_side():
+    return lax.axis_index("lon") == lax.axis_size("lon") - 1
+
+
+def products(split_hi, split_lo):
+    dims = (((1,), (1,)), ((), ()))
+    main = lax.dot_general(split_hi[...], split_hi[...], dims, preferred_element_type=F32)
+    cross = lax.dot_general(split_hi[...], split_lo[...], dims, preferred_element_type=F32)
+    return main + cross + cross.T
+
+
+def store_split(split_hi, split_lo, rows, at, scaled):
+    high = scaled.astype(jnp.bfloat16)
+    split_hi[rows, at] = high
+    split_lo[rows, at] = (scaled - high.astype(F32)).astype(jnp.bfloat16)
+
+
+def rows_of(refs, where):
+    return list(zip(*[halves(refs[(k,) + where]) for k in range(5)]))
+
+
+def probe_edges(sizes, w, got_low, got_high):
+    edges = []
+    for got in (got_low, got_high):
+        row = got[sizes.count : sizes.count + 1, :].astype(jnp.int32)
+        edges.append(spread(pltpu.roll(row, (LANES - w * sizes.lons) % LANES, 1)))
+    return edges
+
+
+def inner_kernel(
+    far, sizes, sk, wd, oc, ea, no, ka, ar, got_low, got_high,
+    applied, coef, partial, split_hi, split_lo, ext, root,
+):
+    n, count, lats, words = sizes.lons, sizes.count, sizes.lats, sizes.words
+
+    @pl.when(far_side() == far)
+    def _():
+        lat_id = lax.axis_index("lat")
+        sea = oc[...].astype(F32)
+        ext[0, 8 : 8 + n, :] = sea
+        ext[0, 8 + n : 9 + n, :] = jnp.zeros((1, lats), F32)
+        ext[1, 8 : 8 + n, :] = ea[...] * sea * ext[0, 9 : 9 + n, :]
+        ext[1, 7:8, :] = jnp.zeros((1, lats), F32)
+        east_w = ext[1, 8 : 8 + n, :]
+        west_w = ext[1, 7 : 7 + n, :]
+
+        sea_low, north_low = (edge_columns(got_low, sizes, words + k) for k in (0, 1))
+        sea_high = edge_columns(got_high, sizes, words)
+        sea_parts = halves(sea)
+        half_north = [no[:, h * LANES : (h + 1) * LANES] * part for h, part in enumerate(sea_parts)]
+        at_low = jnp.where(lat_id == 0, 0.0, 1.0)
+        at_high = jnp.where(lat_id == sizes.lat_axis - 1, 0.0, 1.0)
+        edge_high = jnp.broadcast_to(sea_high * at_high, (n, LANES))
+        edge_low = jnp.broadcast_to(sea_low * north_low * at_low, (n, LANES))
+        sea_north, _ = lat_shifts(sea_parts, edge_low, edge_high)
+        _, flow_south = lat_shifts(half_north, edge_low, edge_high)
+        north_w = jnp.concatenate([a * b for a, b in zip(half_north, sea_north)], axis=1)
+        south_w = jnp.concatenate([a * b for a, b in zip(flow_south, sea_parts)], axis=1)
+        coef[0] = sea * (ka[...] + east_w + west_w + north_w + south_w)
+        coef[1] = east_w
+        coef[2] = west_w
+        coef[3] = north_w
+        coef[4] = south_w
+        root[...] = jnp.sqrt(ar[...])
+
+        def one_block(start, get, low_edge, high_edge, keep):
+            rows = pl.ds(start, BITS)
+            west, middle = get(0), get(1)
+            for i in range(1, n - 1):
+                east = get(i + 1)
+                north, south = lat_shifts(
+                    middle, edge_at(low_edge, i, 0), edge_at(high_edge, i, LANES - 1)
+                )
+                weights = rows_of(coef, (slice(i, i + 1), slice(None)))
+                for h, part in enumerate(stencil(weights, middle, east, west, north, south)):
+                    here = slice(h * LANES, (h + 1) * LANES)
+                    if keep:
+                        applied[i - 1, rows, here] = part
+                    at = slice((i - 1) * lats + h * LANES, (i - 1) * lats + (h + 1) * LANES)
+                    store_split(split_hi, split_lo, rows, at, part * root[i : i + 1, here])
+                west, middle = middle, east
+
+        def sketch_block(k, carry):
+            start = pl.multiple_of(k * BITS, BITS)
+            rows = pl.ds(start, BITS)
+            one_block(start, lambda i: halves(sk[rows, i, :]), got_low[rows, :], got_high[rows, :], True)
+            return carry
+
+        lax.fori_loop(0, count // BITS, sketch_block, 0)
+        for w in range(words):
+            one_block(
+                count + w * BITS,
+                lambda i: [spread(part) for part in halves(wd[w, i : i + 1, :])],
+                *probe_edges(sizes, w, got_low, got_high),
+                False,
+            )
+        partial[...] = products(split_hi, split_lo)
+
+
 def gram_kernel(
-    sizes, sk, wd, oc, ea, no, ka, ar, west_row, east_row, got_low, got_high,
-    gram, applied, coef, split_hi, split_lo, ext, root, whole,
+    sizes, sk, wd, oc, ea, ka, ar, west_row, east_row, got_low, got_high,
+    coef_near, coef_far, partial_near, partial_far,
+    gram, ends, end_coef, split_hi, split_lo, whole,
 ):
     n, count, lats, words = sizes.lons, sizes.count, sizes.lats, sizes.words
     base = count + words
-    lat_id = lax.axis_index("lat")
-    before, after = west_row[base : base + 3, :], east_row[base : base + 1, :]
-
-    sea = oc[...].astype(F32)
-    ext[0, 8 : 8 + n, :] = sea
-    ext[0, 8 + n : 9 + n, :] = after[0:1]
-    ext[1, 8 : 8 + n, :] = ea[...] * sea * ext[0, 9 : 9 + n, :]
-    ext[1, 7:8, :] = before[1:2] * before[0:1] * sea[0:1]
-    east_w = ext[1, 8 : 8 + n, :]
-    west_w = ext[1, 7 : 7 + n, :]
-
-    sea_low, north_low = (edge_columns(got_low, sizes, words + k) for k in (0, 1))
-    sea_high = edge_columns(got_high, sizes, words)
-    ids = lane_ids(n)
-    sea_parts = halves(sea)
-    half_north = [no[:, h * LANES : (h + 1) * LANES] * part for h, part in enumerate(sea_parts)]
-    at_low = jnp.where(lat_id == 0, 0.0, 1.0)
-    at_high = jnp.where(lat_id == sizes.lat_axis - 1, 0.0, 1.0)
-    edge_high = jnp.broadcast_to(sea_high * at_high, (n, LANES))
-    edge_low = jnp.broadcast_to(sea_low * north_low * at_low, (n, LANES))
-    sea_north, _ = lat_shifts(sea_parts, edge_low, edge_high)
-    _, flow_south = lat_shifts(half_north, edge_low, edge_high)
-    north_w = jnp.concatenate([a * b for a, b in zip(half_north, sea_north)], axis=1)
-    south_w = jnp.concatenate([a * b for a, b in zip(flow_south, sea_parts)], axis=1)
-    coef[0] = sea * (ka[...] + east_w + west_w + north_w + south_w)
-    coef[1] = east_w
-    coef[2] = west_w
-    coef[3] = north_w
-    coef[4] = south_w
-    root[...] = jnp.sqrt(ar[...])
-
-    def weights_at(i):
-        rows = [coef[k, i : i + 1, :] for k in range(5)]
-        return list(zip(*[halves(r) for r in rows]))
+    far = far_side()
+
+    def inner(k, i):
+        return lax.select(far, coef_far[k, i : i + 1, :], coef_near[k, i : i + 1, :])
+
+    root = []
+    for side, i in enumerate((0, n - 1)):
+        sea = oc[i : i + 1, :].astype(F32)
+        east_w, west_w, north_w, south_w = (inner(k, i) for k in range(1, 5))
+        if side == 0:
+            west_w = west_row[base + 1 : base + 2, :] * west_row[base : base + 1, :] * sea
+        else:
+            east_w = ea[i : i + 1, :] * sea * east_row[base : base + 1, :]
+        center = sea * (ka[i : i + 1, :] + east_w + west_w + north_w + south_w)
+        for k, row in enumerate((center, east_w, west_w, north_w, south_w)):
+            end_coef[k, side : side + 1, :] = row
+        root.append(jnp.sqrt(ar[i : i + 1, :]))
 
     def one_block(start, get, low_edge, high_edge, keep):
-        west, middle = get(-1), get(0)
-        for i in range(n):
-            east = get(i + 1)
-            north, south = lat_shifts(
-                middle, edge_at(low_edge, i, 0), edge_at(high_edge, i, LANES - 1)
-            )
-            out = stencil(weights_at(i), middle, east, west, north, south)
-            for h, part in enumerate(out):
+        rows = pl.ds(start, BITS)
+        for side, i in enumerate((0, n - 1)):
+            middle = get(i)
+            north, south = lat_shifts(middle, edge_at(low_edge, i, 0), edge_at(high_edge, i, LANES - 1))
+            weights = rows_of(end_coef, (slice(side, side + 1), slice(None)))
+            for h, part in enumerate(stencil(weights, middle, get(i + 1), get(i - 1), north, south)):
+                here = slice(h * LANES, (h + 1) * LANES)
                 if keep:
-                    applied[i, pl.ds(start, BITS), h * LANES : (h + 1) * LANES] = part
-                scaled = part * root[i : i + 1, h * LANES : (h + 1) * LANES]
-                high = scaled.astype(jnp.bfloat16)
-                at = slice(i * lats + h * LANES, i * lats + (h + 1) * LANES)
-                split_hi[pl.ds(start, BITS), at] = high
-                split_lo[pl.ds(start, BITS), at] = (scaled - high.astype(F32)).astype(jnp.bfloat16)
-            west, middle = middle, east
-
-    def sketch_block(k, carry):
-        start = pl.multiple_of(k * BITS, BITS)
-        rows = pl.ds(start, BITS)
+                    ends[side, rows, here] = part
+                at = slice(side * lats + h * LANES, side * lats + (h + 1) * LANES)
+                store_split(split_hi, split_lo, rows, at, part * root[side][:, here])
+
+    for start in range(0, count, BITS):
+        rows = slice(start, start + BITS)
 
         def get(i):
             if i == -1:
@@ -208,31 +284,20 @@
             return halves(sk[rows, i, :])
 
         one_block(start, get, got_low[rows, :], got_high[rows, :], True)
-        return carry
-
-    lax.fori_loop(0, count // BITS, sketch_block, 0)
     for w in range(words):
-        before_w, after_w = (ref[count + w : count + w + 1, :] for ref in (west_row, east_row))
 
         def get(i):
             if i == -1:
-                row = before_w.astype(jnp.int32)
+                row = west_row[count + w : count + w + 1, :].astype(jnp.int32)
             elif i == n:
-                row = after_w.astype(jnp.int32)
+                row = east_row[count + w : count + w + 1, :].astype(jnp.int32)
             else:
                 row = wd[w, i : i + 1, :]
             return [spread(part) for part in halves(row)]
 
-        edges = []
-        for got in (got_low, got_high):
-            row = got[count : count + 1, :].astype(jnp.int32)
-            edges.append(spread(pltpu.roll(row, (LANES - w * n) % LANES, 1)))
-        one_block(count + w * BITS, get, edges[0], edges[1], False)
-
-    dims = (((1,), (1,)), ((), ()))
-    main = lax.dot_general(split_hi[...], split_hi[...], dims, preferred_element_type=F32)
-    cross = lax.dot_general(split_hi[...], split_lo[...], dims, preferred_element_type=F32)
-    total = main + cross + cross.T
+        one_block(count + w * BITS, get, *probe_edges(sizes, w, got_low, got_high), False)
+
+    total = lax.select(far, partial_far[...], partial_near[...]) + products(split_hi, split_lo)
     if not sizes.folded:
         gram[...] = total
         return
@@ -263,30 +328,37 @@
     out[...] = jnp.where(down <= across, upper, upper.T)[0 : sizes.cols, 0 : sizes.cols]
 
 
-def edge_kernel(sizes, ar, west_row, east_row, applied, *edges):
+def edge_kernel(sizes, ar, west_row, east_row, near, far, ends, *edges):
     n, count, lats = sizes.lons, sizes.count, sizes.lats
     last = lats - LANES
     base = count + sizes.words
 
-    def block(k, carry):
-        start = pl.multiple_of(k * BITS, BITS)
-        rows = pl.ds(start, BITS)
-        ids = lane_ids(BITS)
-        total = [jnp.zeros((BITS, LANES), F32) for _ in edges]
-        for i in range(n + 2):
-            if i < n:
-                low = applied[i, rows, 0:LANES] * ar[i : i + 1, 0:LANES]
-                high = applied[i, rows, last:] * ar[i : i + 1, last:]
-            else:
-                side = west_row if i == n else east_row
-                low, high = side[rows, 0:LANES], side[rows, last:]
-            moved = edge_rows_of(sizes, low, high, i)
-            total = [jnp.where(ids == i, m, t) for m, t in zip(moved, total)]
-        for edge, t in zip(edges, total):
-            edge[rows, :] = t
-        return carry
-
-    lax.fori_loop(0, count // BITS, block, 0)
+    def fill(applied):
+        def block(k, carry):
+            start = pl.multiple_of(k * BITS, BITS)
+            rows = pl.ds(start, BITS)
+            ids = lane_ids(BITS)
+            total = [jnp.zeros((BITS, LANES), F32) for _ in edges]
+            for i in range(n + 2):
+                if i >= n:
+                    side = west_row if i == n else east_row
+                    low, high = side[rows, 0:LANES], side[rows, last:]
+                else:
+                    if 0 < i < n - 1:
+                        low, high = applied[i - 1, rows, 0:LANES], applied[i - 1, rows, last:]
+                    else:
+                        low, high = ends[min(i, 1), rows, 0:LANES], ends[min(i, 1), rows, last:]
+                    low, high = low * ar[i : i + 1, 0:LANES], high * ar[i : i + 1, last:]
+                moved = edge_rows_of(sizes, low, high, i)
+                total = [jnp.where(ids == i, m, t) for m, t in zip(moved, total)]
+            for edge, t in zip(edges, total):
+                edge[rows, :] = t
+            return carry
+
+        lax.fori_loop(0, count // BITS, block, 0)
+
+    pl.when(far_side())(lambda: fill(far))
+    pl.when(jnp.logical_not(far_side()))(lambda: fill(near))
     tails = [jnp.zeros((8, LANES), F32) for _ in edges]
     ids, sub = lane_ids(8), lax.broadcasted_iota(jnp.int32, (8, LANES), 0)
     for k, row in enumerate((base, base + 2)):
@@ -304,26 +376,59 @@
         edge[count : count + 8, :] = t
 
 
+def image_inner_kernel(part, sizes, ar, near, far, coef_near, coef_far, ends, end_coef, got_low, got_high, out):
+    n, count = sizes.lons, sizes.count
+    blocks = count // BITS // 2
+
+    def fill(applied, coef):
+        def block(k, carry):
+            start = pl.multiple_of((part * blocks + k) * BITS, BITS)
+            rows, here = pl.ds(start, BITS), pl.ds(pl.multiple_of(k * BITS, BITS), BITS)
+            low_edge, high_edge = got_low[rows, :], got_high[rows, :]
+
+            def get(i):
+                source = applied[i - 1, rows, :] if 0 < i < n - 1 else ends[min(i, 1), rows, :]
+                return halves(source * ar[i : i + 1, :])
+
+            west, middle = get(0), get(1)
+            for i in range(1, n - 1):
+                east = get(i + 1)
+                north, south = lat_shifts(
+                    middle, edge_at(low_edge, i, 0), edge_at(high_edge, i, LANES - 1)
+                )
+                weights = rows_of(coef, (slice(i, i + 1), slice(None)))
+                for h, tile in enumerate(stencil(weights, middle, east, west, north, south)):
+                    out[i - 1, here, h * LANES : (h + 1) * LANES] = tile
+                west, middle = middle, east
+            return carry
+
+        lax.fori_loop(0, blocks, block, 0)
+
+    pl.when(far_side())(lambda: fill(far, coef_far))
+    pl.when(jnp.logical_not(far_side()))(lambda: fill(near, coef_near))
+
+
 def image_kernel(
-    sizes, sk, oc, ar, west_row, east_row, far_west, far_east, applied, coef, got_low, got_high, out,
+    sizes, sk, ar, west_row, east_row, far_west, far_east, near, far, ends, end_coef,
+    got_low, got_high, inner_0, inner_1, out, buffer, sems,
 ):
     n, count = sizes.lons, sizes.count
     base = count + sizes.words
     lat_id = lax.axis_index("lat")
     at_low = jnp.where(lat_id == 0, 0.0, 1.0)
     at_high = jnp.where(lat_id == sizes.lat_axis - 1, 0.0, 1.0)
-    near = [ref[base : base + 5, :] for ref in (west_row, east_row)]
-    far = [ref[count : count + 2, :] for ref in (far_west, far_east)]
+    near_rows = [ref[base : base + 5, :] for ref in (west_row, east_row)]
+    far_rows = [ref[count : count + 2, :] for ref in (far_west, far_east)]
     ghost = []
     for side in (0, 1):
-        rows = near[side]
+        rows = near_rows[side]
         sea, east, north, kappa, area = (rows[k : k + 1] for k in range(5))
         if side == 0:
-            east_w = coef[2, 0:1, :]
-            west_w = far[0][1:2] * far[0][0:1] * sea
+            east_w = end_coef[2, 0:1, :]
+            west_w = far_rows[0][1:2] * far_rows[0][0:1] * sea
         else:
-            east_w = east * sea * far[1][0:1]
-            west_w = coef[1, n - 1 : n, :]
+            east_w = east * sea * far_rows[1][0:1]
+            west_w = end_coef[1, 1:2, :]
         lane = n + side
         low = got_low[count : count + 8, :]
         high = got_high[count : count + 8, :]
@@ -338,55 +443,69 @@
         center = sea * (kappa + east_w + west_w + north_w + south_w)
         ghost.append(list(zip(*[halves(r * area) for r in (center, east_w, west_w, north_w, south_w)])))
 
-    def weights_at(i):
-        rows = [coef[k, i : i + 1, :] for k in range(5)]
-        return list(zip(*[halves(r) for r in rows]))
-
-    def block(k, carry):
+    far_lon = far_side()
+
+    def copy_out(k):
         start = pl.multiple_of(k * BITS, BITS)
-        rows = pl.ds(start, BITS)
+        return pltpu.make_async_copy(buffer.at[k], out.at[pl.ds(start, BITS)], sems.at[k])
+
+    def block_of(k, half, inner):
+        start = pl.multiple_of(k * BITS, BITS)
+        rows, here = pl.ds(start, BITS), pl.ds(pl.multiple_of((k - half) * BITS, BITS), BITS)
         low_edge, high_edge = got_low[rows, :], got_high[rows, :]
-
-        def get(i):
-            if 0 <= i < n:
-                return halves(applied[i, rows, :] * ar[i : i + 1, :])
-            side = 0 if i < 0 else 1
+        for i in range(1, n - 1):
+            buffer[k, :, i, :] = inner[i - 1, here, :]
+        for side, i in enumerate((0, n - 1)):
             middle = halves((west_row, east_row)[side][rows, :])
             beyond = halves((far_west, far_east)[side][rows, :])
-            inner = halves(sk[rows, 0 if side == 0 else n - 1, :])
-            east, west = (inner, beyond) if side == 0 else (beyond, inner)
+            own = halves(sk[rows, i, :])
+            east, west = (own, beyond) if side == 0 else (beyond, own)
             north, south = lat_shifts(
                 middle,
                 edge_at(low_edge, n + side, 0),
                 edge_at(high_edge, n + side, LANES - 1),
             )
-            return stencil(ghost[side], middle, east, west, north, south)
-
-        west, middle = get(-1), get(0)
-        for i in range(n):
-            east = get(i + 1)
+            outer = stencil(ghost[side], middle, east, west, north, south)
+            middle = halves(ends[side, rows, :] * ar[i : i + 1, :])
+            next_in = 1 if side == 0 else n - 2
+            inward = lax.select(far_lon, far[next_in - 1, rows, :], near[next_in - 1, rows, :])
+            inward = halves(inward * ar[next_in : next_in + 1, :])
+            east, west = (inward, outer) if side == 0 else (outer, inward)
             north, south = lat_shifts(
                 middle, edge_at(low_edge, i, 0), edge_at(high_edge, i, LANES - 1)
             )
-            parts = stencil(weights_at(i), middle, east, west, north, south)
-            for h, part in enumerate(parts):
-                out[rows, i, h * LANES : (h + 1) * LANES] = part
-            west, middle = middle, east
+            weights = rows_of(end_coef, (slice(side, side + 1), slice(None)))
+            for h, tile in enumerate(stencil(weights, middle, east, west, north, south)):
+                buffer[k, :, i, h * LANES : (h + 1) * LANES] = tile
+        copy_out(k).start()
+
+    half = count // BITS // 2
+
+    def first(k, carry):
+        block_of(k, 0, inner_0)
         return carry
 
-    lax.fori_loop(0, count // BITS, block, 0)
-
-
-def call(kernel, sizes, outs, args, scratch=(), inputs=pltpu.VMEM, limit=16 << 20):
+    def second(k, carry):
+        block_of(k, half, inner_1)
+        return carry
+
+    lax.fori_loop(0, half, first, 0)
+    lax.fori_loop(half, 2 * half, second, 0)
+    for k in range(2 * half):
+        copy_out(k).wait()
+
+
+def call(kernel, sizes, outs, args, scratch=(), inputs=None, out_space=pltpu.VMEM, alias=None):
     outs = [o if isinstance(o, jax.ShapeDtypeStruct) else jax.ShapeDtypeStruct(o, F32) for o in outs]
-    vmem = pl.BlockSpec(memory_space=pltpu.VMEM)
+    spaces = inputs or [pltpu.VMEM] * len(args)
     return pl.pallas_call(
         functools.partial(kernel, sizes),
         out_shape=outs,
-        in_specs=[pl.BlockSpec(memory_space=inputs)] * len(args),
-        out_specs=[vmem] * len(outs),
+        in_specs=[pl.BlockSpec(memory_space=space) for space in spaces],
+        out_specs=[pl.BlockSpec(memory_space=out_space)] * len(outs),
         scratch_shapes=list(scratch),
-        compiler_params=pltpu.CompilerParams(vmem_limit_bytes=limit),
+        input_output_aliases=alias or {},
+        compiler_params=pltpu.CompilerParams(vmem_limit_bytes=16 << 20),
     )(*args)
 
 
@@ -427,43 +546,64 @@
     edge_count = 1 if sizes.paired else 2
 
     shapes = [jax.ShapeDtypeStruct(f.shape, f.dtype) for f in fields]
-    *fields, to_east, to_west, far_to_east, far_to_west = call(
+    loaded = call(
         load_kernel,
         sizes,
-        shapes + [line, line, far_line, far_line],
+        shapes + [line, line, far_line, far_line] + [edge] * edge_count,
         [pltpu.with_memory_space_constraint(f, pltpu.HBM) for f in fields],
         [pltpu.SemaphoreType.DMA((7,))],
-        inputs=pltpu.HBM,
+        inputs=[pltpu.HBM] * len(fields),
     )
-    fields = tuple(fields)
-    sketch, probe_bits, ocean, _, north_cond, _, inv_area = fields
+    fields, (to_east, to_west, far_to_east, far_to_west), packed = tuple(loaded[:7]), loaded[7:11], loaded[11:]
+    sketch, probe_bits, ocean, east_cond, north_cond, kappa_sq, inv_area = fields
     west_row = lax.ppermute(to_east, "lon", eastward)
     east_row = lax.ppermute(to_west, "lon", westward)
     far_east = lax.ppermute(far_to_west, "lon", westward)
-    packed = call(pack_kernel, sizes, [edge] * edge_count, (sketch, probe_bits, ocean, north_cond))
     low, high = swap_edges(packed)
+    far_east = lax.ppermute(far_to_west, "lon", westward)
     far_west = lax.ppermute(far_to_east, "lon", eastward)
 
-    gram, applied, coef = call(
+    def split(lons):
+        return [pltpu.VMEM((sizes.cols, lons * lats), jnp.bfloat16)] * 2
+
+    inner = [
+        call(
+            functools.partial(inner_kernel, far),
+            sizes,
+            [(n - 2, count, lats), (5, n, lats), (sizes.cols, sizes.cols)],
+            fields + (low, high),
+            split(n - 2) + [pltpu.VMEM((2, n + 16, lats), F32), pltpu.VMEM((n, lats), F32)],
+        )
+        for far in (False, True)
+    ]
+    (near, coef_near, partial_near), (far, coef_far, partial_far) = inner
+    gram, ends, end_coef = call(
         gram_kernel,
         sizes,
-        [(sizes.cols // 2, LANES) if sizes.folded else (sizes.cols, sizes.cols), (n, count, lats), (5, n, lats)],
-        fields + (west_row, east_row, low, high),
-        [
-            pltpu.VMEM((sizes.cols, n * lats), jnp.bfloat16),
-            pltpu.VMEM((sizes.cols, n * lats), jnp.bfloat16),
-            pltpu.VMEM((2, n + 16, lats), F32),
-            pltpu.VMEM((n, lats), F32),
-            pltpu.VMEM((sizes.cols, LANES), F32),
-        ],
+        [(sizes.cols // 2, LANES) if sizes.folded else (sizes.cols, sizes.cols), (2, count, lats), (5, 2, lats)],
+        (sketch, probe_bits, ocean, east_cond, kappa_sq, inv_area, west_row, east_row, low, high)
+        + (coef_near, coef_far, partial_near, partial_far),
+        split(2) + [pltpu.VMEM((sizes.cols, LANES), F32)],
     )
-    edges = call(edge_kernel, sizes, [edge] * edge_count, (inv_area, west_row, east_row, applied))
+    edges = call(edge_kernel, sizes, [edge] * edge_count, (inv_area, west_row, east_row, near, far, ends))
     low2, high2 = swap_edges(edges)
+    inner_images = [
+        call(
+            functools.partial(image_inner_kernel, part),
+            sizes,
+            [(n - 2, count // 2, lats)],
+            (inv_area, near, far, coef_near, coef_far, ends, end_coef, low2, high2),
+        )[0]
+        for part in range(2)
+    ]
     (image,) = call(
         image_kernel,
         sizes,
         [sketch.shape],
-        (sketch, ocean, inv_area, west_row, east_row, far_west, far_east, applied, coef, low2, high2),
+        (sketch, inv_area, west_row, east_row, far_west, far_east, near, far, ends, end_coef, low2, high2)
+        + tuple(inner_images),
+        [pltpu.VMEM((count // BITS, BITS, n, lats), F32), pltpu.SemaphoreType.DMA((count // BITS,))],
+        out_space=pltpu.HBM,
     )
     steps = exchanges()
     for k, pairs in enumerate(steps):

time: 33.3 us -> 31.2 us (0.937)
  waiting for transfers between devices: 10.3 us -> 7.39 us
  starting transfers between devices: 13.8 us -> 14.4 us
    ppermute x5, waiting for transfers between devices: 8.58 us -> 6.17 us  [local(): other = lax.ppermute(gram, ('lon', 'lat'), pairs)]
    ppermute x1, starting transfers between devices: 4.12 us -> 4.73 us  [local(): far_east = lax.ppermute(far_to_west, 'lon', westward)]
    ppermute x1, waiting for transfers between devices: 0.55 us -> 0.01 us  [local(): west_row = lax.ppermute(to_east, 'lon', eastward)]
    pallas_call x6 -> x9, Pallas kernels: 8.28 us -> 8.45 us  [call(): pl.pallas_call(functools.partial(kernel, sizes), out_shape=outs, in_specs...]
  transfers between devices with their start and end apart: 11 -> 11, of which waited for: 6 -> 5; matrix products, arithmetic and copies ran while one was open for 0% -> 0% of each run, Pallas kernels for 11% -> 17%
where the time goes in v4:
time: 31.2 us; the launch traced here: 31 us
  starting transfers between devices  14.4 us (46%)
  Pallas kernels  8.45 us (27%)
  waiting for transfers between devices  7.39 us (24%)
  between operations  0.74 us (2%)
    pallas_call x9, Pallas kernels, call(): pl.pallas_call(functools.partial(kernel, sizes), out_shape=outs, in_specs...  8.45 us
    ppermute x5, waiting for transfers between devices, local(): other = lax.ppermute(gram, ('lon', 'lat'), pairs)  6.17 us
    ppermute x1, starting transfers between devices, local(): far_east = lax.ppermute(far_to_west, 'lon', westward)  4.73 us
    ppermute x1, starting transfers between devices, local(): east_row = lax.ppermute(to_west, 'lon', westward)  4.06 us
    ppermute x1, starting transfers between devices, local(): west_row = lax.ppermute(to_east, 'lon', eastward)  3.02 us
    ppermute x1, starting transfers between devices, local(): far_west = lax.ppermute(far_to_east, 'lon', eastward)  1.79 us
    ppermute x2, waiting for transfers between devices, swap_edges(): got = lax.ppermute(edges[0], 'lat', [(0, 1), (1, 0)])  1.21 us
    ppermute x5, starting transfers between devices, local(): other = lax.ppermute(gram, ('lon', 'lat'), pairs)  0.69 us
  transfers between devices with their start and end apart: 11, of which 5 were waited for; matrix products, arithmetic and copies ran while one was open for 0% of the time, Pallas kernels for 17%

profile of v4, /device:TPU:0, one launch (start us, length us, event | category | flops | bytes accessed | tf_op | source)
XLA Modules:
  0.0 31.0 jit_solution(11560873291360299388)
XLA Ops:
  0.6 1.9 %shard_map.86 = (f32[64,16,256]{2,1,0:T(8,128)S(1)}, s32[2,16,256]{2,1,0:T(8,128)S(1)}, s32[16,256]{1,0:T(8,128)S(1)}, f32[16,256]{1,0:T(8,128)S(1)}, f32[16,256...) custom-call(f32[64,16,256]{2,1,0:T(8,128)} %refs_0_.1, ...), custom_call_target="tpu_custom_call" | custom-call | tf_op jit(solution)/shard_map/pallas_call | solution.py:501
  2.5 3.0 %collective-permute-start = (f32[72,256]{1,0:T(8,128)S(1)}, f32[72,256]{1,0:T(8,128)S(1)}, u32[]{:S(2)}, u32[]{:S(2)}) collective-permute-start(f32[72,256]{1,0:T(8,128)S(1)} %get-tuple-element.25), channel_id=1, source_target_pairs={{0,2},{2,4},{4,6},{6,8},{8,10},{10,12},{12,14},{14,16},{16,18},{18... | collective-permute-start | bytes 221192 | tf_op jit(solution)/shard_map/ppermute | solution.py:559
  5.6 4.1 %collective-permute-start.1 = (f32[72,256]{1,0:T(8,128)S(1)}, f32[72,256]{1,0:T(8,128)S(1)}, u32[]{:S(2)}, u32[]{:S(2)}) collective-permute-start(f32[72,256]{1,0:T(8,128)S(1)} %get-tuple-element.26), channel_id=1, source_target_pairs={{2,0},{4,2},{6,4},{8,6},{10,8},{12,10},{14,12},{16,14},{18,16},{20... | collective-permute-start | bytes 221192 | tf_op jit(solution)/shard_map/ppermute | solution.py:560
  9.6 0.0 collective-permute-start.4
  9.6 1.2 %collective-permute-done.4.got_low.got_high = f32[72,128]{1,0:T(8,128)S(1)} collective-permute-done((f32[72,128]{1,0:T(8,128)S(1)}, f32[72,128]{1,0:T(8,128)S(1)}, u32[]{:S(2)}, u32[]{:S(2)}) %collective-permute-start.4) | collective-permute-done | bytes 36896 | tf_op jit(solution)/shard_map/ppermute | solution.py:529
  10.8 2.0 %shard_map.87 = (f32[14,64,256]{2,1,0:T(8,128)S(1)}, f32[5,16,256]{2,1,0:T(8,128)S(1)}, f32[96,96]{1,0:T(8,128)S(1)}) custom-call(f32[64,16,256]{2,1,0:T(8,128)S(1)} %get-tuple-element.23.sk, s32[2,16,256]{2,1,0:T(8,128)S(1)} %get-tuple-element.29.wd, s32[16,256]{1,0:T(8,128)S(1)} %get-tuple-element.30.oc, f32[16,256]{1,0:T(8,128)S(1)} %get-tuple-element.31.ea, ...), custom_call_target="tpu_custom_call" | custom-call | tf_op jit(solution)/shard_map/pallas_call | solution.py:501
  12.9 0.0 collective-permute-done.west_row
  12.9 0.0 collective-permute-done.1.east_row
  12.9 0.6 %shard_map.89 = (f32[48,128]{1,0:T(8,128)S(1)}, f32[2,64,256]{2,1,0:T(8,128)S(1)}, f32[5,2,256]{2,1,0:T(2,128)S(1)}) custom-call(f32[64,16,256]{2,1,0:T(8,128)S(1)} %get-tuple-element.23.sk, s32[2,16,256]{2,1,0:T(8,128)S(1)} %get-tuple-element.29.wd, s32[16,256]{1,0:T(8,128)S(1)} %get-tuple-element.30.oc, f32[16,256]{1,0:T(8,128)S(1)} %get-tuple-element.31.ea, ...), custom_call_target="tpu_custom_call" | custom-call | tf_op jit(solution)/shard_map/pallas_call | solution.py:501
  13.5 0.2 collective-permute-start.6
  13.8 1.0 %collective-permute-done.6 = f32[48,128]{1,0:T(8,128)S(1)} collective-permute-done((f32[48,128]{1,0:T(8,128)S(1)}, f32[48,128]{1,0:T(8,128)S(1)}, u32[]{:S(2)}, u32[]{:S(2)}) %collective-permute-start.6) | collective-permute-done | bytes 24608 | tf_op jit(solution)/shard_map/ppermute | solution.py:610
  14.8 0.0 collective-permute-start.7
  14.8 1.8 %collective-permute-start.2 = (f32[72,256]{1,0:T(8,128)S(1)}, f32[72,256]{1,0:T(8,128)S(1)}, u32[]{:S(2)}, u32[]{:S(2)}) collective-permute-start(f32[72,256]{1,0:T(8,128)S(1)} %get-tuple-element.27), channel_id=1, source_target_pairs={{0,2},{2,4},{4,6},{6,8},{8,10},{10,12},{12,14},{14,16},{16,18},{18... | collective-permute-start | bytes 221192 | tf_op jit(solution)/shard_map/ppermute | solution.py:564
  16.6 1.5 %collective-permute-done.7 = f32[48,128]{1,0:T(8,128)S(1)} collective-permute-done((f32[48,128]{1,0:T(8,128)S(1)}, f32[48,128]{1,0:T(8,128)S(1)}, u32[]{:S(2)}, u32[]{:S(2)}) %collective-permute-start.7) | collective-permute-done | bytes 24608 | tf_op jit(solution)/shard_map/ppermute | solution.py:610
  18.0 0.0 collective-permute-start.8
  18.1 4.7 %collective-permute-start.3 = (f32[72,256]{1,0:T(8,128)S(1)}, f32[72,256]{1,0:T(8,128)S(1)}, u32[]{:S(2)}, u32[]{:S(2)}) collective-permute-start(f32[72,256]{1,0:T(8,128)S(1)} %get-tuple-element.28), channel_id=1, source_target_pairs={{2,0},{4,2},{6,4},{8,6},{10,8},{12,10},{14,12},{16,14},{18,16},{20... | collective-permute-start | bytes 221192 | tf_op jit(solution)/shard_map/ppermute | solution.py:563
  22.8 0.0 collective-permute-done.8
  22.8 0.1 collective-permute-start.9
  22.9 0.5 %shard_map.90 = f32[72,128]{1,0:T(8,128)S(1)} custom-call(f32[16,256]{1,0:T(8,128)S(1)} %get-tuple-element.24.ar, f32[72,256]{1,0:T(8,128)S(1)} %collective-permute-done.west_row, f32[72,256]{1,0:T(8,128)S(1)} %collective-permute-done.1.east_row, f32[14,64,256]{2,1,0:T(8,128)S(1)} %get-tuple-element.35.near, f32[14,64,256]{2,1,0:T(8,128)S(1)} %get-tuple-element.36.far, ...), custom_call_target="tpu_custom_call" | custom-call | tf_op jit(solution)/shard_map/pallas_call | solution.py:501
  23.4 0.2 collective-permute-start.5
  23.6 2.5 %collective-permute-done.9 = f32[48,128]{1,0:T(8,128)S(1)} collective-permute-done((f32[48,128]{1,0:T(8,128)S(1)}, f32[48,128]{1,0:T(8,128)S(1)}, u32[]{:S(2)}, u32[]{:S(2)}) %collective-permute-start.9) | collective-permute-done | bytes 24608 | tf_op jit(solution)/shard_map/ppermute | solution.py:610
  26.1 0.4 %collective-permute-start.10 = (f32[48,128]{1,0:T(8,128)S(1)}, f32[48,128]{1,0:T(8,128)S(1)}, u32[]{:S(2)}, u32[]{:S(2)}) collective-permute-start(f32[48,128]{1,0:T(8,128)S(1)} %add.15.mine), channel_id=1, source_target_pairs={{0,17},{1,16},{2,19},{3,18},{4,21},{5,20},{6,23},{7,22},{8,25},{9,... | collective-permute-start | bytes 73736 | tf_op jit(solution)/shard_map/ppermute | solution.py:610
  26.5 0.0 collective-permute-done.5.got_low.got_high
  26.5 0.5 %shard_map.91.inner_0 = f32[14,32,256]{2,1,0:T(8,128)S(1)} custom-call(f32[16,256]{1,0:T(8,128)S(1)} %get-tuple-element.24.ar, f32[14,64,256]{2,1,0:T(8,128)S(1)} %get-tuple-element.35.near, f32[14,64,256]{2,1,0:T(8,128)S(1)} %get-tuple-element.36.far, f32[5,16,256]{2,1,0:T(8,128)S(1)} %get-tuple-element.37.coef_near, ...), custom_call_target="tpu_custom_call" | custom-call | tf_op jit(solution)/shard_map/pallas_call | solution.py:501
  27.0 0.5 %shard_map.92.inner_1 = f32[14,32,256]{2,1,0:T(8,128)S(1)} custom-call(f32[16,256]{1,0:T(8,128)S(1)} %get-tuple-element.24.ar, f32[14,64,256]{2,1,0:T(8,128)S(1)} %get-tuple-element.35.near, f32[14,64,256]{2,1,0:T(8,128)S(1)} %get-tuple-element.36.far, f32[5,16,256]{2,1,0:T(8,128)S(1)} %get-tuple-element.37.coef_near, ...), custom_call_target="tpu_custom_call" | custom-call | tf_op jit(solution)/shard_map/pallas_call | solution.py:501
  27.5 0.0 collective-permute-done.2.far_west
  27.5 0.0 collective-permute-done.3.far_east
  27.6 1.6 %shard_map.93 = f32[64,16,256]{2,1,0:T(8,128)} custom-call(f32[64,16,256]{2,1,0:T(8,128)S(1)} %get-tuple-element.23.sk, f32[16,256]{1,0:T(8,128)S(1)} %get-tuple-element.24.ar, f32[72,256]{1,0:T(8,128)S(1)} %collective-permute-done.west_row, f32[72,256]{1,0:T(8,128)S(1)} %collective-permute-done.1.east_row, f32[72,256]{1,0:T(8,128)S(1)} %collective-permute-done.2.far_west, ...), custom_call_target="tpu_custom_call" | custom-call | tf_op jit(solution)/shard_map/pallas_call | solution.py:501
  29.1 1.1 %collective-permute-done.10.other = f32[48,128]{1,0:T(8,128)S(1)} collective-permute-done((f32[48,128]{1,0:T(8,128)S(1)}, f32[48,128]{1,0:T(8,128)S(1)}, u32[]{:S(2)}, u32[]{:S(2)}) %collective-permute-start.10) | collective-permute-done | bytes 24608 | tf_op jit(solution)/shard_map/ppermute | solution.py:610
  30.3 0.8 %shard_map.94 = f32[96,96]{1,0:T(8,128)} custom-call(f32[48,128]{1,0:T(8,128)S(1)} %add.15.mine, f32[48,128]{1,0:T(8,128)S(1)} %collective-permute-done.10.other), custom_call_target="tpu_custom_call" | custom-call | tf_op jit(solution)/shard_map/pallas_call | solution.py:501
  (5 shorter events, 0.0 us)
Async XLA Ops:
  2.5 10.3 %collective-permute-start = (f32[72,256]{1,0:T(8,128)S(1)}, f32[72,256]{1,0:T(8,128)S(1)}, u32[]{:S(2)}, u32[]{:S(2)}) collective-permute-start(f32[72,256]{1,0:T(8,128)S(1)} %get-tuple-element.25), channel_id=1, source_target_pairs={{0,2},{2,4},{4,6},{6,8},{8,10},{10,12},{12,14},{14,16},{16,18},{18... | collective-permute-start | bytes 221192 | tf_op jit(solution)/shard_map/ppermute | solution.py:559
  5.6 7.3 %collective-permute-start.1 = (f32[72,256]{1,0:T(8,128)S(1)}, f32[72,256]{1,0:T(8,128)S(1)}, u32[]{:S(2)}, u32[]{:S(2)}) collective-permute-start(f32[72,256]{1,0:T(8,128)S(1)} %get-tuple-element.26), channel_id=1, source_target_pairs={{2,0},{4,2},{6,4},{8,6},{10,8},{12,10},{14,12},{16,14},{18,16},{20... | collective-permute-start | bytes 221192 | tf_op jit(solution)/shard_map/ppermute | solution.py:560
  9.6 1.2 %collective-permute-start.4 = (f32[72,128]{1,0:T(8,128)S(1)}, f32[72,128]{1,0:T(8,128)S(1)}, u32[]{:S(2)}, u32[]{:S(2)}) collective-permute-start(f32[72,128]{1,0:T(8,128)S(1)} %get-tuple-element.34), channel_id=1, source_target_pairs={{0,1},{1,0},{2,3},{3,2},{4,5},{5,4},{6,7},{7,6},{8,9},{9,8},{10,11... | collective-permute-start | bytes 110600 | tf_op jit(solution)/shard_map/ppermute | solution.py:529
  13.5 1.3 %collective-permute-start.6 = (f32[48,128]{1,0:T(8,128)S(1)}, f32[48,128]{1,0:T(8,128)S(1)}, u32[]{:S(2)}, u32[]{:S(2)}) collective-permute-start(f32[48,128]{1,0:T(8,128)S(1)} %get-tuple-element.43), channel_id=1, source_target_pairs={{0,1},{1,0},{2,3},{3,2},{4,5},{5,4},{6,7},{7,6},{8,9},{9,8},{10,11... | collective-permute-start | bytes 73736 | tf_op jit(solution)/shard_map/ppermute | solution.py:610
  14.8 3.3 %collective-permute-start.7 = (f32[48,128]{1,0:T(8,128)S(1)}, f32[48,128]{1,0:T(8,128)S(1)}, u32[]{:S(2)}, u32[]{:S(2)}) collective-permute-start(f32[48,128]{1,0:T(8,128)S(1)} %add.12), channel_id=1, source_target_pairs={{0,3},{1,2},{2,1},{3,0},{4,7},{5,6},{6,5},{7,4},{8,11},{9,10},{10,... | collective-permute-start | bytes 73736 | tf_op jit(solution)/shard_map/ppermute | solution.py:610
  14.8 12.7 %collective-permute-start.2 = (f32[72,256]{1,0:T(8,128)S(1)}, f32[72,256]{1,0:T(8,128)S(1)}, u32[]{:S(2)}, u32[]{:S(2)}) collective-permute-start(f32[72,256]{1,0:T(8,128)S(1)} %get-tuple-element.27), channel_id=1, source_target_pairs={{0,2},{2,4},{4,6},{6,8},{8,10},{10,12},{12,14},{14,16},{16,18},{18... | collective-permute-start | bytes 221192 | tf_op jit(solution)/shard_map/ppermute | solution.py:564
  18.0 4.7 %collective-permute-start.8 = (f32[48,128]{1,0:T(8,128)S(1)}, f32[48,128]{1,0:T(8,128)S(1)}, u32[]{:S(2)}, u32[]{:S(2)}) collective-permute-start(f32[48,128]{1,0:T(8,128)S(1)} %add.13), channel_id=1, source_target_pairs={{0,5},{1,4},{2,7},{3,6},{4,1},{5,0},{6,3},{7,2},{8,13},{9,12},{10,... | collective-permute-start | bytes 73736 | tf_op jit(solution)/shard_map/ppermute | solution.py:610
  18.1 9.5 %collective-permute-start.3 = (f32[72,256]{1,0:T(8,128)S(1)}, f32[72,256]{1,0:T(8,128)S(1)}, u32[]{:S(2)}, u32[]{:S(2)}) collective-permute-start(f32[72,256]{1,0:T(8,128)S(1)} %get-tuple-element.28), channel_id=1, source_target_pairs={{2,0},{4,2},{6,4},{8,6},{10,8},{12,10},{14,12},{16,14},{18,16},{20... | collective-permute-start | bytes 221192 | tf_op jit(solution)/shard_map/ppermute | solution.py:563
  22.8 3.3 %collective-permute-start.9 = (f32[48,128]{1,0:T(8,128)S(1)}, f32[48,128]{1,0:T(8,128)S(1)}, u32[]{:S(2)}, u32[]{:S(2)}) collective-permute-start(f32[48,128]{1,0:T(8,128)S(1)} %add.14), channel_id=1, source_target_pairs={{0,9},{1,8},{2,11},{3,10},{4,13},{5,12},{6,15},{7,14},{8,1},{9,0},... | collective-permute-start | bytes 73736 | tf_op jit(solution)/shard_map/ppermute | solution.py:610
  23.4 3.1 %collective-permute-start.5 = (f32[72,128]{1,0:T(8,128)S(1)}, f32[72,128]{1,0:T(8,128)S(1)}, u32[]{:S(2)}, u32[]{:S(2)}) collective-permute-start(f32[72,128]{1,0:T(8,128)S(1)} %shard_map.90), channel_id=1, source_target_pairs={{0,1},{1,0},{2,3},{3,2},{4,5},{5,4},{6,7},{7,6},{8,9},{9,8},{10,11... | collective-permute-start | bytes 110600 | tf_op jit(solution)/shard_map/ppermute | solution.py:529
  26.1 4.2 %collective-permute-start.10 = (f32[48,128]{1,0:T(8,128)S(1)}, f32[48,128]{1,0:T(8,128)S(1)}, u32[]{:S(2)}, u32[]{:S(2)}) collective-permute-start(f32[48,128]{1,0:T(8,128)S(1)} %add.15.mine), channel_id=1, source_target_pairs={{0,17},{1,16},{2,19},{3,18},{4,21},{5,20},{6,23},{7,22},{8,25},{9,... | collective-permute-start | bytes 73736 | tf_op jit(solution)/shard_map/ppermute | solution.py:610

commit v5 on v4

--- a/solution.py
+++ b/solution.py
@@ -72,7 +72,7 @@
 
 def end_row(sizes, sk, wd, oc, fields, first, r):
     count, base = sizes.count, sizes.count + sizes.words
-    first[0:count, :] = sk[:, r, :]
+    first[0:count, :] = sk[r]
     for w in range(sizes.words):
         first[count + w : count + w + 1, :] = wd[w, r : r + 1, :].astype(F32)
     first[base : base + 1, :] = oc[r : r + 1, :].astype(F32)
@@ -84,60 +84,48 @@
 
 
 def load_kernel(sizes, *refs):
-    given, held, rows, edges, sems = refs[:7], refs[7:14], refs[14:18], refs[18:-1], refs[-1]
+    given, held, rows, tiles, sems = refs[:7], refs[7:14], refs[14:18], refs[18:-1], refs[-1]
     n, count = sizes.lons, sizes.count
-    copies = [pltpu.make_async_copy(g, h, sems.at[k]) for k, (g, h) in enumerate(zip(given, held))]
+    last = sizes.lats - LANES
+    low_first = lax.axis_index("lat") == 0
+    pairs = [(given[0].at[:, i, :], held[0].at[i]) for i in range(n)]
+    pairs += list(zip(given[1:], held[1:]))
+    copies = [pltpu.make_async_copy(g, h, sems.at[k]) for k, (g, h) in enumerate(pairs)]
     for copy in copies:
         copy.start()
-    for copy in copies:
+    sk, wd, oc, ea, no = held[:5]
+    base = sizes.words * n
+
+    def end(ref, k):
+        low, high = ref[..., 0:LANES], ref[..., last:]
+        if sizes.paired:
+            return lax.select(low_first, high, low)
+        return (low, high)[k]
+
+    for copy in copies[n:]:
         copy.wait()
-    sk, wd, oc, ea = held[:4]
-    for ref, r in zip(rows[:2], (n - 1, 0)):
-        end_row(sizes, sk, wd, oc, held[3:], ref, r)
-    for ref, r in zip(rows[2:], (n - 2, 1)):
-        ref[0:count, :] = sk[:, r, :]
-        ref[count : count + 1, :] = oc[r : r + 1, :].astype(F32)
-        ref[count + 1 : count + 2, :] = ea[r : r + 1, :]
-        ref[count + 2 :, :] = jnp.zeros((ref.shape[0] - count - 2, sizes.lats), F32)
-
-
-    no = held[4]
-    last = sizes.lats - LANES
-    for start in range(0, count, BITS):
-        ids = lane_ids(BITS)
-        total = [jnp.zeros((BITS, LANES), F32) for _ in edges]
-        for i in range(n):
-            low = sk[start : start + BITS, i, 0:LANES]
-            high = sk[start : start + BITS, i, last:]
-            moved = edge_rows_of(sizes, low, high, i)
-            total = [jnp.where(ids == i, m, t) for m, t in zip(moved, total)]
-        for edge, t in zip(edges, total):
-            edge[start : start + BITS, :] = t
-
-    def ends_of(at):
-        parts = [wd[w, :, at : at + LANES].astype(F32) for w in range(sizes.words)]
-        parts += [oc[:, at : at + LANES].astype(F32), no[:, at : at + LANES]]
-        spare = LANES - n * len(parts)
-        parts.append(jnp.zeros((spare, LANES), F32))
-        return jnp.concatenate(parts, axis=0).T
-
-    low, high = ends_of(0)[0:1, :], ends_of(last)[LANES - 1 :, :]
-    if sizes.paired:
-        rows = [lax.select(lax.axis_index("lat") == 0, high, low)]
-    else:
-        rows = [low, high]
-    for edge, row in zip(edges, rows):
-        edge[count:, :] = jnp.broadcast_to(row, (sizes.edge_rows - count, LANES))
-
-
-def edge_columns(edge, sizes, index):
-    row = edge[sizes.count : sizes.count + 1, :]
-    turned = jnp.broadcast_to(row, (LANES, LANES)).T
-    return turned[index * sizes.lons : (index + 1) * sizes.lons, 0:1]
+    for k, tile in enumerate(tiles):
+        words = end(wd, k).astype(F32)
+        for w in range(sizes.words):
+            tile[n, w * n : (w + 1) * n, :] = words[w]
+        tile[n, base : base + n, :] = end(oc, k).astype(F32)
+        tile[n, base + n : base + 2 * n, :] = end(no, k)
+    for i in range(n):
+        copies[i].wait()
+        for k, tile in enumerate(tiles):
+            tile[i, 0:count] = end(sk.at[i], k)
+        if i in (0, n - 1):
+            end_row(sizes, sk, wd, oc, held[3:], rows[0 if i else 1], i)
+        if i in (1, n - 2):
+            ref = rows[3 if i == 1 else 2]
+            ref[0:count, :] = sk[i]
+            ref[count : count + 1, :] = oc[i : i + 1, :].astype(F32)
+            ref[count + 1 : count + 2, :] = ea[i : i + 1, :]
+            ref[count + 2 :, :] = jnp.zeros((ref.shape[0] - count - 2, sizes.lats), F32)
 
 
 def far_side():
-    return lax.axis_index("lon") == lax.axis_size("lon") - 1
+    return lax.axis_index("lon") >= 3
 
 
 def products(split_hi, split_lo):
@@ -153,15 +141,37 @@
     split_lo[rows, at] = (scaled - high.astype(F32)).astype(jnp.bfloat16)
 
 
-def rows_of(refs, where):
-    return list(zip(*[halves(refs[(k,) + where]) for k in range(5)]))
+def put_row(ref, where, rows, field):
+    for h, part in enumerate(halves(field)):
+        ref[where + (h, rows)] = part
+
+
+def get_row(ref, where, i):
+    tiles = [ref[where + (h, slice(i, i + 1))] for h in range(ref.shape[-3])]
+    return jnp.concatenate(tiles, axis=1)
+
+
+def spread_row(ref, where, i):
+    tiles = [ref[where + (h, pl.ds(i, 8, stride=0))] for h in range(ref.shape[-3])]
+    return [jnp.concatenate([tile] * (BITS // 8), axis=0) for tile in tiles]
+
+
+def rows_of(ref, i):
+    return list(zip(*[spread_row(ref, (k,), i) for k in range(5)]))
+
+
+def sketch_edges(got_low, got_high, rows):
+    return lambda i: (pltpu.roll(got_low[i, rows, :], 1, 1), pltpu.roll(got_high[i, rows, :], LANES - 1, 1))
 
 
 def probe_edges(sizes, w, got_low, got_high):
-    edges = []
-    for got in (got_low, got_high):
-        row = got[sizes.count : sizes.count + 1, :].astype(jnp.int32)
-        edges.append(spread(pltpu.roll(row, (LANES - w * sizes.lons) % LANES, 1)))
+    n = sizes.lons
+
+    def edges(i):
+        at = w * n + i
+        low, high = (got[n, at : at + 1, :].astype(jnp.int32) for got in (got_low, got_high))
+        return spread(pltpu.roll(low, 1, 1)), spread(pltpu.roll(high, LANES - 1, 1))
+
     return edges
 
 
@@ -182,46 +192,44 @@
         east_w = ext[1, 8 : 8 + n, :]
         west_w = ext[1, 7 : 7 + n, :]
 
-        sea_low, north_low = (edge_columns(got_low, sizes, words + k) for k in (0, 1))
-        sea_high = edge_columns(got_high, sizes, words)
         sea_parts = halves(sea)
         half_north = [no[:, h * LANES : (h + 1) * LANES] * part for h, part in enumerate(sea_parts)]
         at_low = jnp.where(lat_id == 0, 0.0, 1.0)
         at_high = jnp.where(lat_id == sizes.lat_axis - 1, 0.0, 1.0)
-        edge_high = jnp.broadcast_to(sea_high * at_high, (n, LANES))
-        edge_low = jnp.broadcast_to(sea_low * north_low * at_low, (n, LANES))
+        edge_high = pltpu.roll(got_high[n, words * n : (words + 1) * n, :], LANES - 1, 1) * at_high
+        flow_low = got_low[n, words * n : (words + 1) * n, :] * got_low[n, (words + 1) * n : (words + 2) * n, :]
+        edge_low = pltpu.roll(flow_low, 1, 1) * at_low
         sea_north, _ = lat_shifts(sea_parts, edge_low, edge_high)
         _, flow_south = lat_shifts(half_north, edge_low, edge_high)
         north_w = jnp.concatenate([a * b for a, b in zip(half_north, sea_north)], axis=1)
         south_w = jnp.concatenate([a * b for a, b in zip(flow_south, sea_parts)], axis=1)
-        coef[0] = sea * (ka[...] + east_w + west_w + north_w + south_w)
-        coef[1] = east_w
-        coef[2] = west_w
-        coef[3] = north_w
-        coef[4] = south_w
-        root[...] = jnp.sqrt(ar[...])
-
-        def one_block(start, get, low_edge, high_edge, keep):
+        put_row(coef, (0,), slice(0, n), sea * (ka[...] + east_w + west_w + north_w + south_w))
+        put_row(coef, (1,), slice(0, n), east_w)
+        put_row(coef, (2,), slice(0, n), west_w)
+        put_row(coef, (3,), slice(0, n), north_w)
+        put_row(coef, (4,), slice(0, n), south_w)
+        put_row(coef, (5,), slice(0, n), ar[...])
+        put_row(root, (), slice(0, n), jnp.sqrt(ar[...]))
+
+        def one_block(start, get, edges, keep):
             rows = pl.ds(start, BITS)
             west, middle = get(0), get(1)
             for i in range(1, n - 1):
                 east = get(i + 1)
-                north, south = lat_shifts(
-                    middle, edge_at(low_edge, i, 0), edge_at(high_edge, i, LANES - 1)
-                )
-                weights = rows_of(coef, (slice(i, i + 1), slice(None)))
+                north, south = lat_shifts(middle, *edges(i))
+                weights, scale = rows_of(coef, i), spread_row(root, (), i)
                 for h, part in enumerate(stencil(weights, middle, east, west, north, south)):
                     here = slice(h * LANES, (h + 1) * LANES)
                     if keep:
                         applied[i - 1, rows, here] = part
                     at = slice((i - 1) * lats + h * LANES, (i - 1) * lats + (h + 1) * LANES)
-                    store_split(split_hi, split_lo, rows, at, part * root[i : i + 1, here])
+                    store_split(split_hi, split_lo, rows, at, part * scale[h])
                 west, middle = middle, east
 
         def sketch_block(k, carry):
             start = pl.multiple_of(k * BITS, BITS)
             rows = pl.ds(start, BITS)
-            one_block(start, lambda i: halves(sk[rows, i, :]), got_low[rows, :], got_high[rows, :], True)
+            one_block(start, lambda i: halves(sk[i, rows, :]), sketch_edges(got_low, got_high, rows), True)
             return carry
 
         lax.fori_loop(0, count // BITS, sketch_block, 0)
@@ -229,7 +237,7 @@
             one_block(
                 count + w * BITS,
                 lambda i: [spread(part) for part in halves(wd[w, i : i + 1, :])],
-                *probe_edges(sizes, w, got_low, got_high),
+                probe_edges(sizes, w, got_low, got_high),
                 False,
             )
         partial[...] = products(split_hi, split_lo)
@@ -245,7 +253,7 @@
     far = far_side()
 
     def inner(k, i):
-        return lax.select(far, coef_far[k, i : i + 1, :], coef_near[k, i : i + 1, :])
+        return lax.select(far, get_row(coef_far, (k,), i), get_row(coef_near, (k,), i))
 
     root = []
     for side, i in enumerate((0, n - 1)):
@@ -257,15 +265,15 @@
             east_w = ea[i : i + 1, :] * sea * east_row[base : base + 1, :]
         center = sea * (ka[i : i + 1, :] + east_w + west_w + north_w + south_w)
         for k, row in enumerate((center, east_w, west_w, north_w, south_w)):
-            end_coef[k, side : side + 1, :] = row
+            put_row(end_coef, (k,), slice(side, side + 1), row)
         root.append(jnp.sqrt(ar[i : i + 1, :]))
 
-    def one_block(start, get, low_edge, high_edge, keep):
+    def one_block(start, get, edges, keep):
         rows = pl.ds(start, BITS)
         for side, i in enumerate((0, n - 1)):
             middle = get(i)
-            north, south = lat_shifts(middle, edge_at(low_edge, i, 0), edge_at(high_edge, i, LANES - 1))
-            weights = rows_of(end_coef, (slice(side, side + 1), slice(None)))
+            north, south = lat_shifts(middle, *edges(i))
+            weights = rows_of(end_coef, side)
             for h, part in enumerate(stencil(weights, middle, get(i + 1), get(i - 1), north, south)):
                 here = slice(h * LANES, (h + 1) * LANES)
                 if keep:
@@ -281,9 +289,9 @@
                 return halves(west_row[rows, :])
             if i == n:
                 return halves(east_row[rows, :])
-            return halves(sk[rows, i, :])
-
-        one_block(start, get, got_low[rows, :], got_high[rows, :], True)
+            return halves(sk[i, rows, :])
+
+        one_block(start, get, sketch_edges(got_low, got_high, rows), True)
     for w in range(words):
 
         def get(i):
@@ -295,7 +303,7 @@
                 row = wd[w, i : i + 1, :]
             return [spread(part) for part in halves(row)]
 
-        one_block(count + w * BITS, get, *probe_edges(sizes, w, got_low, got_high), False)
+        one_block(count + w * BITS, get, probe_edges(sizes, w, got_low, got_high), False)
 
     total = lax.select(far, partial_far[...], partial_near[...]) + products(split_hi, split_lo)
     if not sizes.folded:
@@ -376,7 +384,7 @@
         edge[count : count + 8, :] = t
 
 
-def image_inner_kernel(part, sizes, ar, near, far, coef_near, coef_far, ends, end_coef, got_low, got_high, out):
+def image_inner_kernel(part, sizes, near, far, coef_near, coef_far, ends, got_low, got_high, out):
     n, count = sizes.lons, sizes.count
     blocks = count // BITS // 2
 
@@ -388,7 +396,7 @@
 
             def get(i):
                 source = applied[i - 1, rows, :] if 0 < i < n - 1 else ends[min(i, 1), rows, :]
-                return halves(source * ar[i : i + 1, :])
+                return [a * b for a, b in zip(halves(source), spread_row(coef, (5,), i))]
 
             west, middle = get(0), get(1)
             for i in range(1, n - 1):
@@ -396,7 +404,7 @@
                 north, south = lat_shifts(
                     middle, edge_at(low_edge, i, 0), edge_at(high_edge, i, LANES - 1)
                 )
-                weights = rows_of(coef, (slice(i, i + 1), slice(None)))
+                weights = rows_of(coef, i)
                 for h, tile in enumerate(stencil(weights, middle, east, west, north, south)):
                     out[i - 1, here, h * LANES : (h + 1) * LANES] = tile
                 west, middle = middle, east
@@ -424,11 +432,11 @@
         rows = near_rows[side]
         sea, east, north, kappa, area = (rows[k : k + 1] for k in range(5))
         if side == 0:
-            east_w = end_coef[2, 0:1, :]
+            east_w = get_row(end_coef, (2,), 0)
             west_w = far_rows[0][1:2] * far_rows[0][0:1] * sea
         else:
             east_w = east * sea * far_rows[1][0:1]
-            west_w = end_coef[1, 1:2, :]
+            west_w = get_row(end_coef, (1,), 1)
         lane = n + side
         low = got_low[count : count + 8, :]
         high = got_high[count : count + 8, :]
@@ -444,21 +452,23 @@
         ghost.append(list(zip(*[halves(r * area) for r in (center, east_w, west_w, north_w, south_w)])))
 
     far_lon = far_side()
-
-    def copy_out(k):
+    copies = []
+    for part, inner in enumerate((inner_0, inner_1)):
+        columns = pl.ds(part * (count // 2), count // 2)
+        copies += [(inner.at[i - 1], out.at[columns, i, :]) for i in range(1, n - 1)]
+    copies += [(buffer.at[side], out.at[:, i, :]) for side, i in enumerate((0, n - 1))]
+    copies = [pltpu.make_async_copy(a, b, sems.at[k]) for k, (a, b) in enumerate(copies)]
+    for copy in copies[:-2]:
+        copy.start()
+
+    def block(k, carry):
         start = pl.multiple_of(k * BITS, BITS)
-        return pltpu.make_async_copy(buffer.at[k], out.at[pl.ds(start, BITS)], sems.at[k])
-
-    def block_of(k, half, inner):
-        start = pl.multiple_of(k * BITS, BITS)
-        rows, here = pl.ds(start, BITS), pl.ds(pl.multiple_of((k - half) * BITS, BITS), BITS)
+        rows = pl.ds(start, BITS)
         low_edge, high_edge = got_low[rows, :], got_high[rows, :]
-        for i in range(1, n - 1):
-            buffer[k, :, i, :] = inner[i - 1, here, :]
         for side, i in enumerate((0, n - 1)):
             middle = halves((west_row, east_row)[side][rows, :])
             beyond = halves((far_west, far_east)[side][rows, :])
-            own = halves(sk[rows, i, :])
+            own = halves(sk[i, rows, :])
             east, west = (own, beyond) if side == 0 else (beyond, own)
             north, south = lat_shifts(
                 middle,
@@ -474,25 +484,16 @@
             north, south = lat_shifts(
                 middle, edge_at(low_edge, i, 0), edge_at(high_edge, i, LANES - 1)
             )
-            weights = rows_of(end_coef, (slice(side, side + 1), slice(None)))
+            weights = rows_of(end_coef, side)
             for h, tile in enumerate(stencil(weights, middle, east, west, north, south)):
-                buffer[k, :, i, h * LANES : (h + 1) * LANES] = tile
-        copy_out(k).start()
-
-    half = count // BITS // 2
-
-    def first(k, carry):
-        block_of(k, 0, inner_0)
+                buffer[side, rows, h * LANES : (h + 1) * LANES] = tile
         return carry
 
-    def second(k, carry):
-        block_of(k, half, inner_1)
-        return carry
-
-    lax.fori_loop(0, half, first, 0)
-    lax.fori_loop(half, 2 * half, second, 0)
-    for k in range(2 * half):
-        copy_out(k).wait()
+    lax.fori_loop(0, count // BITS, block, 0)
+    for copy in copies[-2:]:
+        copy.start()
+    for copy in copies:
+        copy.wait()
 
 
 def call(kernel, sizes, outs, args, scratch=(), inputs=None, out_space=pltpu.VMEM, alias=None):
@@ -512,9 +513,11 @@
 def exchanges():
     lons, lats = lax.axis_size("lon"), lax.axis_size("lat")
     steps = [[(i * lats + j, i * lats + (j ^ bit)) for i in range(lons) for j in range(lats)] for bit in powers(lats)]
+    lon_bits = powers(lons)
+    lon_bits[:2] = reversed(lon_bits[:2])
     steps += [
         [(i * lats + j, (i ^ bit) * lats + (lats - 1 - j)) for i in range(lons) for j in range(lats)]
-        for bit in powers(lons)
+        for bit in lon_bits
     ]
     return steps
 
@@ -546,12 +549,13 @@
     edge_count = 1 if sizes.paired else 2
 
     shapes = [jax.ShapeDtypeStruct(f.shape, f.dtype) for f in fields]
+    shapes[0] = jax.ShapeDtypeStruct((n, count, lats), F32)
     loaded = call(
         load_kernel,
         sizes,
-        shapes + [line, line, far_line, far_line] + [edge] * edge_count,
+        shapes + [line, line, far_line, far_line] + [(n + 1, max(count, (sizes.words + 2) * n), LANES)] * edge_count,
         [pltpu.with_memory_space_constraint(f, pltpu.HBM) for f in fields],
-        [pltpu.SemaphoreType.DMA((7,))],
+        [pltpu.SemaphoreType.DMA((6 + n,))],
         inputs=[pltpu.HBM] * len(fields),
     )
     fields, (to_east, to_west, far_to_east, far_to_west), packed = tuple(loaded[:7]), loaded[7:11], loaded[11:]
@@ -570,9 +574,9 @@
         call(
             functools.partial(inner_kernel, far),
             sizes,
-            [(n - 2, count, lats), (5, n, lats), (sizes.cols, sizes.cols)],
+            [(n - 2, count, lats), (6, lats // LANES, n + 8, LANES), (sizes.cols, sizes.cols)],
             fields + (low, high),
-            split(n - 2) + [pltpu.VMEM((2, n + 16, lats), F32), pltpu.VMEM((n, lats), F32)],
+            split(n - 2) + [pltpu.VMEM((2, n + 16, lats), F32), pltpu.VMEM((lats // LANES, n + 8, LANES), F32)],
         )
         for far in (False, True)
     ]
@@ -580,7 +584,7 @@
     gram, ends, end_coef = call(
         gram_kernel,
         sizes,
-        [(sizes.cols // 2, LANES) if sizes.folded else (sizes.cols, sizes.cols), (2, count, lats), (5, 2, lats)],
+        [(sizes.cols // 2, LANES) if sizes.folded else (sizes.cols, sizes.cols), (2, count, lats), (5, lats // LANES, 16, LANES)],
         (sketch, probe_bits, ocean, east_cond, kappa_sq, inv_area, west_row, east_row, low, high)
         + (coef_near, coef_far, partial_near, partial_far),
         split(2) + [pltpu.VMEM((sizes.cols, LANES), F32)],
@@ -592,17 +596,17 @@
             functools.partial(image_inner_kernel, part),
             sizes,
             [(n - 2, count // 2, lats)],
-            (inv_area, near, far, coef_near, coef_far, ends, end_coef, low2, high2),
+            (near, far, coef_near, coef_far, ends, low2, high2),
         )[0]
         for part in range(2)
     ]
     (image,) = call(
         image_kernel,
         sizes,
-        [sketch.shape],
+        [(count, n, lats)],
         (sketch, inv_area, west_row, east_row, far_west, far_east, near, far, ends, end_coef, low2, high2)
         + tuple(inner_images),
-        [pltpu.VMEM((count // BITS, BITS, n, lats), F32), pltpu.SemaphoreType.DMA((count // BITS,))],
+        [pltpu.VMEM((2, count, lats), F32), pltpu.SemaphoreType.DMA((2 * n - 2,))],
         out_space=pltpu.HBM,
     )
     steps = exchanges()

time: 31.2 us -> 31.8 us (1.019)
  waiting for transfers between devices: 7.39 us -> 8.12 us
  Pallas kernels: 8.45 us -> 8.04 us
    ppermute x2, waiting for transfers between devices: 1.21 us -> 0.01 us  [swap_edges(): got = lax.ppermute(edges[0], 'lat', [(0, 1), (1, 0)])]
    ppermute x5, waiting for transfers between devices: 6.17 us -> 7.17 us  [local(): other = lax.ppermute(gram, ('lon', 'lat'), pairs)]
    ppermute x1, waiting for transfers between devices: 0.01 us -> 0.93 us  [local(): west_row = lax.ppermute(to_east, 'lon', eastward)]
    ppermute x1, starting transfers between devices: 3.02 us -> 2.54 us  [local(): west_row = lax.ppermute(to_east, 'lon', eastward)]
    ppermute x2, starting transfers between devices: 0.16 us -> 0.57 us  [swap_edges(): got = lax.ppermute(edges[0], 'lat', [(0, 1), (1, 0)])]
    pallas_call x9, Pallas kernels: 8.45 us -> 8.04 us  [call(): pl.pallas_call(functools.partial(kernel, sizes), out_shape=outs, in_specs...]
    ppermute x1, starting transfers between devices: 4.73 us -> 5.13 us  [local(): far_east = lax.ppermute(far_to_west, 'lon', westward)]
  transfers between devices with their start and end apart: 11 -> 11, of which waited for: 5 -> 5; matrix products, arithmetic and copies ran while one was open for 0% -> 0% of each run, Pallas kernels for 17% -> 16%
where the time goes in v5:
time: 31.8 us; the launch traced here: 31.6 us
  starting transfers between devices  14.7 us (46%)
  waiting for transfers between devices  8.12 us (26%)
  Pallas kernels  8.04 us (25%)
  between operations  0.75 us (2%)
    pallas_call x9, Pallas kernels, call(): pl.pallas_call(functools.partial(kernel, sizes), out_shape=outs, in_specs...  8.04 us
    ppermute x5, waiting for transfers between devices, local(): other = lax.ppermute(gram, ('lon', 'lat'), pairs)  7.17 us
    ppermute x1, starting transfers between devices, local(): far_east = lax.ppermute(far_to_west, 'lon', westward)  5.13 us
    ppermute x1, starting transfers between devices, local(): east_row = lax.ppermute(to_west, 'lon', westward)  4.06 us
    ppermute x1, starting transfers between devices, local(): west_row = lax.ppermute(to_east, 'lon', eastward)  2.54 us
    ppermute x1, starting transfers between devices, local(): far_west = lax.ppermute(far_to_east, 'lon', eastward)  2.03 us
    ppermute x1, waiting for transfers between devices, local(): west_row = lax.ppermute(to_east, 'lon', eastward)  0.93 us
  transfers between devices with their start and end apart: 11, of which 5 were waited for; matrix products, arithmetic and copies ran while one was open for 0% of the time, Pallas kernels for 16%

profile of v5, /device:TPU:0, one launch (start us, length us, event | category | flops | bytes accessed | tf_op | source)
XLA Modules:
  0.0 31.6 jit_solution(8407348560138901850)
XLA Ops:
  0.6 1.6 %shard_map.86 = (f32[16,64,256]{2,1,0:T(8,128)S(1)}, s32[2,16,256]{2,1,0:T(8,128)S(1)}, s32[16,256]{1,0:T(8,128)S(1)}, f32[16,256]{1,0:T(8,128)S(1)}, f32[16,256...) custom-call(f32[64,16,256]{2,1,0:T(8,128)} %refs_0_.1, ...), custom_call_target="tpu_custom_call" | custom-call | tf_op jit(solution)/shard_map/pallas_call | solution.py:502
  2.3 0.6 %collective-permute-start.4 = (f32[17,64,128]{2,1,0:T(8,128)S(1)}, f32[17,64,128]{2,1,0:T(8,128)S(1)}, u32[]{:S(2)}, u32[]{:S(2)}) collective-permute-start(f32[17,64,128]{2,1,0:T(8,128)S(1)} %get-tuple-element.34), channel_id=1, source_target_pairs={{0,1},{1,0},{2,3},{3,2},{4,5},{5,4},{6,7},{7,6},{8,9},{9,8},{10,11... | collective-permute-start | bytes 1671176 | tf_op jit(solution)/shard_map/ppermute | solution.py:532
  2.8 2.5 %collective-permute-start = (f32[72,256]{1,0:T(8,128)S(1)}, f32[72,256]{1,0:T(8,128)S(1)}, u32[]{:S(2)}, u32[]{:S(2)}) collective-permute-start(f32[72,256]{1,0:T(8,128)S(1)} %get-tuple-element.25), channel_id=1, source_target_pairs={{0,2},{2,4},{4,6},{6,8},{8,10},{10,12},{12,14},{14,16},{16,18},{18... | collective-permute-start | bytes 221192 | tf_op jit(solution)/shard_map/ppermute | solution.py:563
  5.4 4.1 %collective-permute-start.1 = (f32[72,256]{1,0:T(8,128)S(1)}, f32[72,256]{1,0:T(8,128)S(1)}, u32[]{:S(2)}, u32[]{:S(2)}) collective-permute-start(f32[72,256]{1,0:T(8,128)S(1)} %get-tuple-element.26), channel_id=1, source_target_pairs={{2,0},{4,2},{6,4},{8,6},{10,8},{12,10},{14,12},{16,14},{18,16},{20... | collective-permute-start | bytes 221192 | tf_op jit(solution)/shard_map/ppermute | solution.py:564
  9.4 0.0 collective-permute-done.4.got_low.got_high
  9.4 1.9 %shard_map.87 = (f32[14,64,256]{2,1,0:T(8,128)S(1)}, f32[6,2,24,128]{3,2,1,0:T(8,128)S(1)}, f32[96,96]{1,0:T(8,128)S(1)}) custom-call(f32[16,64,256]{2,1,0:T(8,128)S(1)} %get-tuple-element.23.sk, s32[2,16,256]{2,1,0:T(8,128)S(1)} %get-tuple-element.29.wd, s32[16,256]{1,0:T(8,128)S(1)} %get-tuple-element.30.oc, f32[16,256]{1,0:T(8,128)S(1)} %get-tuple-element.31.ea, ...), custom_call_target="tpu_custom_call" | custom-call | tf_op jit(solution)/shard_map/pallas_call | solution.py:502
  11.3 0.9 %collective-permute-done.west_row = f32[72,256]{1,0:T(8,128)S(1)} collective-permute-done((f32[72,256]{1,0:T(8,128)S(1)}, f32[72,256]{1,0:T(8,128)S(1)}, u32[]{:S(2)}, u32[]{:S(2)}) %collective-permute-start) | collective-permute-done | bytes 73760 | tf_op jit(solution)/shard_map/ppermute | solution.py:563
  12.3 0.0 collective-permute-done.1.east_row
  12.3 0.6 %shard_map.89 = (f32[48,128]{1,0:T(8,128)S(1)}, f32[2,64,256]{2,1,0:T(8,128)S(1)}, f32[5,2,16,128]{3,2,1,0:T(8,128)S(1)}) custom-call(f32[16,64,256]{2,1,0:T(8,128)S(1)} %get-tuple-element.23.sk, s32[2,16,256]{2,1,0:T(8,128)S(1)} %get-tuple-element.29.wd, s32[16,256]{1,0:T(8,128)S(1)} %get-tuple-element.30.oc, f32[16,256]{1,0:T(8,128)S(1)} %get-tuple-element.31.ea, ...), custom_call_target="tpu_custom_call" | custom-call | tf_op jit(solution)/shard_map/pallas_call | solution.py:502
  12.9 0.1 collective-permute-start.6
  12.9 1.2 %collective-permute-done.6 = f32[48,128]{1,0:T(8,128)S(1)} collective-permute-done((f32[48,128]{1,0:T(8,128)S(1)}, f32[48,128]{1,0:T(8,128)S(1)}, u32[]{:S(2)}, u32[]{:S(2)}) %collective-permute-start.6) | collective-permute-done | bytes 24608 | tf_op jit(solution)/shard_map/ppermute | solution.py:614
  14.1 0.0 collective-permute-start.7
  14.1 2.0 %collective-permute-start.2 = (f32[72,256]{1,0:T(8,128)S(1)}, f32[72,256]{1,0:T(8,128)S(1)}, u32[]{:S(2)}, u32[]{:S(2)}) collective-permute-start(f32[72,256]{1,0:T(8,128)S(1)} %get-tuple-element.27), channel_id=1, source_target_pairs={{0,2},{2,4},{4,6},{6,8},{8,10},{10,12},{12,14},{14,16},{16,18},{18... | collective-permute-start | bytes 221192 | tf_op jit(solution)/shard_map/ppermute | solution.py:568
  16.2 1.2 %collective-permute-done.7 = f32[48,128]{1,0:T(8,128)S(1)} collective-permute-done((f32[48,128]{1,0:T(8,128)S(1)}, f32[48,128]{1,0:T(8,128)S(1)}, u32[]{:S(2)}, u32[]{:S(2)}) %collective-permute-start.7) | collective-permute-done | bytes 24608 | tf_op jit(solution)/shard_map/ppermute | solution.py:614
  17.4 0.2 collective-permute-start.8
  17.6 5.1 %collective-permute-start.3 = (f32[72,256]{1,0:T(8,128)S(1)}, f32[72,256]{1,0:T(8,128)S(1)}, u32[]{:S(2)}, u32[]{:S(2)}) collective-permute-start(f32[72,256]{1,0:T(8,128)S(1)} %get-tuple-element.28), channel_id=1, source_target_pairs={{2,0},{4,2},{6,4},{8,6},{10,8},{12,10},{14,12},{16,14},{18,16},{20... | collective-permute-start | bytes 221192 | tf_op jit(solution)/shard_map/ppermute | solution.py:567
  22.8 0.0 collective-permute-done.8
  22.8 0.1 collective-permute-start.9
  22.8 0.5 %shard_map.90 = f32[72,128]{1,0:T(8,128)S(1)} custom-call(f32[16,256]{1,0:T(8,128)S(1)} %get-tuple-element.24.ar, f32[72,256]{1,0:T(8,128)S(1)} %collective-permute-done.west_row, f32[72,256]{1,0:T(8,128)S(1)} %collective-permute-done.1.east_row, f32[14,64,256]{2,1,0:T(8,128)S(1)} %get-tuple-element.35.near, f32[14,64,256]{2,1,0:T(8,128)S(1)} %get-tuple-element.36.far, ...), custom_call_target="tpu_custom_call" | custom-call | tf_op jit(solution)/shard_map/pallas_call | solution.py:502
  23.4 0.0 collective-permute-start.5
  23.4 2.9 %collective-permute-done.9 = f32[48,128]{1,0:T(8,128)S(1)} collective-permute-done((f32[48,128]{1,0:T(8,128)S(1)}, f32[48,128]{1,0:T(8,128)S(1)}, u32[]{:S(2)}, u32[]{:S(2)}) %collective-permute-start.9) | collective-permute-done | bytes 24608 | tf_op jit(solution)/shard_map/ppermute | solution.py:614
  26.3 0.0 collective-permute-start.10
  26.3 0.0 collective-permute-done.5.got_low.got_high
  26.3 0.5 %shard_map.91.inner_0 = f32[14,32,256]{2,1,0:T(8,128)S(1)} custom-call(f32[14,64,256]{2,1,0:T(8,128)S(1)} %get-tuple-element.35.near, f32[14,64,256]{2,1,0:T(8,128)S(1)} %get-tuple-element.36.far, f32[6,2,24,128]{3,2,1,0:T(8,128)S(1)} %get-tuple-element.37.coef_near, f32[6,2,24,128]{3,2,1,0:T(8,128)S(1)} %get-tuple-element.38.coef_far, ...), custom_call_target="tpu_custom_call" | custom-call | tf_op jit(solution)/shard_map/pallas_call | solution.py:502
  26.8 0.5 %shard_map.92.inner_1 = f32[14,32,256]{2,1,0:T(8,128)S(1)} custom-call(f32[14,64,256]{2,1,0:T(8,128)S(1)} %get-tuple-element.35.near, f32[14,64,256]{2,1,0:T(8,128)S(1)} %get-tuple-element.36.far, f32[6,2,24,128]{3,2,1,0:T(8,128)S(1)} %get-tuple-element.37.coef_near, f32[6,2,24,128]{3,2,1,0:T(8,128)S(1)} %get-tuple-element.38.coef_far, ...), custom_call_target="tpu_custom_call" | custom-call | tf_op jit(solution)/shard_map/pallas_call | solution.py:502
  27.4 0.0 collective-permute-done.2.far_west
  27.4 0.0 collective-permute-done.3.far_east
  27.4 1.6 %shard_map.93 = f32[64,16,256]{2,1,0:T(8,128)} custom-call(f32[16,64,256]{2,1,0:T(8,128)S(1)} %get-tuple-element.23.sk, f32[16,256]{1,0:T(8,128)S(1)} %get-tuple-element.24.ar, f32[72,256]{1,0:T(8,128)S(1)} %collective-permute-done.west_row, f32[72,256]{1,0:T(8,128)S(1)} %collective-permute-done.1.east_row, f32[72,256]{1,0:T(8,128)S(1)} %collective-permute-done.2.far_west, ...), custom_call_target="tpu_custom_call" | custom-call | tf_op jit(solution)/shard_map/pallas_call | solution.py:502
  29.0 1.9 %collective-permute-done.10.other = f32[48,128]{1,0:T(8,128)S(1)} collective-permute-done((f32[48,128]{1,0:T(8,128)S(1)}, f32[48,128]{1,0:T(8,128)S(1)}, u32[]{:S(2)}, u32[]{:S(2)}) %collective-permute-start.10) | collective-permute-done | bytes 24608 | tf_op jit(solution)/shard_map/ppermute | solution.py:614
  30.9 0.8 %shard_map.94 = f32[96,96]{1,0:T(8,128)} custom-call(f32[48,128]{1,0:T(8,128)S(1)} %add.15.mine, f32[48,128]{1,0:T(8,128)S(1)} %collective-permute-done.10.other), custom_call_target="tpu_custom_call" | custom-call | tf_op jit(solution)/shard_map/pallas_call | solution.py:502
  (5 shorter events, 0.0 us)
Async XLA Ops:
  2.3 7.2 %collective-permute-start.4 = (f32[17,64,128]{2,1,0:T(8,128)S(1)}, f32[17,64,128]{2,1,0:T(8,128)S(1)}, u32[]{:S(2)}, u32[]{:S(2)}) collective-permute-start(f32[17,64,128]{2,1,0:T(8,128)S(1)} %get-tuple-element.34), channel_id=1, source_target_pairs={{0,1},{1,0},{2,3},{3,2},{4,5},{5,4},{6,7},{7,6},{8,9},{9,8},{10,11... | collective-permute-start | bytes 1671176 | tf_op jit(solution)/shard_map/ppermute | solution.py:532
  2.8 9.4 %collective-permute-start = (f32[72,256]{1,0:T(8,128)S(1)}, f32[72,256]{1,0:T(8,128)S(1)}, u32[]{:S(2)}, u32[]{:S(2)}) collective-permute-start(f32[72,256]{1,0:T(8,128)S(1)} %get-tuple-element.25), channel_id=1, source_target_pairs={{0,2},{2,4},{4,6},{6,8},{8,10},{10,12},{12,14},{14,16},{16,18},{18... | collective-permute-start | bytes 221192 | tf_op jit(solution)/shard_map/ppermute | solution.py:563
  5.4 6.9 %collective-permute-start.1 = (f32[72,256]{1,0:T(8,128)S(1)}, f32[72,256]{1,0:T(8,128)S(1)}, u32[]{:S(2)}, u32[]{:S(2)}) collective-permute-start(f32[72,256]{1,0:T(8,128)S(1)} %get-tuple-element.26), channel_id=1, source_target_pairs={{2,0},{4,2},{6,4},{8,6},{10,8},{12,10},{14,12},{16,14},{18,16},{20... | collective-permute-start | bytes 221192 | tf_op jit(solution)/shard_map/ppermute | solution.py:564
  12.9 1.3 %collective-permute-start.6 = (f32[48,128]{1,0:T(8,128)S(1)}, f32[48,128]{1,0:T(8,128)S(1)}, u32[]{:S(2)}, u32[]{:S(2)}) collective-permute-start(f32[48,128]{1,0:T(8,128)S(1)} %get-tuple-element.43), channel_id=1, source_target_pairs={{0,1},{1,0},{2,3},{3,2},{4,5},{5,4},{6,7},{7,6},{8,9},{9,8},{10,11... | collective-permute-start | bytes 73736 | tf_op jit(solution)/shard_map/ppermute | solution.py:614
  14.1 3.3 %collective-permute-start.7 = (f32[48,128]{1,0:T(8,128)S(1)}, f32[48,128]{1,0:T(8,128)S(1)}, u32[]{:S(2)}, u32[]{:S(2)}) collective-permute-start(f32[48,128]{1,0:T(8,128)S(1)} %add.12), channel_id=1, source_target_pairs={{0,5},{1,4},{2,7},{3,6},{4,1},{5,0},{6,3},{7,2},{8,13},{9,12},{10,... | collective-permute-start | bytes 73736 | tf_op jit(solution)/shard_map/ppermute | solution.py:614
  14.1 13.2 %collective-permute-start.2 = (f32[72,256]{1,0:T(8,128)S(1)}, f32[72,256]{1,0:T(8,128)S(1)}, u32[]{:S(2)}, u32[]{:S(2)}) collective-permute-start(f32[72,256]{1,0:T(8,128)S(1)} %get-tuple-element.27), channel_id=1, source_target_pairs={{0,2},{2,4},{4,6},{6,8},{8,10},{10,12},{12,14},{14,16},{16,18},{18... | collective-permute-start | bytes 221192 | tf_op jit(solution)/shard_map/ppermute | solution.py:568
  17.4 5.4 %collective-permute-start.8 = (f32[48,128]{1,0:T(8,128)S(1)}, f32[48,128]{1,0:T(8,128)S(1)}, u32[]{:S(2)}, u32[]{:S(2)}) collective-permute-start(f32[48,128]{1,0:T(8,128)S(1)} %add.13), channel_id=1, source_target_pairs={{0,3},{1,2},{2,1},{3,0},{4,7},{5,6},{6,5},{7,4},{8,11},{9,10},{10,... | collective-permute-start | bytes 73736 | tf_op jit(solution)/shard_map/ppermute | solution.py:614
  17.6 9.7 %collective-permute-start.3 = (f32[72,256]{1,0:T(8,128)S(1)}, f32[72,256]{1,0:T(8,128)S(1)}, u32[]{:S(2)}, u32[]{:S(2)}) collective-permute-start(f32[72,256]{1,0:T(8,128)S(1)} %get-tuple-element.28), channel_id=1, source_target_pairs={{2,0},{4,2},{6,4},{8,6},{10,8},{12,10},{14,12},{16,14},{18,16},{20... | collective-permute-start | bytes 221192 | tf_op jit(solution)/shard_map/ppermute | solution.py:567
  22.8 3.5 %collective-permute-start.9 = (f32[48,128]{1,0:T(8,128)S(1)}, f32[48,128]{1,0:T(8,128)S(1)}, u32[]{:S(2)}, u32[]{:S(2)}) collective-permute-start(f32[48,128]{1,0:T(8,128)S(1)} %add.14), channel_id=1, source_target_pairs={{0,9},{1,8},{2,11},{3,10},{4,13},{5,12},{6,15},{7,14},{8,1},{9,0},... | collective-permute-start | bytes 73736 | tf_op jit(solution)/shard_map/ppermute | solution.py:614
  23.4 2.9 %collective-permute-start.5 = (f32[72,128]{1,0:T(8,128)S(1)}, f32[72,128]{1,0:T(8,128)S(1)}, u32[]{:S(2)}, u32[]{:S(2)}) collective-permute-start(f32[72,128]{1,0:T(8,128)S(1)} %shard_map.90), channel_id=1, source_target_pairs={{0,1},{1,0},{2,3},{3,2},{4,5},{5,4},{6,7},{7,6},{8,9},{9,8},{10,11... | collective-permute-start | bytes 110600 | tf_op jit(solution)/shard_map/ppermute | solution.py:532
  26.3 4.6 %collective-permute-start.10 = (f32[48,128]{1,0:T(8,128)S(1)}, f32[48,128]{1,0:T(8,128)S(1)}, u32[]{:S(2)}, u32[]{:S(2)}) collective-permute-start(f32[48,128]{1,0:T(8,128)S(1)} %add.15.mine), channel_id=1, source_target_pairs={{0,17},{1,16},{2,19},{3,18},{4,21},{5,20},{6,23},{7,22},{8,25},{9,... | collective-permute-start | bytes 73736 | tf_op jit(solution)/shard_map/ppermute | solution.py:614

commit v6 on v5

--- a/solution.py
+++ b/solution.py
@@ -10,6 +10,7 @@
 
 LANES = 128
 BITS = 16
+FOLDS = ((8,), (7,), (6,), (5,), (9, 10, 11))
 F32 = jnp.float32
 
 
@@ -46,6 +47,15 @@
 
 def edge_at(edge, lane, target):
     return pltpu.roll(edge, (target - lane) % LANES, 1)
+
+
+def fold_place(sizes, r, other):
+    start = sizes.cols
+    for before in FOLDS[r]:
+        width = sizes.cols - 8 * before
+        if before == other:
+            return start % LANES, width
+        start += width
 
 
 class Sizes:
@@ -57,7 +67,7 @@
         self.edge_rows = -(-(self.count + 2) // 8) * 8
         self.lat_axis = lax.axis_size("lat")
         self.paired = self.lat_axis == 2
-        self.folded = 4 * self.cols == 3 * LANES and self.cols % 48 == 0
+        self.folded = 4 * self.cols == 3 * LANES
         self.cells = lax.axis_size("lon") * self.lons * self.lat_axis * self.lats
 
 
@@ -125,7 +135,7 @@
 
 
 def far_side():
-    return lax.axis_index("lon") >= 3
+    return lax.axis_index("lon") >= 5
 
 
 def products(split_hi, split_lo):
@@ -309,14 +319,15 @@
     if not sizes.folded:
         gram[...] = total
         return
-    block, short = sizes.cols // 3, sizes.cols // 6
     whole[:, 0 : sizes.cols] = total
-    rows = [whole[k * short : (k + 1) * short, :] for k in range(6)]
-    ids = lane_ids(block)
-    gram[0:block, :] = jnp.where(ids < sizes.cols, whole[0:block, :], pltpu.roll(whole[block : 2 * block, :], 2 * block, 1))
-    ids = lane_ids(short) // block
-    moved = [pltpu.roll(rows[2], 2 * block, 1), pltpu.roll(rows[3], 3 * block, 1), rows[4], pltpu.roll(rows[5], block, 1)]
-    gram[block:, :] = jnp.where(ids == 0, moved[0], jnp.where(ids == 1, moved[1], jnp.where(ids == 2, moved[2], moved[3])))
+    ids = lane_ids(8)
+    for r, parts in enumerate(FOLDS):
+        kept = whole[8 * r : 8 * r + 8, :]
+        for other in parts:
+            start, width = fold_place(sizes, r, other)
+            moved = pltpu.roll(whole[8 * other : 8 * other + 8, :], (start - 8 * other) % LANES, 1)
+            kept = jnp.where((ids - start) % LANES < width, moved, kept)
+        gram[8 * r : 8 * r + 8, :] = kept
 
 
 def unfold_kernel(sizes, mine, other, out):
@@ -324,15 +335,17 @@
     if not sizes.folded:
         out[...] = total
         return
-    block = sizes.cols // 3
-    top, low = total[0:block, :], total[block:, :]
-    ids = lane_ids(block)
-    middle = jnp.concatenate([pltpu.roll(low, 2 * block, 1), pltpu.roll(low, block, 1)], axis=0)
-    second = jnp.where(ids < 2 * block, pltpu.roll(top, 2 * block, 1), middle)
-    third = jnp.concatenate([low, pltpu.roll(low, 3 * block, 1)], axis=0)
-    upper = jnp.concatenate([top, second, third, jnp.zeros((block, LANES), F32)], axis=0)
-    across = lane_ids(LANES) // block
-    down = lax.broadcasted_iota(jnp.int32, (LANES, LANES), 0) // block
+    blocks = {}
+    for r, parts in enumerate(FOLDS):
+        kept = total[8 * r : 8 * r + 8, :]
+        blocks[r] = kept
+        for other in parts:
+            start, _ = fold_place(sizes, r, other)
+            blocks[other] = pltpu.roll(kept, (8 * other - start) % LANES, 1)
+    rows = [blocks[r] for r in sorted(blocks)]
+    upper = jnp.concatenate(rows + [jnp.zeros((LANES - sizes.cols, LANES), F32)], axis=0)
+    across = lane_ids(LANES) // 8
+    down = lax.broadcasted_iota(jnp.int32, (LANES, LANES), 0) // 8
     out[...] = jnp.where(down <= across, upper, upper.T)[0 : sizes.cols, 0 : sizes.cols]
 
 
@@ -584,7 +597,7 @@
     gram, ends, end_coef = call(
         gram_kernel,
         sizes,
-        [(sizes.cols // 2, LANES) if sizes.folded else (sizes.cols, sizes.cols), (2, count, lats), (5, lats // LANES, 16, LANES)],
+        [(8 * len(FOLDS), LANES) if sizes.folded else (sizes.cols, sizes.cols), (2, count, lats), (5, lats // LANES, 16, LANES)],
         (sketch, probe_bits, ocean, east_cond, kappa_sq, inv_area, west_row, east_row, low, high)
         + (coef_near, coef_far, partial_near, partial_far),
         split(2) + [pltpu.VMEM((sizes.cols, LANES), F32)],

time: 31.8 us -> 31.6 us (level)
  starting transfers between devices: 14.7 us -> 13.6 us
  waiting for transfers between devices: 8.12 us -> 9.05 us
    ppermute x1, starting transfers between devices: 5.13 us -> 3.64 us  [local(): far_east = lax.ppermute(far_to_west, 'lon', westward)]
    ppermute x5, waiting for transfers between devices: 7.17 us -> 8.11 us  [local(): other = lax.ppermute(gram, ('lon', 'lat'), pairs)]
    ppermute x5, starting transfers between devices: 0.39 us -> 0.72 us  [local(): other = lax.ppermute(gram, ('lon', 'lat'), pairs)]
where the time goes in v6:
time: 31.6 us; the launch traced here: 31.4 us
  starting transfers between devices  13.6 us (43%)
  waiting for transfers between devices  9.05 us (29%)
  Pallas kernels  8.02 us (25%)
  between operations  0.73 us (2%)
    ppermute x5, waiting for transfers between devices, local(): other = lax.ppermute(gram, ('lon', 'lat'), pairs)  8.11 us
    pallas_call x9, Pallas kernels, call(): pl.pallas_call(functools.partial(kernel, sizes), out_shape=outs, in_specs...  8.02 us
    ppermute x1, starting transfers between devices, local(): east_row = lax.ppermute(to_west, 'lon', westward)  4.06 us
    ppermute x1, starting transfers between devices, local(): far_east = lax.ppermute(far_to_west, 'lon', westward)  3.64 us
    ppermute x1, starting transfers between devices, local(): west_row = lax.ppermute(to_east, 'lon', eastward)  2.54 us
    ppermute x1, starting transfers between devices, local(): far_west = lax.ppermute(far_to_east, 'lon', eastward)  2.03 us
    ppermute x1, waiting for transfers between devices, local(): west_row = lax.ppermute(to_east, 'lon', eastward)  0.93 us
    ppermute x5, starting transfers between devices, local(): other = lax.ppermute(gram, ('lon', 'lat'), pairs)  0.72 us
  transfers between devices with their start and end apart: 11, of which 5 were waited for; matrix products, arithmetic and copies ran while one was open for 0% of the time, Pallas kernels for 16%

profile of v6, /device:TPU:0, one launch (start us, length us, event | category | flops | bytes accessed | tf_op | source)
XLA Modules:
  0.0 31.4 jit_solution(11958700188512889587)
XLA Ops:
  0.6 1.6 %shard_map.86 = (f32[16,64,256]{2,1,0:T(8,128)S(1)}, s32[2,16,256]{2,1,0:T(8,128)S(1)}, s32[16,256]{1,0:T(8,128)S(1)}, f32[16,256]{1,0:T(8,128)S(1)}, f32[16,256...) custom-call(f32[64,16,256]{2,1,0:T(8,128)} %refs_0_.1, ...), custom_call_target="tpu_custom_call" | custom-call | tf_op jit(solution)/shard_map/pallas_call | solution.py:515
  2.3 0.6 %collective-permute-start.4 = (f32[17,64,128]{2,1,0:T(8,128)S(1)}, f32[17,64,128]{2,1,0:T(8,128)S(1)}, u32[]{:S(2)}, u32[]{:S(2)}) collective-permute-start(f32[17,64,128]{2,1,0:T(8,128)S(1)} %get-tuple-element.34), channel_id=1, source_target_pairs={{0,1},{1,0},{2,3},{3,2},{4,5},{5,4},{6,7},{7,6},{8,9},{9,8},{10,11... | collective-permute-start | bytes 1671176 | tf_op jit(solution)/shard_map/ppermute | solution.py:545
  2.8 2.5 %collective-permute-start = (f32[72,256]{1,0:T(8,128)S(1)}, f32[72,256]{1,0:T(8,128)S(1)}, u32[]{:S(2)}, u32[]{:S(2)}) collective-permute-start(f32[72,256]{1,0:T(8,128)S(1)} %get-tuple-element.25), channel_id=1, source_target_pairs={{0,2},{2,4},{4,6},{6,8},{8,10},{10,12},{12,14},{14,16},{16,18},{18... | collective-permute-start | bytes 221192 | tf_op jit(solution)/shard_map/ppermute | solution.py:576
  5.4 4.1 %collective-permute-start.1 = (f32[72,256]{1,0:T(8,128)S(1)}, f32[72,256]{1,0:T(8,128)S(1)}, u32[]{:S(2)}, u32[]{:S(2)}) collective-permute-start(f32[72,256]{1,0:T(8,128)S(1)} %get-tuple-element.26), channel_id=1, source_target_pairs={{2,0},{4,2},{6,4},{8,6},{10,8},{12,10},{14,12},{16,14},{18,16},{20... | collective-permute-start | bytes 221192 | tf_op jit(solution)/shard_map/ppermute | solution.py:577
  9.4 0.0 collective-permute-done.4.got_low.got_high
  9.4 1.9 %shard_map.87 = (f32[14,64,256]{2,1,0:T(8,128)S(1)}, f32[6,2,24,128]{3,2,1,0:T(8,128)S(1)}, f32[96,96]{1,0:T(8,128)S(1)}) custom-call(f32[16,64,256]{2,1,0:T(8,128)S(1)} %get-tuple-element.23.sk, s32[2,16,256]{2,1,0:T(8,128)S(1)} %get-tuple-element.29.wd, s32[16,256]{1,0:T(8,128)S(1)} %get-tuple-element.30.oc, f32[16,256]{1,0:T(8,128)S(1)} %get-tuple-element.31.ea, ...), custom_call_target="tpu_custom_call" | custom-call | tf_op jit(solution)/shard_map/pallas_call | solution.py:515
  11.3 0.9 %collective-permute-done.west_row = f32[72,256]{1,0:T(8,128)S(1)} collective-permute-done((f32[72,256]{1,0:T(8,128)S(1)}, f32[72,256]{1,0:T(8,128)S(1)}, u32[]{:S(2)}, u32[]{:S(2)}) %collective-permute-start) | collective-permute-done | bytes 73760 | tf_op jit(solution)/shard_map/ppermute | solution.py:576
  12.3 0.0 collective-permute-done.1.east_row
  12.3 0.6 %shard_map.89 = (f32[40,128]{1,0:T(8,128)S(1)}, f32[2,64,256]{2,1,0:T(8,128)S(1)}, f32[5,2,16,128]{3,2,1,0:T(8,128)S(1)}) custom-call(f32[16,64,256]{2,1,0:T(8,128)S(1)} %get-tuple-element.23.sk, s32[2,16,256]{2,1,0:T(8,128)S(1)} %get-tuple-element.29.wd, s32[16,256]{1,0:T(8,128)S(1)} %get-tuple-element.30.oc, f32[16,256]{1,0:T(8,128)S(1)} %get-tuple-element.31.ea, ...), custom_call_target="tpu_custom_call" | custom-call | tf_op jit(solution)/shard_map/pallas_call | solution.py:515
  12.9 0.1 collective-permute-start.6
  12.9 1.2 %collective-permute-done.6 = f32[40,128]{1,0:T(8,128)S(1)} collective-permute-done((f32[40,128]{1,0:T(8,128)S(1)}, f32[40,128]{1,0:T(8,128)S(1)}, u32[]{:S(2)}, u32[]{:S(2)}) %collective-permute-start.6) | collective-permute-done | bytes 20512 | tf_op jit(solution)/shard_map/ppermute | solution.py:627
  14.1 0.0 collective-permute-start.7
  14.1 2.0 %collective-permute-start.2 = (f32[72,256]{1,0:T(8,128)S(1)}, f32[72,256]{1,0:T(8,128)S(1)}, u32[]{:S(2)}, u32[]{:S(2)}) collective-permute-start(f32[72,256]{1,0:T(8,128)S(1)} %get-tuple-element.27), channel_id=1, source_target_pairs={{0,2},{2,4},{4,6},{6,8},{8,10},{10,12},{12,14},{14,16},{16,18},{18... | collective-permute-start | bytes 221192 | tf_op jit(solution)/shard_map/ppermute | solution.py:581
  16.1 3.6 %collective-permute-start.3 = (f32[72,256]{1,0:T(8,128)S(1)}, f32[72,256]{1,0:T(8,128)S(1)}, u32[]{:S(2)}, u32[]{:S(2)}) collective-permute-start(f32[72,256]{1,0:T(8,128)S(1)} %get-tuple-element.28), channel_id=1, source_target_pairs={{2,0},{4,2},{6,4},{8,6},{10,8},{12,10},{14,12},{16,14},{18,16},{20... | collective-permute-start | bytes 221192 | tf_op jit(solution)/shard_map/ppermute | solution.py:580
  19.8 0.0 collective-permute-done.7
  19.8 0.1 collective-permute-start.8
  19.9 3.2 %collective-permute-done.8 = f32[40,128]{1,0:T(8,128)S(1)} collective-permute-done((f32[40,128]{1,0:T(8,128)S(1)}, f32[40,128]{1,0:T(8,128)S(1)}, u32[]{:S(2)}, u32[]{:S(2)}) %collective-permute-start.8) | collective-permute-done | bytes 20512 | tf_op jit(solution)/shard_map/ppermute | solution.py:627
  23.1 0.0 collective-permute-start.9
  23.1 0.5 %shard_map.90 = f32[72,128]{1,0:T(8,128)S(1)} custom-call(f32[16,256]{1,0:T(8,128)S(1)} %get-tuple-element.24.ar, f32[72,256]{1,0:T(8,128)S(1)} %collective-permute-done.west_row, f32[72,256]{1,0:T(8,128)S(1)} %collective-permute-done.1.east_row, f32[14,64,256]{2,1,0:T(8,128)S(1)} %get-tuple-element.35.near, f32[14,64,256]{2,1,0:T(8,128)S(1)} %get-tuple-element.36.far, ...), custom_call_target="tpu_custom_call" | custom-call | tf_op jit(solution)/shard_map/pallas_call | solution.py:515
  23.6 0.0 collective-permute-start.5
  23.6 2.6 %collective-permute-done.9 = f32[40,128]{1,0:T(8,128)S(1)} collective-permute-done((f32[40,128]{1,0:T(8,128)S(1)}, f32[40,128]{1,0:T(8,128)S(1)}, u32[]{:S(2)}, u32[]{:S(2)}) %collective-permute-start.9) | collective-permute-done | bytes 20512 | tf_op jit(solution)/shard_map/ppermute | solution.py:627
  26.3 0.6 %collective-permute-start.10 = (f32[40,128]{1,0:T(8,128)S(1)}, f32[40,128]{1,0:T(8,128)S(1)}, u32[]{:S(2)}, u32[]{:S(2)}) collective-permute-start(f32[40,128]{1,0:T(8,128)S(1)} %add.15.mine), channel_id=1, source_target_pairs={{0,17},{1,16},{2,19},{3,18},{4,21},{5,20},{6,23},{7,22},{8,25},{9,... | collective-permute-start | bytes 61448 | tf_op jit(solution)/shard_map/ppermute | solution.py:627
  26.9 0.0 collective-permute-done.5.got_low.got_high
  26.9 0.5 %shard_map.91.inner_0 = f32[14,32,256]{2,1,0:T(8,128)S(1)} custom-call(f32[14,64,256]{2,1,0:T(8,128)S(1)} %get-tuple-element.35.near, f32[14,64,256]{2,1,0:T(8,128)S(1)} %get-tuple-element.36.far, f32[6,2,24,128]{3,2,1,0:T(8,128)S(1)} %get-tuple-element.37.coef_near, f32[6,2,24,128]{3,2,1,0:T(8,128)S(1)} %get-tuple-element.38.coef_far, ...), custom_call_target="tpu_custom_call" | custom-call | tf_op jit(solution)/shard_map/pallas_call | solution.py:515
  27.4 0.5 %shard_map.92.inner_1 = f32[14,32,256]{2,1,0:T(8,128)S(1)} custom-call(f32[14,64,256]{2,1,0:T(8,128)S(1)} %get-tuple-element.35.near, f32[14,64,256]{2,1,0:T(8,128)S(1)} %get-tuple-element.36.far, f32[6,2,24,128]{3,2,1,0:T(8,128)S(1)} %get-tuple-element.37.coef_near, f32[6,2,24,128]{3,2,1,0:T(8,128)S(1)} %get-tuple-element.38.coef_far, ...), custom_call_target="tpu_custom_call" | custom-call | tf_op jit(solution)/shard_map/pallas_call | solution.py:515
  27.9 0.0 collective-permute-done.2.far_west
  27.9 0.0 collective-permute-done.3.far_east
  27.9 1.6 %shard_map.93 = f32[64,16,256]{2,1,0:T(8,128)} custom-call(f32[16,64,256]{2,1,0:T(8,128)S(1)} %get-tuple-element.23.sk, f32[16,256]{1,0:T(8,128)S(1)} %get-tuple-element.24.ar, f32[72,256]{1,0:T(8,128)S(1)} %collective-permute-done.west_row, f32[72,256]{1,0:T(8,128)S(1)} %collective-permute-done.1.east_row, f32[72,256]{1,0:T(8,128)S(1)} %collective-permute-done.2.far_west, ...), custom_call_target="tpu_custom_call" | custom-call | tf_op jit(solution)/shard_map/pallas_call | solution.py:515
  29.5 1.1 %collective-permute-done.10.other = f32[40,128]{1,0:T(8,128)S(1)} collective-permute-done((f32[40,128]{1,0:T(8,128)S(1)}, f32[40,128]{1,0:T(8,128)S(1)}, u32[]{:S(2)}, u32[]{:S(2)}) %collective-permute-start.10) | collective-permute-done | bytes 20512 | tf_op jit(solution)/shard_map/ppermute | solution.py:627
  30.6 0.8 %shard_map.94 = f32[96,96]{1,0:T(8,128)} custom-call(f32[40,128]{1,0:T(8,128)S(1)} %add.15.mine, f32[40,128]{1,0:T(8,128)S(1)} %collective-permute-done.10.other), custom_call_target="tpu_custom_call" | custom-call | tf_op jit(solution)/shard_map/pallas_call | solution.py:515
  (5 shorter events, 0.0 us)
Async XLA Ops:
  2.3 7.2 %collective-permute-start.4 = (f32[17,64,128]{2,1,0:T(8,128)S(1)}, f32[17,64,128]{2,1,0:T(8,128)S(1)}, u32[]{:S(2)}, u32[]{:S(2)}) collective-permute-start(f32[17,64,128]{2,1,0:T(8,128)S(1)} %get-tuple-element.34), channel_id=1, source_target_pairs={{0,1},{1,0},{2,3},{3,2},{4,5},{5,4},{6,7},{7,6},{8,9},{9,8},{10,11... | collective-permute-start | bytes 1671176 | tf_op jit(solution)/shard_map/ppermute | solution.py:545
  2.8 9.4 %collective-permute-start = (f32[72,256]{1,0:T(8,128)S(1)}, f32[72,256]{1,0:T(8,128)S(1)}, u32[]{:S(2)}, u32[]{:S(2)}) collective-permute-start(f32[72,256]{1,0:T(8,128)S(1)} %get-tuple-element.25), channel_id=1, source_target_pairs={{0,2},{2,4},{4,6},{6,8},{8,10},{10,12},{12,14},{14,16},{16,18},{18... | collective-permute-start | bytes 221192 | tf_op jit(solution)/shard_map/ppermute | solution.py:576
  5.4 6.9 %collective-permute-start.1 = (f32[72,256]{1,0:T(8,128)S(1)}, f32[72,256]{1,0:T(8,128)S(1)}, u32[]{:S(2)}, u32[]{:S(2)}) collective-permute-start(f32[72,256]{1,0:T(8,128)S(1)} %get-tuple-element.26), channel_id=1, source_target_pairs={{2,0},{4,2},{6,4},{8,6},{10,8},{12,10},{14,12},{16,14},{18,16},{20... | collective-permute-start | bytes 221192 | tf_op jit(solution)/shard_map/ppermute | solution.py:577
  12.9 1.3 %collective-permute-start.6 = (f32[40,128]{1,0:T(8,128)S(1)}, f32[40,128]{1,0:T(8,128)S(1)}, u32[]{:S(2)}, u32[]{:S(2)}) collective-permute-start(f32[40,128]{1,0:T(8,128)S(1)} %get-tuple-element.43), channel_id=1, source_target_pairs={{0,1},{1,0},{2,3},{3,2},{4,5},{5,4},{6,7},{7,6},{8,9},{9,8},{10,11... | collective-permute-start | bytes 61448 | tf_op jit(solution)/shard_map/ppermute | solution.py:627
  14.1 5.7 %collective-permute-start.7 = (f32[40,128]{1,0:T(8,128)S(1)}, f32[40,128]{1,0:T(8,128)S(1)}, u32[]{:S(2)}, u32[]{:S(2)}) collective-permute-start(f32[40,128]{1,0:T(8,128)S(1)} %add.12), channel_id=1, source_target_pairs={{0,5},{1,4},{2,7},{3,6},{4,1},{5,0},{6,3},{7,2},{8,13},{9,12},{10,... | collective-permute-start | bytes 61448 | tf_op jit(solution)/shard_map/ppermute | solution.py:627
  14.1 13.8 %collective-permute-start.2 = (f32[72,256]{1,0:T(8,128)S(1)}, f32[72,256]{1,0:T(8,128)S(1)}, u32[]{:S(2)}, u32[]{:S(2)}) collective-permute-start(f32[72,256]{1,0:T(8,128)S(1)} %get-tuple-element.27), channel_id=1, source_target_pairs={{0,2},{2,4},{4,6},{6,8},{8,10},{10,12},{12,14},{14,16},{16,18},{18... | collective-permute-start | bytes 221192 | tf_op jit(solution)/shard_map/ppermute | solution.py:581
  16.1 11.8 %collective-permute-start.3 = (f32[72,256]{1,0:T(8,128)S(1)}, f32[72,256]{1,0:T(8,128)S(1)}, u32[]{:S(2)}, u32[]{:S(2)}) collective-permute-start(f32[72,256]{1,0:T(8,128)S(1)} %get-tuple-element.28), channel_id=1, source_target_pairs={{2,0},{4,2},{6,4},{8,6},{10,8},{12,10},{14,12},{16,14},{18,16},{20... | collective-permute-start | bytes 221192 | tf_op jit(solution)/shard_map/ppermute | solution.py:580
  19.8 3.3 %collective-permute-start.8 = (f32[40,128]{1,0:T(8,128)S(1)}, f32[40,128]{1,0:T(8,128)S(1)}, u32[]{:S(2)}, u32[]{:S(2)}) collective-permute-start(f32[40,128]{1,0:T(8,128)S(1)} %add.13), channel_id=1, source_target_pairs={{0,3},{1,2},{2,1},{3,0},{4,7},{5,6},{6,5},{7,4},{8,11},{9,10},{10,... | collective-permute-start | bytes 61448 | tf_op jit(solution)/shard_map/ppermute | solution.py:627
  23.1 3.2 %collective-permute-start.9 = (f32[40,128]{1,0:T(8,128)S(1)}, f32[40,128]{1,0:T(8,128)S(1)}, u32[]{:S(2)}, u32[]{:S(2)}) collective-permute-start(f32[40,128]{1,0:T(8,128)S(1)} %add.14), channel_id=1, source_target_pairs={{0,9},{1,8},{2,11},{3,10},{4,13},{5,12},{6,15},{7,14},{8,1},{9,0},... | collective-permute-start | bytes 61448 | tf_op jit(solution)/shard_map/ppermute | solution.py:627
  23.6 3.2 %collective-permute-start.5 = (f32[72,128]{1,0:T(8,128)S(1)}, f32[72,128]{1,0:T(8,128)S(1)}, u32[]{:S(2)}, u32[]{:S(2)}) collective-permute-start(f32[72,128]{1,0:T(8,128)S(1)} %shard_map.90), channel_id=1, source_target_pairs={{0,1},{1,0},{2,3},{3,2},{4,5},{5,4},{6,7},{7,6},{8,9},{9,8},{10,11... | collective-permute-start | bytes 110600 | tf_op jit(solution)/shard_map/ppermute | solution.py:545
  26.3 4.3 %collective-permute-start.10 = (f32[40,128]{1,0:T(8,128)S(1)}, f32[40,128]{1,0:T(8,128)S(1)}, u32[]{:S(2)}, u32[]{:S(2)}) collective-permute-start(f32[40,128]{1,0:T(8,128)S(1)} %add.15.mine), channel_id=1, source_target_pairs={{0,17},{1,16},{2,19},{3,18},{4,21},{5,20},{6,23},{7,22},{8,25},{9,... | collective-permute-start | bytes 61448 | tf_op jit(solution)/shard_map/ppermute | solution.py:627

commit v7 on v6

--- a/solution.py
+++ b/solution.py
@@ -213,13 +213,12 @@
         _, flow_south = lat_shifts(half_north, edge_low, edge_high)
         north_w = jnp.concatenate([a * b for a, b in zip(half_north, sea_north)], axis=1)
         south_w = jnp.concatenate([a * b for a, b in zip(flow_south, sea_parts)], axis=1)
-        put_row(coef, (0,), slice(0, n), sea * (ka[...] + east_w + west_w + north_w + south_w))
-        put_row(coef, (1,), slice(0, n), east_w)
-        put_row(coef, (2,), slice(0, n), west_w)
-        put_row(coef, (3,), slice(0, n), north_w)
-        put_row(coef, (4,), slice(0, n), south_w)
-        put_row(coef, (5,), slice(0, n), ar[...])
-        put_row(root, (), slice(0, n), jnp.sqrt(ar[...]))
+        rooted = jnp.sqrt(ar[...])
+        center = sea * (ka[...] + east_w + west_w + north_w + south_w)
+        for k, field in enumerate((center, east_w, west_w, north_w, south_w)):
+            put_row(coef, (k,), slice(0, n), field)
+            put_row(root, (k,), slice(0, n), field * rooted)
+        put_row(coef, (5,), slice(0, n), rooted)
 
         def one_block(start, get, edges, keep):
             rows = pl.ds(start, BITS)
@@ -227,13 +226,13 @@
             for i in range(1, n - 1):
                 east = get(i + 1)
                 north, south = lat_shifts(middle, *edges(i))
-                weights, scale = rows_of(coef, i), spread_row(root, (), i)
+                weights = rows_of(root, i)
                 for h, part in enumerate(stencil(weights, middle, east, west, north, south)):
                     here = slice(h * LANES, (h + 1) * LANES)
                     if keep:
                         applied[i - 1, rows, here] = part
                     at = slice((i - 1) * lats + h * LANES, (i - 1) * lats + (h + 1) * LANES)
-                    store_split(split_hi, split_lo, rows, at, part * scale[h])
+                    store_split(split_hi, split_lo, rows, at, part)
                 west, middle = middle, east
 
         def sketch_block(k, carry):
@@ -265,7 +264,6 @@
     def inner(k, i):
         return lax.select(far, get_row(coef_far, (k,), i), get_row(coef_near, (k,), i))
 
-    root = []
     for side, i in enumerate((0, n - 1)):
         sea = oc[i : i + 1, :].astype(F32)
         east_w, west_w, north_w, south_w = (inner(k, i) for k in range(1, 5))
@@ -276,20 +274,20 @@
         center = sea * (ka[i : i + 1, :] + east_w + west_w + north_w + south_w)
         for k, row in enumerate((center, east_w, west_w, north_w, south_w)):
             put_row(end_coef, (k,), slice(side, side + 1), row)
-        root.append(jnp.sqrt(ar[i : i + 1, :]))
+            put_row(end_coef, (k,), slice(8 + side, 9 + side), row * jnp.sqrt(ar[i : i + 1, :]))
 
     def one_block(start, get, edges, keep):
         rows = pl.ds(start, BITS)
         for side, i in enumerate((0, n - 1)):
             middle = get(i)
             north, south = lat_shifts(middle, *edges(i))
-            weights = rows_of(end_coef, side)
+            weights = rows_of(end_coef, 8 + side)
             for h, part in enumerate(stencil(weights, middle, get(i + 1), get(i - 1), north, south)):
                 here = slice(h * LANES, (h + 1) * LANES)
                 if keep:
                     ends[side, rows, here] = part
                 at = slice(side * lats + h * LANES, side * lats + (h + 1) * LANES)
-                store_split(split_hi, split_lo, rows, at, part * root[side][:, here])
+                store_split(split_hi, split_lo, rows, at, part)
 
     for start in range(0, count, BITS):
         rows = slice(start, start + BITS)
@@ -352,6 +350,7 @@
 def edge_kernel(sizes, ar, west_row, east_row, near, far, ends, *edges):
     n, count, lats = sizes.lons, sizes.count, sizes.lats
     last = lats - LANES
+    rooted = jnp.sqrt(ar[...])
     base = count + sizes.words
 
     def fill(applied):
@@ -369,7 +368,7 @@
                         low, high = applied[i - 1, rows, 0:LANES], applied[i - 1, rows, last:]
                     else:
                         low, high = ends[min(i, 1), rows, 0:LANES], ends[min(i, 1), rows, last:]
-                    low, high = low * ar[i : i + 1, 0:LANES], high * ar[i : i + 1, last:]
+                    low, high = low * rooted[i : i + 1, 0:LANES], high * rooted[i : i + 1, last:]
                 moved = edge_rows_of(sizes, low, high, i)
                 total = [jnp.where(ids == i, m, t) for m, t in zip(moved, total)]
             for edge, t in zip(edges, total):
@@ -489,10 +488,10 @@
                 edge_at(high_edge, n + side, LANES - 1),
             )
             outer = stencil(ghost[side], middle, east, west, north, south)
-            middle = halves(ends[side, rows, :] * ar[i : i + 1, :])
+            middle = halves(ends[side, rows, :] * jnp.sqrt(ar[i : i + 1, :]))
             next_in = 1 if side == 0 else n - 2
             inward = lax.select(far_lon, far[next_in - 1, rows, :], near[next_in - 1, rows, :])
-            inward = halves(inward * ar[next_in : next_in + 1, :])
+            inward = halves(inward * jnp.sqrt(ar[next_in : next_in + 1, :]))
             east, west = (inward, outer) if side == 0 else (outer, inward)
             north, south = lat_shifts(
                 middle, edge_at(low_edge, i, 0), edge_at(high_edge, i, LANES - 1)
@@ -589,7 +588,7 @@
             sizes,
             [(n - 2, count, lats), (6, lats // LANES, n + 8, LANES), (sizes.cols, sizes.cols)],
             fields + (low, high),
-            split(n - 2) + [pltpu.VMEM((2, n + 16, lats), F32), pltpu.VMEM((lats // LANES, n + 8, LANES), F32)],
+            split(n - 2) + [pltpu.VMEM((2, n + 16, lats), F32), pltpu.VMEM((5, lats // LANES, n + 8, LANES), F32)],
         )
         for far in (False, True)
     ]
@@ -597,7 +596,7 @@
     gram, ends, end_coef = call(
         gram_kernel,
         sizes,
-        [(8 * len(FOLDS), LANES) if sizes.folded else (sizes.cols, sizes.cols), (2, count, lats), (5, lats // LANES, 16, LANES)],
+        [(8 * len(FOLDS), LANES) if sizes.folded else (sizes.cols, sizes.cols), (2, count, lats), (5, lats // LANES, 24, LANES)],
         (sketch, probe_bits, ocean, east_cond, kappa_sq, inv_area, west_row, east_row, low, high)
         + (coef_near, coef_far, partial_near, partial_far),
         split(2) + [pltpu.VMEM((sizes.cols, LANES), F32)],

time: 31.6 us -> 31.6 us (level)
  no operation moved by 1% of the time
where the time goes in v7:
time: 31.6 us; the launch traced here: 31.4 us
  starting transfers between devices  13.6 us (43%)
  waiting for transfers between devices  9.09 us (29%)
  Pallas kernels  7.97 us (25%)
  between operations  0.73 us (2%)
    ppermute x5, waiting for transfers between devices, local(): other = lax.ppermute(gram, ('lon', 'lat'), pairs)  8.13 us
    pallas_call x9, Pallas kernels, call(): pl.pallas_call(functools.partial(kernel, sizes), out_shape=outs, in_specs...  7.97 us
    ppermute x1, starting transfers between devices, local(): east_row = lax.ppermute(to_west, 'lon', westward)  4.06 us
    ppermute x1, starting transfers between devices, local(): far_east = lax.ppermute(far_to_west, 'lon', westward)  3.64 us
    ppermute x1, starting transfers between devices, local(): west_row = lax.ppermute(to_east, 'lon', eastward)  2.54 us
    ppermute x1, starting transfers between devices, local(): far_west = lax.ppermute(far_to_east, 'lon', eastward)  2.03 us
    ppermute x1, waiting for transfers between devices, local(): west_row = lax.ppermute(to_east, 'lon', eastward)  0.96 us
    ppermute x5, starting transfers between devices, local(): other = lax.ppermute(gram, ('lon', 'lat'), pairs)  0.72 us
  transfers between devices with their start and end apart: 11, of which 5 were waited for; matrix products, arithmetic and copies ran while one was open for 0% of the time, Pallas kernels for 16%

profile of v7, /device:TPU:0, one launch (start us, length us, event | category | flops | bytes accessed | tf_op | source)
XLA Modules:
  0.0 31.4 jit_solution(4367383574503889175)
XLA Ops:
  0.6 1.6 %shard_map.86 = (f32[16,64,256]{2,1,0:T(8,128)S(1)}, s32[2,16,256]{2,1,0:T(8,128)S(1)}, s32[16,256]{1,0:T(8,128)S(1)}, f32[16,256]{1,0:T(8,128)S(1)}, f32[16,256...) custom-call(f32[64,16,256]{2,1,0:T(8,128)} %refs_0_.1, ...), custom_call_target="tpu_custom_call" | custom-call | tf_op jit(solution)/shard_map/pallas_call | solution.py:514
  2.3 0.6 %collective-permute-start.4 = (f32[17,64,128]{2,1,0:T(8,128)S(1)}, f32[17,64,128]{2,1,0:T(8,128)S(1)}, u32[]{:S(2)}, u32[]{:S(2)}) collective-permute-start(f32[17,64,128]{2,1,0:T(8,128)S(1)} %get-tuple-element.34), channel_id=1, source_target_pairs={{0,1},{1,0},{2,3},{3,2},{4,5},{5,4},{6,7},{7,6},{8,9},{9,8},{10,11... | collective-permute-start | bytes 1671176 | tf_op jit(solution)/shard_map/ppermute | solution.py:544
  2.8 2.5 %collective-permute-start = (f32[72,256]{1,0:T(8,128)S(1)}, f32[72,256]{1,0:T(8,128)S(1)}, u32[]{:S(2)}, u32[]{:S(2)}) collective-permute-start(f32[72,256]{1,0:T(8,128)S(1)} %get-tuple-element.25), channel_id=1, source_target_pairs={{0,2},{2,4},{4,6},{6,8},{8,10},{10,12},{12,14},{14,16},{16,18},{18... | collective-permute-start | bytes 221192 | tf_op jit(solution)/shard_map/ppermute | solution.py:575
  5.4 4.1 %collective-permute-start.1 = (f32[72,256]{1,0:T(8,128)S(1)}, f32[72,256]{1,0:T(8,128)S(1)}, u32[]{:S(2)}, u32[]{:S(2)}) collective-permute-start(f32[72,256]{1,0:T(8,128)S(1)} %get-tuple-element.26), channel_id=1, source_target_pairs={{2,0},{4,2},{6,4},{8,6},{10,8},{12,10},{14,12},{16,14},{18,16},{20... | collective-permute-start | bytes 221192 | tf_op jit(solution)/shard_map/ppermute | solution.py:576
  9.4 0.0 collective-permute-done.4.got_low.got_high
  9.4 1.8 %shard_map.87 = (f32[14,64,256]{2,1,0:T(8,128)S(1)}, f32[6,2,24,128]{3,2,1,0:T(8,128)S(1)}, f32[96,96]{1,0:T(8,128)S(1)}) custom-call(f32[16,64,256]{2,1,0:T(8,128)S(1)} %get-tuple-element.23.sk, s32[2,16,256]{2,1,0:T(8,128)S(1)} %get-tuple-element.29.wd, s32[16,256]{1,0:T(8,128)S(1)} %get-tuple-element.30.oc, f32[16,256]{1,0:T(8,128)S(1)} %get-tuple-element.31.ea, ...), custom_call_target="tpu_custom_call" | custom-call | tf_op jit(solution)/shard_map/pallas_call | solution.py:514
  11.3 1.0 %collective-permute-done.west_row = f32[72,256]{1,0:T(8,128)S(1)} collective-permute-done((f32[72,256]{1,0:T(8,128)S(1)}, f32[72,256]{1,0:T(8,128)S(1)}, u32[]{:S(2)}, u32[]{:S(2)}) %collective-permute-start) | collective-permute-done | bytes 73760 | tf_op jit(solution)/shard_map/ppermute | solution.py:575
  12.3 0.0 collective-permute-done.1.east_row
  12.3 0.6 %shard_map.89 = (f32[40,128]{1,0:T(8,128)S(1)}, f32[2,64,256]{2,1,0:T(8,128)S(1)}, f32[5,2,24,128]{3,2,1,0:T(8,128)S(1)}) custom-call(f32[16,64,256]{2,1,0:T(8,128)S(1)} %get-tuple-element.23.sk, s32[2,16,256]{2,1,0:T(8,128)S(1)} %get-tuple-element.29.wd, s32[16,256]{1,0:T(8,128)S(1)} %get-tuple-element.30.oc, f32[16,256]{1,0:T(8,128)S(1)} %get-tuple-element.31.ea, ...), custom_call_target="tpu_custom_call" | custom-call | tf_op jit(solution)/shard_map/pallas_call | solution.py:514
  12.9 0.1 collective-permute-start.6
  12.9 1.2 %collective-permute-done.6 = f32[40,128]{1,0:T(8,128)S(1)} collective-permute-done((f32[40,128]{1,0:T(8,128)S(1)}, f32[40,128]{1,0:T(8,128)S(1)}, u32[]{:S(2)}, u32[]{:S(2)}) %collective-permute-start.6) | collective-permute-done | bytes 20512 | tf_op jit(solution)/shard_map/ppermute | solution.py:626
  14.1 0.0 collective-permute-start.7
  14.1 2.0 %collective-permute-start.2 = (f32[72,256]{1,0:T(8,128)S(1)}, f32[72,256]{1,0:T(8,128)S(1)}, u32[]{:S(2)}, u32[]{:S(2)}) collective-permute-start(f32[72,256]{1,0:T(8,128)S(1)} %get-tuple-element.27), channel_id=1, source_target_pairs={{0,2},{2,4},{4,6},{6,8},{8,10},{10,12},{12,14},{14,16},{16,18},{18... | collective-permute-start | bytes 221192 | tf_op jit(solution)/shard_map/ppermute | solution.py:580
  16.1 3.6 %collective-permute-start.3 = (f32[72,256]{1,0:T(8,128)S(1)}, f32[72,256]{1,0:T(8,128)S(1)}, u32[]{:S(2)}, u32[]{:S(2)}) collective-permute-start(f32[72,256]{1,0:T(8,128)S(1)} %get-tuple-element.28), channel_id=1, source_target_pairs={{2,0},{4,2},{6,4},{8,6},{10,8},{12,10},{14,12},{16,14},{18,16},{20... | collective-permute-start | bytes 221192 | tf_op jit(solution)/shard_map/ppermute | solution.py:579
  19.8 0.0 collective-permute-done.7
  19.8 0.1 collective-permute-start.8
  19.9 3.2 %collective-permute-done.8 = f32[40,128]{1,0:T(8,128)S(1)} collective-permute-done((f32[40,128]{1,0:T(8,128)S(1)}, f32[40,128]{1,0:T(8,128)S(1)}, u32[]{:S(2)}, u32[]{:S(2)}) %collective-permute-start.8) | collective-permute-done | bytes 20512 | tf_op jit(solution)/shard_map/ppermute | solution.py:626
  23.1 0.0 collective-permute-start.9
  23.1 0.5 %shard_map.90 = f32[72,128]{1,0:T(8,128)S(1)} custom-call(f32[16,256]{1,0:T(8,128)S(1)} %get-tuple-element.24.ar, f32[72,256]{1,0:T(8,128)S(1)} %collective-permute-done.west_row, f32[72,256]{1,0:T(8,128)S(1)} %collective-permute-done.1.east_row, f32[14,64,256]{2,1,0:T(8,128)S(1)} %get-tuple-element.35.near, f32[14,64,256]{2,1,0:T(8,128)S(1)} %get-tuple-element.36.far, ...), custom_call_target="tpu_custom_call" | custom-call | tf_op jit(solution)/shard_map/pallas_call | solution.py:514
  23.6 0.0 collective-permute-start.5
  23.6 2.6 %collective-permute-done.9 = f32[40,128]{1,0:T(8,128)S(1)} collective-permute-done((f32[40,128]{1,0:T(8,128)S(1)}, f32[40,128]{1,0:T(8,128)S(1)}, u32[]{:S(2)}, u32[]{:S(2)}) %collective-permute-start.9) | collective-permute-done | bytes 20512 | tf_op jit(solution)/shard_map/ppermute | solution.py:626
  26.3 0.6 %collective-permute-start.10 = (f32[40,128]{1,0:T(8,128)S(1)}, f32[40,128]{1,0:T(8,128)S(1)}, u32[]{:S(2)}, u32[]{:S(2)}) collective-permute-start(f32[40,128]{1,0:T(8,128)S(1)} %add.15.mine), channel_id=1, source_target_pairs={{0,17},{1,16},{2,19},{3,18},{4,21},{5,20},{6,23},{7,22},{8,25},{9,... | collective-permute-start | bytes 61448 | tf_op jit(solution)/shard_map/ppermute | solution.py:626
  26.9 0.0 collective-permute-done.5.got_low.got_high
  26.9 0.5 %shard_map.91.inner_0 = f32[14,32,256]{2,1,0:T(8,128)S(1)} custom-call(f32[14,64,256]{2,1,0:T(8,128)S(1)} %get-tuple-element.35.near, f32[14,64,256]{2,1,0:T(8,128)S(1)} %get-tuple-element.36.far, f32[6,2,24,128]{3,2,1,0:T(8,128)S(1)} %get-tuple-element.37.coef_near, f32[6,2,24,128]{3,2,1,0:T(8,128)S(1)} %get-tuple-element.38.coef_far, ...), custom_call_target="tpu_custom_call" | custom-call | tf_op jit(solution)/shard_map/pallas_call | solution.py:514
  27.4 0.5 %shard_map.92.inner_1 = f32[14,32,256]{2,1,0:T(8,128)S(1)} custom-call(f32[14,64,256]{2,1,0:T(8,128)S(1)} %get-tuple-element.35.near, f32[14,64,256]{2,1,0:T(8,128)S(1)} %get-tuple-element.36.far, f32[6,2,24,128]{3,2,1,0:T(8,128)S(1)} %get-tuple-element.37.coef_near, f32[6,2,24,128]{3,2,1,0:T(8,128)S(1)} %get-tuple-element.38.coef_far, ...), custom_call_target="tpu_custom_call" | custom-call | tf_op jit(solution)/shard_map/pallas_call | solution.py:514
  27.9 0.0 collective-permute-done.2.far_west
  27.9 0.0 collective-permute-done.3.far_east
  27.9 1.6 %shard_map.93 = f32[64,16,256]{2,1,0:T(8,128)} custom-call(f32[16,64,256]{2,1,0:T(8,128)S(1)} %get-tuple-element.23.sk, f32[16,256]{1,0:T(8,128)S(1)} %get-tuple-element.24.ar, f32[72,256]{1,0:T(8,128)S(1)} %collective-permute-done.west_row, f32[72,256]{1,0:T(8,128)S(1)} %collective-permute-done.1.east_row, f32[72,256]{1,0:T(8,128)S(1)} %collective-permute-done.2.far_west, ...), custom_call_target="tpu_custom_call" | custom-call | tf_op jit(solution)/shard_map/pallas_call | solution.py:514
  29.5 1.1 %collective-permute-done.10.other = f32[40,128]{1,0:T(8,128)S(1)} collective-permute-done((f32[40,128]{1,0:T(8,128)S(1)}, f32[40,128]{1,0:T(8,128)S(1)}, u32[]{:S(2)}, u32[]{:S(2)}) %collective-permute-start.10) | collective-permute-done | bytes 20512 | tf_op jit(solution)/shard_map/ppermute | solution.py:626
  30.6 0.8 %shard_map.94 = f32[96,96]{1,0:T(8,128)} custom-call(f32[40,128]{1,0:T(8,128)S(1)} %add.15.mine, f32[40,128]{1,0:T(8,128)S(1)} %collective-permute-done.10.other), custom_call_target="tpu_custom_call" | custom-call | tf_op jit(solution)/shard_map/pallas_call | solution.py:514
  (5 shorter events, 0.0 us)
Async XLA Ops:
  2.3 7.2 %collective-permute-start.4 = (f32[17,64,128]{2,1,0:T(8,128)S(1)}, f32[17,64,128]{2,1,0:T(8,128)S(1)}, u32[]{:S(2)}, u32[]{:S(2)}) collective-permute-start(f32[17,64,128]{2,1,0:T(8,128)S(1)} %get-tuple-element.34), channel_id=1, source_target_pairs={{0,1},{1,0},{2,3},{3,2},{4,5},{5,4},{6,7},{7,6},{8,9},{9,8},{10,11... | collective-permute-start | bytes 1671176 | tf_op jit(solution)/shard_map/ppermute | solution.py:544
  2.8 9.4 %collective-permute-start = (f32[72,256]{1,0:T(8,128)S(1)}, f32[72,256]{1,0:T(8,128)S(1)}, u32[]{:S(2)}, u32[]{:S(2)}) collective-permute-start(f32[72,256]{1,0:T(8,128)S(1)} %get-tuple-element.25), channel_id=1, source_target_pairs={{0,2},{2,4},{4,6},{6,8},{8,10},{10,12},{12,14},{14,16},{16,18},{18... | collective-permute-start | bytes 221192 | tf_op jit(solution)/shard_map/ppermute | solution.py:575
  5.4 6.9 %collective-permute-start.1 = (f32[72,256]{1,0:T(8,128)S(1)}, f32[72,256]{1,0:T(8,128)S(1)}, u32[]{:S(2)}, u32[]{:S(2)}) collective-permute-start(f32[72,256]{1,0:T(8,128)S(1)} %get-tuple-element.26), channel_id=1, source_target_pairs={{2,0},{4,2},{6,4},{8,6},{10,8},{12,10},{14,12},{16,14},{18,16},{20... | collective-permute-start | bytes 221192 | tf_op jit(solution)/shard_map/ppermute | solution.py:576
  12.9 1.3 %collective-permute-start.6 = (f32[40,128]{1,0:T(8,128)S(1)}, f32[40,128]{1,0:T(8,128)S(1)}, u32[]{:S(2)}, u32[]{:S(2)}) collective-permute-start(f32[40,128]{1,0:T(8,128)S(1)} %get-tuple-element.43), channel_id=1, source_target_pairs={{0,1},{1,0},{2,3},{3,2},{4,5},{5,4},{6,7},{7,6},{8,9},{9,8},{10,11... | collective-permute-start | bytes 61448 | tf_op jit(solution)/shard_map/ppermute | solution.py:626
  14.1 5.7 %collective-permute-start.7 = (f32[40,128]{1,0:T(8,128)S(1)}, f32[40,128]{1,0:T(8,128)S(1)}, u32[]{:S(2)}, u32[]{:S(2)}) collective-permute-start(f32[40,128]{1,0:T(8,128)S(1)} %add.12), channel_id=1, source_target_pairs={{0,5},{1,4},{2,7},{3,6},{4,1},{5,0},{6,3},{7,2},{8,13},{9,12},{10,... | collective-permute-start | bytes 61448 | tf_op jit(solution)/shard_map/ppermute | solution.py:626
  14.1 13.8 %collective-permute-start.2 = (f32[72,256]{1,0:T(8,128)S(1)}, f32[72,256]{1,0:T(8,128)S(1)}, u32[]{:S(2)}, u32[]{:S(2)}) collective-permute-start(f32[72,256]{1,0:T(8,128)S(1)} %get-tuple-element.27), channel_id=1, source_target_pairs={{0,2},{2,4},{4,6},{6,8},{8,10},{10,12},{12,14},{14,16},{16,18},{18... | collective-permute-start | bytes 221192 | tf_op jit(solution)/shard_map/ppermute | solution.py:580
  16.1 11.8 %collective-permute-start.3 = (f32[72,256]{1,0:T(8,128)S(1)}, f32[72,256]{1,0:T(8,128)S(1)}, u32[]{:S(2)}, u32[]{:S(2)}) collective-permute-start(f32[72,256]{1,0:T(8,128)S(1)} %get-tuple-element.28), channel_id=1, source_target_pairs={{2,0},{4,2},{6,4},{8,6},{10,8},{12,10},{14,12},{16,14},{18,16},{20... | collective-permute-start | bytes 221192 | tf_op jit(solution)/shard_map/ppermute | solution.py:579
  19.8 3.3 %collective-permute-start.8 = (f32[40,128]{1,0:T(8,128)S(1)}, f32[40,128]{1,0:T(8,128)S(1)}, u32[]{:S(2)}, u32[]{:S(2)}) collective-permute-start(f32[40,128]{1,0:T(8,128)S(1)} %add.13), channel_id=1, source_target_pairs={{0,3},{1,2},{2,1},{3,0},{4,7},{5,6},{6,5},{7,4},{8,11},{9,10},{10,... | collective-permute-start | bytes 61448 | tf_op jit(solution)/shard_map/ppermute | solution.py:626
  23.1 3.2 %collective-permute-start.9 = (f32[40,128]{1,0:T(8,128)S(1)}, f32[40,128]{1,0:T(8,128)S(1)}, u32[]{:S(2)}, u32[]{:S(2)}) collective-permute-start(f32[40,128]{1,0:T(8,128)S(1)} %add.14), channel_id=1, source_target_pairs={{0,9},{1,8},{2,11},{3,10},{4,13},{5,12},{6,15},{7,14},{8,1},{9,0},... | collective-permute-start | bytes 61448 | tf_op jit(solution)/shard_map/ppermute | solution.py:626
  23.6 3.3 %collective-permute-start.5 = (f32[72,128]{1,0:T(8,128)S(1)}, f32[72,128]{1,0:T(8,128)S(1)}, u32[]{:S(2)}, u32[]{:S(2)}) collective-permute-start(f32[72,128]{1,0:T(8,128)S(1)} %shard_map.90), channel_id=1, source_target_pairs={{0,1},{1,0},{2,3},{3,2},{4,5},{5,4},{6,7},{7,6},{8,9},{9,8},{10,11... | collective-permute-start | bytes 110600 | tf_op jit(solution)/shard_map/ppermute | solution.py:544
  26.3 4.3 %collective-permute-start.10 = (f32[40,128]{1,0:T(8,128)S(1)}, f32[40,128]{1,0:T(8,128)S(1)}, u32[]{:S(2)}, u32[]{:S(2)}) collective-permute-start(f32[40,128]{1,0:T(8,128)S(1)} %add.15.mine), channel_id=1, source_target_pairs={{0,17},{1,16},{2,19},{3,18},{4,21},{5,20},{6,23},{7,22},{8,25},{9,... | collective-permute-start | bytes 61448 | tf_op jit(solution)/shard_map/ppermute | solution.py:626
